TPU v7x, 32 devices: a whole 2x2x4 slice. The times are simulated.
32 devices in a mesh: scan: 8 (over z, core), det: 4 (over y, x).
Axes of the slice: x: 2, y: 2, z: 4, core: 2. Of those that a mesh axis runs over, the one named last changes fastest.
Arguments:
- patterns: float32 [8, 64, 128, 128], P('scan', None, 'det'), may hold values from -24 to 24, as said below
- encoder_one: float32 [3, 3, 1, 16], replicated, may hold values from -2 to 2
- encoder_two: float32 [3, 3, 16, 32], replicated, may hold values from -0.5 to 0.5
- real_space: float32 [3, 3, 32, 32], replicated, may hold values from -0.375 to 0.375
- decoder_one: float32 [3, 3, 32, 16], replicated, may hold values from -0.5 to 0.5
- decoder_two: float32 [3, 3, 16, 1], replicated, may hold values from -1 to 1
Outputs:
- rebuilt: float32 [8, 64, 128, 128], P('scan', None, 'det')
- misfit: float32 [8, 64], P('scan')
Inputs may be any that keep to these rules, and one draw needn't show every extreme that they name: `patterns`: detector intensities after background subtraction, in arbitrary units.
All inputs are finite; a program needn't handle non-finite values.
Results may differ from a plain program's by a relative error of at most 0.00011.
Values sent between devices are 32-bit elements; how exact they have to be, the bound alone decides.
No kernel may reach another device: no remote copies, remote signals or barrier semaphores. Data moves between devices by JAX's collectives and lax.ppermute only.
A program may use at most 128 MiB of HBM per device.

v0:
```python
import functools

import jax
import jax.numpy as jnp
from jax import lax
from jax.experimental import pallas as pl
from jax.experimental.pallas import tpu as pltpu
from jax.sharding import PartitionSpec as P

ABOVE = 7
BELOW = 4
LANES = 128
F32 = jnp.float32
BF16 = jnp.bfloat16


def silu(v):
    return (0.5 * v) * (1.0 + jnp.tanh(0.5 * v))


def split(v):
    high = v.astype(BF16)
    low = (v - high.astype(F32)).astype(BF16)
    return high, low


def iota(shape, dim):
    return lax.broadcasted_iota(jnp.int32, shape, dim)


def spread(values, width):
    k = values.shape[1]
    pick = (iota((k, width), 1) % k == iota((k, width), 0)).astype(F32)
    return jnp.dot(values, pick, precision=lax.Precision.HIGHEST, preferred_element_type=F32)


def put(ref, start, rows, value, lanes=None):
    high, low = split(value)
    third = ref.shape[0] // 3
    lanes = slice(None) if lanes is None else lanes
    ref[start : start + rows, lanes] = high
    ref[third + start : third + start + rows, lanes] = high
    ref[2 * third + start : 2 * third + start + rows, lanes] = low


def stack(block, times):
    return jnp.concatenate([block] * times, axis=0)


ROW_TAPS = {(0, 0): (0, 1), (1, 0): (2,), (0, 1): (0,), (1, 1): (1, 2)}


def weights_body(e1, e2, rs, d1, d2, w1, w2, wm, wd1, wd2):
    f1 = e1.shape[3]
    f2 = e2.shape[3]
    taps = jnp.concatenate([e1[a, b] for a in range(3) for b in range(3)], axis=0)
    wide = spread(taps, w1.shape[1])
    shape = (LANES, w1.shape[1])
    delta = iota(shape, 0) - 2 * (iota(shape, 1) // f1) + 1
    for a in range(3):
        value = jnp.zeros(shape, F32)
        for b in range(3):
            value = jnp.where(delta == b, wide[3 * a + b : 3 * a + b + 1, :], value)
        put(w1, a * LANES, LANES, value)
    shape = (3 * LANES, w2.shape[1])
    delta = iota(shape, 0) // f1 - LANES // f1 - 2 * (iota(shape, 1) // f2) + 1
    for a in range(3):
        value = jnp.zeros(shape, F32)
        for b in range(3):
            value = jnp.where(delta == b, stack(spread(e2[a, b], shape[1]), shape[0] // f1), value)
        put(w2, a * shape[0], shape[0], value)
    odd = lax.axis_index("scan") % 2
    shape = (LANES, LANES)
    same = iota(shape, 0) // f2 == iota(shape, 1) // f2
    for place in range(3):
        for b in range(3):
            if place == 0:
                block = rs[1, b]
            else:
                first = odd == (0 if place == 2 else 1)
                block = jnp.where(first, rs[0, b], rs[2, b])
            value = jnp.where(same, stack(spread(block, LANES), LANES // f2), 0.0)
            put(wm, place * LANES, LANES, value, slice(b * LANES, (b + 1) * LANES))
    per = LANES // f2
    for p in range(2):
        lanes = slice(p * LANES, (p + 1) * LANES)
        w_local = iota(shape, 1) // f1
        k = iota(shape, 0)
        wide_edge = jnp.zeros(shape, F32)
        for r in range(2):
            value = jnp.zeros(shape, F32)
            for b in range(3):
                tap = sum(d1[a, b] for a in ROW_TAPS[r, p])
                tap = stack(spread(tap, LANES), per)
                col = (w_local + b + 1) // 2 - 1
                value = value + jnp.where(col == k // f2, tap, 0.0)
                if r == 0:
                    edge = jnp.where(k // f2 == per - 1, -1, jnp.where(k // f2 == 0, per, -9))
                else:
                    edge = jnp.where(k // f2 == 1, -1, jnp.where(k // f2 == 2, per, -9))
                wide_edge = wide_edge + jnp.where(col == edge, tap, 0.0)
            put(wd1, r * LANES, LANES, value, lanes)
        put(wd1, 2 * LANES, LANES, wide_edge, lanes)
    depth = wd2.shape[0] // 6
    shape = (depth, LANES)
    for p in range(2):
        for r in range(2):
            value = jnp.zeros(shape, F32)
            for b in range(3):
                tap = sum(d2[a, b] for a in ROW_TAPS[r, p])
                tap = stack(jnp.broadcast_to(tap, (f1, LANES)), depth // f1)
                col = (iota(shape, 1) + b + 1) // 2 - 1
                value = value + jnp.where(col == iota(shape, 0) // f1, tap, 0.0)
            put(wd2, r * depth, depth, value, slice(p * LANES, (p + 1) * LANES))


def encode_body(x, halo, w1, w2, out, p0, p1, p2, p3, evh, evl, odh, odl, *, strip, cols):
    rows = strip + ABOVE + BELOW
    parts = (p0, p1, p2, p3)
    for e in range(rows):
        if e < ABOVE:
            value = halo[e]
        elif e < ABOVE + strip:
            value = x[pl.ds(e - ABOVE, cols, stride=strip), :]
        else:
            value = halo[e - strip]
        high, low = split(value)
        m = e // 4
        parts[e % 4][m * cols : (m + 1) * cols, :LANES] = high
        parts[e % 4][m * cols : (m + 1) * cols, LANES:] = low
    n_even = evh.shape[0]
    n_odd = odh.shape[0]
    for ref in (evh, evl, odh, odl):
        ref[:, :LANES] = jnp.zeros((ref.shape[0], LANES), BF16)

    def columns(refs, count):
        high = [ref[start : start + count, :LANES] for ref, start in refs]
        low = [ref[start : start + count, LANES:] for ref, start in refs]
        return jnp.concatenate(high + low + high, axis=1)

    def first(g, carry):
        lanes = pl.ds(pl.multiple_of(g * 256, 256), 256)
        target = pl.ds(pl.multiple_of(LANES + g * 256, LANES), 256)
        for refs, high_ref, low_ref, count in (
            (((p0, 0), (p1, 0), (p2, 0)), evh, evl, n_even),
            (((p2, 0), (p3, 0), (p0, cols)), odh, odl, n_odd),
        ):
            value = silu(jnp.dot(columns(refs, count), w1[:, lanes], preferred_element_type=F32))
            high, low = split(value)
            high_ref[:, target] = high
            low_ref[:, target] = low
        return carry

    lax.fori_loop(0, w1.shape[1] // 256, first, 0)
    n_out = n_odd

    def second(g, carry):
        source = pl.ds(pl.multiple_of(g * 256, 256), 3 * LANES)
        high = [evh[:n_out, source], odh[:, source], evh[cols:, source]]
        low = [evl[:n_out, source], odl[:, source], evl[cols:, source]]
        left = jnp.concatenate(high + low + high, axis=1)
        value = silu(jnp.dot(left, w2[...], preferred_element_type=F32))
        out[:, pl.ds(pl.multiple_of(g * 256, 256), 256)] = value
        return carry

    lax.fori_loop(0, w1.shape[1] // 256, second, 0)


def decode_body(own, sibling, other, x, wm, wd1, wd2, rebuilt, part, mixed, dh, dl, *, strip, cols):
    n = own.shape[0]
    blocks = own.shape[1] // LANES
    rows = n // cols
    det = lax.axis_index("det")
    not_first = (det > 0).astype(F32)
    not_last = (det < lax.axis_size("det") - 1).astype(F32)
    mixed[:, :LANES] = jnp.zeros((n, LANES), F32)
    mixed[:, (blocks + 1) * LANES :] = jnp.zeros((n, LANES), F32)
    position = iota((n, LANES), 0) % cols

    def mix(q, carry):
        lanes = pl.ds(pl.multiple_of(q * LANES, LANES), LANES)
        pairs = [split(ref[:, lanes]) for ref in (own, sibling, other)]
        high = [h for h, _ in pairs]
        low = [v for _, v in pairs]
        left = jnp.concatenate(high + low + high, axis=1)
        y = jnp.dot(left, wm[...], preferred_element_type=F32)
        before = jnp.where(position == 0, 0.0, pltpu.roll(y[:, :LANES], 1, 0))
        after = jnp.where(position == cols - 1, 0.0, pltpu.roll(y[:, 2 * LANES :], n - 1, 0))
        value = own[:, lanes] + silu(y[:, LANES : 2 * LANES] + before + after)
        target = pl.ds(pl.multiple_of((q + 1) * LANES, LANES), LANES)
        mixed[: n - cols, target] = value[: n - cols]
        mixed[n - cols :, target] = value[n - cols :] * not_last
        return carry

    lax.fori_loop(0, blocks, mix, 0)
    count = n - cols
    lane = iota((count, LANES), 1)
    middle = (lane >= 32) & (lane < 96)
    outer = iota((n, LANES), 1) >= 96

    def first(q, carry):
        here = pl.ds(pl.multiple_of((q + 1) * LANES, LANES), LANES)
        before = pl.ds(pl.multiple_of(q * LANES, LANES), LANES)
        after = pl.ds(pl.multiple_of((q + 2) * LANES, LANES), LANES)
        high, low = split(mixed[:, here])
        edges = jnp.where(outer, mixed[:, before], mixed[:, after])
        edges = jnp.where(middle, pltpu.roll(edges[cols:], 64, 1), edges[:count])
        edge_high, edge_low = split(edges)
        highs = [high[:count], high[cols:], edge_high]
        lows = [low[:count], low[cols:], edge_low]
        left = jnp.concatenate(highs + lows + highs, axis=1)
        value = silu(jnp.dot(left, wd1[...], preferred_element_type=F32))
        target = pl.ds(pl.multiple_of(q * LANES, LANES), LANES)
        for i in range(rows - 1):
            for p in range(2):
                block = value[i * cols : (i + 1) * cols, p * LANES : (p + 1) * LANES]
                if i == 0 and p == 0:
                    block = block * not_first
                if i == rows - 2 and p == 1:
                    block = block * not_last
                high, low = split(block)
                start = (2 * i + p) * cols
                dh[start : start + cols, target] = high
                dl[start : start + cols, target] = low
        return carry

    lax.fori_loop(0, blocks, first, 0)
    total = jnp.zeros((cols, LANES), F32)
    pairs = strip // 2 + 1
    step = 6
    for begin in range(0, pairs, step):
        size = min(step, pairs - begin)
        top = slice(begin * cols, (begin + size) * cols)
        bottom = slice((begin + 1) * cols, (begin + size + 1) * cols)
        high = [dh[top], dh[bottom]]
        low = [dl[top], dl[bottom]]
        left = jnp.concatenate(high + low + high, axis=1)
        value = jnp.dot(left, wd2[...], preferred_element_type=F32)
        for i in range(size):
            for p in range(2):
                row = 2 * (begin + i) - 1 + p
                if 0 <= row < strip:
                    block = value[i * cols : (i + 1) * cols, p * LANES : (p + 1) * LANES]
                    where = pl.ds(row, cols, stride=strip)
                    rebuilt[where, :] = block
                    error = block - x[where, :]
                    total = total + error * error
    part[...] = jnp.sum(total.T, axis=0, keepdims=True)


def swapped(value, axis, pairs):
    return lax.ppermute(value, axis, [(i, j) for i, j in pairs] + [(j, i) for i, j in pairs])


def on_device(patterns, encoder_one, encoder_two, real_space, decoder_one, decoder_two):
    _, cols, strip, width = patterns.shape
    f1 = encoder_one.shape[3]
    f2 = encoder_two.shape[3]
    n_scan = lax.axis_size("scan")
    n_det = lax.axis_size("det")
    latent_rows = strip // 4 + 2
    latent_lanes = (width // 4) * f2
    hidden_lanes = (width // 2) * f1
    params = pltpu.CompilerParams(vmem_limit_bytes=56 << 20)
    x = patterns.reshape(cols * strip, width)

    down = [(i, i + 1) for i in range(n_det - 1)]
    up = [(i + 1, i) for i in range(n_det - 1)]
    above = lax.ppermute(patterns[0, :, strip - ABOVE :].transpose(1, 0, 2), "det", down)
    below = lax.ppermute(patterns[0, :, :BELOW].transpose(1, 0, 2), "det", up)
    chips = [(i, i + 1) for i in range(1, n_scan - 1, 2)]
    cores = [(i, i + 1) for i in range(0, n_scan, 2)]
    far_x = swapped(x, "scan", chips)
    halo = jnp.concatenate([above, below], axis=0)
    far_halo = swapped(halo, "scan", chips)

    w1, w2, wm, wd1, wd2 = pl.pallas_call(
        weights_body,
        out_shape=[
            jax.ShapeDtypeStruct((9 * LANES, hidden_lanes), BF16),
            jax.ShapeDtypeStruct((27 * LANES, 256), BF16),
            jax.ShapeDtypeStruct((9 * LANES, 3 * LANES), BF16),
            jax.ShapeDtypeStruct((9 * LANES, 2 * LANES), BF16),
            jax.ShapeDtypeStruct((6 * hidden_lanes, 2 * LANES), BF16),
        ],
        compiler_params=params,
        name="weights",
    )(encoder_one, encoder_two, real_space, decoder_one, decoder_two)

    rows4 = strip // 4 + 3
    n_latent = latent_rows * cols

    def encode(strip_x, strip_halo):
        return pl.pallas_call(
            functools.partial(encode_body, strip=strip, cols=cols),
            out_shape=jax.ShapeDtypeStruct((n_latent, latent_lanes), F32),
            scratch_shapes=[pltpu.VMEM((rows4 * cols, 2 * LANES), BF16)] * 4
            + [pltpu.VMEM((n_latent + cols, hidden_lanes + LANES), BF16)] * 2
            + [pltpu.VMEM((n_latent, hidden_lanes + LANES), BF16)] * 2,
            compiler_params=params,
            name="encode",
        )(strip_x, strip_halo, w1, w2)

    own = encode(x, halo)
    sibling = swapped(own, "scan", cores)
    other = encode(far_x, far_halo)
    rebuilt, part = pl.pallas_call(
        functools.partial(decode_body, strip=strip, cols=cols),
        out_shape=[
            jax.ShapeDtypeStruct((cols * strip, width), F32),
            jax.ShapeDtypeStruct((1, cols), F32),
        ],
        scratch_shapes=[
            pltpu.VMEM((n_latent, latent_lanes + 2 * LANES), F32),
            pltpu.VMEM(((strip // 2 + 2) * cols, hidden_lanes), BF16),
            pltpu.VMEM(((strip // 2 + 2) * cols, hidden_lanes), BF16),
        ],
        compiler_params=params,
        name="decode",
    )(own, sibling, other, x, wm, wd1, wd2)
    misfit = lax.psum(part, "det") / (width * width)
    return rebuilt.reshape(patterns.shape), misfit


def solution(mesh):
    return jax.shard_map(
        on_device,
        mesh=mesh,
        in_specs=(P("scan", None, "det", None), P(), P(), P(), P(), P()),
        out_specs=(P("scan", None, "det", None), P("scan", None)),
        check_vma=False,
    )
```

profile of v0, /device:TPU:8, one launch (start us, length us, event | category | flops | bytes accessed | tf_op | source)
XLA Modules:
  0.0 108.1 jit_solution(15963453217898519170)
XLA Ops:
  0.6 1.0 slice.6
  1.7 3.4 %collective-permute-start = (f32[7,64,128]{2,1,0:T(8,128)S(1)}, f32[7,64,128]{2,1,0:T(8,128)S(1)}, u32[]{:S(2)}, u32[]{:S(2)}) collective-permute-start(f32[7,64,128]{2,1,0:T(8,128)S(1)} %bitcast.15), channel_id=1, source_target_pairs={{0,1},{1,2},{2,3},{4,5},{5,6},{6,7},{8,9},{9,10},{10,11},{12,13},{... | collective-permute-start | bytes 688136 | tf_op jit(solution)/shard_map/ppermute | solution.py:269
  5.1 1.0 slice.7
  6.1 1.3 %collective-permute-start.1 = (f32[4,64,128]{2,1,0:T(8,128)S(1)}, f32[4,64,128]{2,1,0:T(8,128)S(1)}, u32[]{:S(2)}, u32[]{:S(2)}) collective-permute-start(f32[4,64,128]{2,1,0:T(8,128)S(1)} %bitcast.16), channel_id=1, source_target_pairs={{1,0},{2,1},{3,2},{5,4},{6,5},{7,6},{9,8},{10,9},{11,10},{13,12},{... | collective-permute-start | bytes 393224 | tf_op jit(solution)/shard_map/ppermute | solution.py:270
  7.4 1.4 %copy.11.d2 = f32[3,3,16,1]{3,2,1,0:T(8,128)} copy(f32[3,3,16,1]{2,3,1,0:T(1,128)} %param.11) | data formatting | bytes 1152 | tf_op args[5]
  8.8 1.7 %copy.10.d1 = f32[3,3,32,16]{3,2,1,0:T(8,128)} copy(f32[3,3,32,16]{2,3,1,0:T(8,128)} %param.10) | data formatting | bytes 36864 | tf_op args[4]
  10.5 6.3 %weights.1 = (bf16[1152,1024]{1,0:T(8,128)(2,1)}, bf16[3456,256]{1,0:T(8,128)(2,1)}, bf16[1152,384]{1,0:T(8,128)(2,1)}, bf16[1152,256]{1,0:T(8,128)(2,1)}, bf16[6144,256]{1,0:T(8,128)(2,1)}) custom-call(f32[3,3,1,16]{3,2,1,0:T(1,128)} %e1.1, f32[3,3,16,32]{3,2,1,0:T(8,128)} %e2.1, f32[3,3,32,32]{3,2,1,0:T(8,128)} %rs.1, f32[3,3,32,16]{3,2,1,0:T(8,128)} %copy.10.d1, ...), custom_call_target="tpu_custom_call" | custom-call | tf_op jit(solution)/shard_map/weights/pallas_call | solution.py:277
  16.8 0.0 collective-permute-done
  16.8 0.0 collective-permute-done.1
  16.8 0.0 copy-start.3
  16.8 0.7 copy-done.3
  17.6 0.0 copy-start
  17.6 15.7 %encode.2.own = f32[640,1024]{1,0:T(8,128)} custom-call(f32[2048,128]{1,0:T(8,128)} %bitcast.12, f32[11,64,128]{2,1,0:T(8,128)} %copy-done.3, bf16[1152,1024]{1,0:T(8,128)(2,1)} %get-tuple-element.9.w1, bf16[3456,256]{1,0:T(8,128)(2,1)} %get-tuple-element.10.w2), custom_call_target="tpu_custom_call" | custom-call | tf_op jit(solution)/shard_map/encode/pallas_call | solution.py:294
  33.3 0.0 collective-permute-start.2
  33.3 0.0 copy-done
  33.3 2.5 %collective-permute-start.3 = (f32[2048,128]{1,0:T(8,128)S(1)}, f32[2048,128]{1,0:T(8,128)S(1)}, u32[]{:S(2)}, u32[]{:S(2)}) collective-permute-start(f32[2048,128]{1,0:T(8,128)S(1)} %bitcast.14), channel_id=1, source_target_pairs={{4,8},{12,16},{20,24},{8,4},{16,12},{24,20},{5,9},{13,17},{21,25},... | collective-permute-start | bytes 3145736 | tf_op jit(solution)/shard_map/ppermute | solution.py:252
  35.8 3.3 %collective-permute-start.4 = (f32[11,64,128]{2,1,0:T(8,128)}, f32[11,64,128]{2,1,0:T(8,128)S(1)}, u32[]{:S(2)}, u32[]{:S(2)}) collective-permute-start(f32[11,64,128]{2,1,0:T(8,128)} %copy-done.3), channel_id=1, source_target_pairs={{4,8},{12,16},{20,24},{8,4},{16,12},{24,20},{5,9},{13,17},{21,25},... | collective-permute-start | bytes 1081352 | tf_op jit(solution)/shard_map/ppermute | solution.py:252
  39.1 14.2 %collective-permute-done.4.halo = f32[11,64,128]{2,1,0:T(8,128)S(1)} collective-permute-done((f32[11,64,128]{2,1,0:T(8,128)}, f32[11,64,128]{2,1,0:T(8,128)S(1)}, u32[]{:S(2)}, u32[]{:S(2)}) %collective-permute-start.4) | collective-permute-done | bytes 360480 | tf_op jit(solution)/shard_map/ppermute | solution.py:252
  53.3 0.0 copy-start.4
  53.3 0.0 collective-permute-done.3.x
  53.3 0.7 copy-done.4
  54.0 0.0 copy-start.2
  54.0 1.0 copy-done.2
  55.0 15.6 %encode.3.other = f32[640,1024]{1,0:T(8,128)} custom-call(f32[2048,128]{1,0:T(8,128)} %copy-done.2, f32[11,64,128]{2,1,0:T(8,128)} %copy-done.4, bf16[1152,1024]{1,0:T(8,128)(2,1)} %get-tuple-element.9.w1, bf16[3456,256]{1,0:T(8,128)(2,1)} %get-tuple-element.10.w2), custom_call_target="tpu_custom_call" | custom-call | tf_op jit(solution)/shard_map/encode/pallas_call | solution.py:294
  70.6 0.0 collective-permute-done.2.sibling
  70.6 0.0 copy-start.1
  70.6 1.6 %copy-done.1 = f32[640,1024]{1,0:T(8,128)} copy-done((f32[640,1024]{1,0:T(8,128)}, f32[640,1024]{1,0:T(8,128)S(1)}, u32[]{:S(2)}) %copy-start.1) | copy-done | bytes 2621464
  72.2 24.1 %decode.1 = (f32[2048,128]{1,0:T(8,128)}, f32[1,64]{1,0:T(1,128)}) custom-call(f32[640,1024]{1,0:T(8,128)} %encode.2.own, f32[640,1024]{1,0:T(8,128)} %copy-done.1, f32[640,1024]{1,0:T(8,128)} %encode.3.other, f32[2048,128]{1,0:T(8,128)} %bitcast.13, bf16[1152,384]{1,0:T(8,128)(2,1)} %get-tuple-element.11.wm, bf16[1152,256]{1,0:T(8,128)(2,1)} %get-tuple-element.12.wd1, ...), custom_call_target="tpu_custom_call" | custom-call | tf_op jit(solution)/shard_map/decode/pallas_call | solution.py:307
  96.3 11.2 %psum.7 = f32[1,64]{1,0:T(1,128)S(1)} all-reduce(f32[1,64]{1,0:T(1,128)} %get-tuple-element.15), channel_id=1, replica_groups=mesh['scan'=8,'det'=4] {'det'}, use_global_device_ids=true, to_apply=%region_0.0 | all-reduce | flops 64 | bytes 512 | tf_op jit(solution)/shard_map/psum | solution.py:321
  107.5 0.5 broadcast_multiply_fusion
  (4 shorter events, 0.1 us)
Async XLA Ops:
  1.7 15.1 %collective-permute-start = (f32[7,64,128]{2,1,0:T(8,128)S(1)}, f32[7,64,128]{2,1,0:T(8,128)S(1)}, u32[]{:S(2)}, u32[]{:S(2)}) collective-permute-start(f32[7,64,128]{2,1,0:T(8,128)S(1)} %bitcast.15), channel_id=1, source_target_pairs={{0,1},{1,2},{2,3},{4,5},{5,6},{6,7},{8,9},{9,10},{10,11},{12,13},{... | collective-permute-start | bytes 688136 | tf_op jit(solution)/shard_map/ppermute | solution.py:269
  6.1 10.7 %collective-permute-start.1 = (f32[4,64,128]{2,1,0:T(8,128)S(1)}, f32[4,64,128]{2,1,0:T(8,128)S(1)}, u32[]{:S(2)}, u32[]{:S(2)}) collective-permute-start(f32[4,64,128]{2,1,0:T(8,128)S(1)} %bitcast.16), channel_id=1, source_target_pairs={{1,0},{2,1},{3,2},{5,4},{6,5},{7,6},{9,8},{10,9},{11,10},{13,12},{... | collective-permute-start | bytes 393224 | tf_op jit(solution)/shard_map/ppermute | solution.py:270
  16.8 0.7 copy-start.3
  17.6 15.7 %copy-start = (f32[1,64,32,128]{3,2,1,0:T(8,128)S(1)}, f32[1,64,32,128]{3,2,1,0:T(8,128)}, u32[]{:S(2)}) copy-start(f32[1,64,32,128]{3,2,1,0:T(8,128)} %param.6) | copy-start | bytes 3145732
  33.3 37.3 %collective-permute-start.2 = (f32[640,1024]{1,0:T(8,128)}, f32[640,1024]{1,0:T(8,128)S(1)}, u32[]{:S(2)}, u32[]{:S(2)}) collective-permute-start(f32[640,1024]{1,0:T(8,128)} %encode.2.own), channel_id=1, source_target_pairs={{0,4},{8,12},{16,20},{24,28},{4,0},{12,8},{20,16},{28,24},{1,5},{9... | collective-permute-start | bytes 7864328 | tf_op jit(solution)/shard_map/ppermute | solution.py:252
  33.3 20.0 %collective-permute-start.3 = (f32[2048,128]{1,0:T(8,128)S(1)}, f32[2048,128]{1,0:T(8,128)S(1)}, u32[]{:S(2)}, u32[]{:S(2)}) collective-permute-start(f32[2048,128]{1,0:T(8,128)S(1)} %bitcast.14), channel_id=1, source_target_pairs={{4,8},{12,16},{20,24},{8,4},{16,12},{24,20},{5,9},{13,17},{21,25},... | collective-permute-start | bytes 3145736 | tf_op jit(solution)/shard_map/ppermute | solution.py:252
  35.8 17.5 %collective-permute-start.4 = (f32[11,64,128]{2,1,0:T(8,128)}, f32[11,64,128]{2,1,0:T(8,128)S(1)}, u32[]{:S(2)}, u32[]{:S(2)}) collective-permute-start(f32[11,64,128]{2,1,0:T(8,128)} %copy-done.3), channel_id=1, source_target_pairs={{4,8},{12,16},{20,24},{8,4},{16,12},{24,20},{5,9},{13,17},{21,25},... | collective-permute-start | bytes 1081352 | tf_op jit(solution)/shard_map/ppermute | solution.py:252
  53.3 0.7 copy-start.4
  54.0 1.0 copy-start.2
  70.6 1.6 %copy-start.1 = (f32[640,1024]{1,0:T(8,128)}, f32[640,1024]{1,0:T(8,128)S(1)}, u32[]{:S(2)}) copy-start(f32[640,1024]{1,0:T(8,128)S(1)} %collective-permute-done.2.sibling) | copy-start | bytes 7864324
where the time goes:
time: 108 us
  Pallas kernels  61.8 us (57%)
  waiting for transfers between devices  14.2 us (13%)
  blocking collectives  11.2 us (10%)
  starting transfers between devices  10.4 us (10%)
  local copies, waits for them, and re-layouts  9.12 us (8%)
    pallas_call x2, Pallas kernels, encode(): pl.pallas_call(functools.partial(encode_body, strip=strip, cols=cols), ou...  31.4 us
    pallas_call x1, Pallas kernels, on_device(): pl.pallas_call(functools.partial(decode_body, strip=strip, cols=cols), ou...  24.1 us
    ppermute x3, waiting for transfers between devices, swapped(): lax.ppermute(value, axis, [(i, j) for i, j in pairs] + [(j, i) for i, j i...  14.2 us
    psum x1, blocking collectives, on_device(): misfit = lax.psum(part, 'det') / (width * width)  11.2 us
    unnamed x15, local copies, waits for them, and re-layouts  7.16 us
    pallas_call x1, Pallas kernels, on_device(): pl.pallas_call(weights_body, out_shape=[jax.ShapeDtypeStruct((9 * LANES,...  6.32 us
    ppermute x3, starting transfers between devices, swapped(): lax.ppermute(value, axis, [(i, j) for i, j in pairs] + [(j, i) for i, j i...  5.73 us
    ppermute x1, starting transfers between devices, on_device(): lax.ppermute(patterns[0, :, strip - ABOVE:].transpose(1, 0, 2), 'det', down)  3.41 us
  transfers between devices with their start and end apart: 5, of which 1 were waited for; matrix products, arithmetic and copies ran while one was open for 4% of the time, Pallas kernels for 20%

commit v1 on v0

v1 whole, which is shorter than its diff:
```python
import functools

import jax
import jax.numpy as jnp
from jax import lax
from jax.experimental import pallas as pl
from jax.experimental.pallas import tpu as pltpu
from jax.sharding import PartitionSpec as P

ABOVE = 7
BELOW = 4
LANES = 128
F32 = jnp.float32
BF16 = jnp.bfloat16
ENCODE_VMEM = 28 << 20
DECODE_VMEM = 36 << 20


def silu(v):
    return (0.5 * v) * (1.0 + jnp.tanh(0.5 * v))


def split(v):
    high = v.astype(BF16)
    low = (v - high.astype(F32)).astype(BF16)
    return high, low


def iota(shape, dim):
    return lax.broadcasted_iota(jnp.int32, shape, dim)


def spread(values, width):
    k = values.shape[1]
    pick = (iota((k, width), 1) % k == iota((k, width), 0)).astype(F32)
    return jnp.dot(values, pick, precision=lax.Precision.HIGHEST, preferred_element_type=F32)


def put(ref, start, value, lanes=None):
    high, low = split(value)
    half = ref.shape[0] // 2
    rows = value.shape[0]
    lanes = slice(None) if lanes is None else lanes
    ref[start : start + rows, lanes] = high
    ref[half + start : half + start + rows, lanes] = low


def thrice(ref):
    half = ref.shape[0] // 2
    return jnp.concatenate([ref[:half], ref[:half], ref[half:]], axis=0)


def stack(block, times):
    return jnp.concatenate([block] * times, axis=0)


def mosaic(refs):
    return jnp.concatenate([refs[a, b] for a in range(3) for b in range(3)], axis=0)


TAPS = 42
ROW_TAPS = {(0, 0): (0, 1), (1, 0): (2,), (0, 1): (0,), (1, 1): (1, 2)}


def encoder_weights_body(e1, e2, w1, w2):
    f1 = e1.shape[3]
    f2 = e2.shape[3]
    wide = spread(mosaic(e1), w1.shape[1])
    shape = (LANES, w1.shape[1])
    k = iota(shape, 0)
    n = iota(shape, 1)
    group = n // 256
    place = (k - 32 * group + 1) & (LANES - 1)
    a = (place >= TAPS).astype(jnp.int32) + (place >= 2 * TAPS).astype(jnp.int32)
    col = place - TAPS * a
    b = col - 2 * ((n // f1) % (256 // f1))
    good = (b >= 0) & (b <= 2) & ((group > 0) | (col > 0))
    key = jnp.where(good, 3 * a + b, -1)
    value = jnp.zeros(shape, F32)
    for tap in range(9):
        value = jnp.where(key == tap, wide[tap : tap + 1, :], value)
    put(w1, 0, value)
    wide = spread(mosaic(e2), w2.shape[1])
    shape = (3 * LANES, w2.shape[1])
    delta = iota(shape, 0) // f1 - LANES // f1 - 2 * (iota(shape, 1) // f2) + 1
    for a in range(3):
        value = jnp.zeros(shape, F32)
        for b in range(3):
            tap = wide[(3 * a + b) * f1 : (3 * a + b + 1) * f1]
            value = jnp.where(delta == b, stack(tap, shape[0] // f1), value)
        put(w2, a * shape[0], value)


def decoder_weights_body(rs, d1, d2, wm, wd1, wd2):
    f2, f1 = d1.shape[3], d1.shape[2]
    odd = lax.axis_index("scan") % 2
    shape = (LANES, LANES)
    same = iota(shape, 0) // f2 == iota(shape, 1) // f2
    wide = spread(mosaic(rs), LANES)
    tap = {(a, b): wide[(3 * a + b) * f2 : (3 * a + b + 1) * f2] for a in range(3) for b in range(3)}
    for place in range(3):
        for b in range(3):
            if place == 0:
                block = tap[1, b]
            else:
                block = jnp.where(odd == (0 if place == 2 else 1), tap[0, b], tap[2, b])
            value = jnp.where(same, stack(block, LANES // f2), 0.0)
            put(wm, place * LANES, value, slice(b * LANES, (b + 1) * LANES))
    per = LANES // f2
    wide = spread(jnp.concatenate([d1[a, b].T for a in range(3) for b in range(3)], axis=0), LANES)
    tap = {(a, b): wide[(3 * a + b) * f2 : (3 * a + b + 1) * f2] for a in range(3) for b in range(3)}
    w_local = iota(shape, 1) // f1
    k = iota(shape, 0)
    for p in range(2):
        lanes = slice(p * LANES, (p + 1) * LANES)
        wide_edge = jnp.zeros(shape, F32)
        for r in range(2):
            value = jnp.zeros(shape, F32)
            for b in range(3):
                block = stack(sum(tap[a, b] for a in ROW_TAPS[r, p]), per)
                col = (w_local + b + 1) // 2 - 1
                value = value + jnp.where(col == k // f2, block, 0.0)
                if r == 0:
                    edge = jnp.where(k // f2 == per - 1, -1, jnp.where(k // f2 == 0, per, -9))
                else:
                    edge = jnp.where(k // f2 == 1, -1, jnp.where(k // f2 == 2, per, -9))
                wide_edge = wide_edge + jnp.where(col == edge, block, 0.0)
            put(wd1, r * LANES, value, lanes)
        put(wd1, 2 * LANES, wide_edge, lanes)
    depth = wd2.shape[0] // 4
    shape = (depth, LANES)
    diagonal = iota((f1, f1), 0) == iota((f1, f1), 1)
    column = {
        (a, b): jnp.sum(jnp.where(diagonal, d2[a, b], 0.0), axis=1, keepdims=True)
        for a in range(3)
        for b in range(3)
    }
    for p in range(2):
        for r in range(2):
            value = jnp.zeros(shape, F32)
            for b in range(3):
                block = jnp.broadcast_to(sum(column[a, b] for a in ROW_TAPS[r, p]), (f1, LANES))
                col = (iota(shape, 1) + b + 1) // 2 - 1
                value = value + jnp.where(col == iota(shape, 0) // f1, stack(block, depth // f1), 0.0)
            put(wd2, r * depth, value, slice(p * LANES, (p + 1) * LANES))


def encode_body(x, halo, w1, w2, out, tap0, tap1, tap2, high_map, low_map, *, strip, cols):
    rows = strip + ABOVE + BELOW
    n_odd = strip // 4 + 2
    n_even = n_odd + 1
    odd_start = n_even * cols

    def place(h):
        start = (h // 2) * cols + (h % 2) * odd_start
        return slice(start, start + cols)

    for e in range(rows):
        if e < ABOVE:
            value = halo[e]
        elif e < ABOVE + strip:
            value = x[pl.ds(e - ABOVE, cols, stride=strip), :]
        else:
            value = halo[e - strip]
        if e % 2:
            tap1[place(e // 2), :] = pltpu.roll(value, TAPS, 1)
        else:
            if e // 2 < n_even + n_odd:
                tap0[place(e // 2), :] = value
            if e > 0:
                tap2[place(e // 2 - 1), :] = pltpu.roll(value, 2 * TAPS, 1)
    total = high_map.shape[0]
    for ref in (high_map, low_map):
        ref[:, :LANES] = jnp.zeros((total, LANES), BF16)
    lane = iota((total, LANES), 1)

    def first(g, carry):
        lanes = pl.ds(pl.multiple_of(g * 256, 256), 256)
        target = pl.ds(pl.multiple_of(LANES + g * 256, LANES), 256)
        at = (lane - 32 * g + 1) & (LANES - 1)
        packed = jnp.where(at < TAPS, tap0[...], jnp.where(at < 2 * TAPS, tap1[...], tap2[...]))
        high, low = split(packed)
        left = jnp.concatenate([high, low, high], axis=1)
        value = silu(jnp.dot(left, thrice(w1.at[:, lanes]), preferred_element_type=F32))
        high, low = split(value)
        high_map[:, target] = high
        low_map[:, target] = low
        return carry

    groups = (high_map.shape[1] - LANES) // 256
    lax.fori_loop(0, groups, first, 0)
    n = n_odd * cols

    def second(g, carry):
        source = pl.ds(pl.multiple_of(g * 256, 256), 3 * LANES)
        starts = (0, odd_start, cols)
        high = [high_map[start : start + n, source] for start in starts]
        low = [low_map[start : start + n, source] for start in starts]
        left = jnp.concatenate(high + low + high, axis=1)
        value = silu(jnp.dot(left, thrice(w2), preferred_element_type=F32))
        out[:, pl.ds(pl.multiple_of(g * 256, 256), 256)] = value
        return carry

    lax.fori_loop(0, groups, second, 0)


def decode_body(own, sibling, other, x, wm, wd1, wd2, rebuilt, part, mixed, dh, dl, *, strip, cols):
    n = own.shape[0]
    blocks = own.shape[1] // LANES
    rows = n // cols
    det = lax.axis_index("det")
    not_first = (det > 0).astype(F32)
    not_last = (det < lax.axis_size("det") - 1).astype(F32)
    mixed[:, :LANES] = jnp.zeros((n, LANES), F32)
    mixed[:, (blocks + 1) * LANES :] = jnp.zeros((n, LANES), F32)
    position = iota((n, LANES), 0) % cols

    def mix(q, carry):
        lanes = pl.ds(pl.multiple_of(q * LANES, LANES), LANES)
        pairs = [split(ref[:, lanes]) for ref in (own, sibling, other)]
        high = [h for h, _ in pairs]
        low = [v for _, v in pairs]
        left = jnp.concatenate(high + low + high, axis=1)
        y = jnp.dot(left, thrice(wm), preferred_element_type=F32)
        before = jnp.where(position == 0, 0.0, pltpu.roll(y[:, :LANES], 1, 0))
        after = jnp.where(position == cols - 1, 0.0, pltpu.roll(y[:, 2 * LANES :], n - 1, 0))
        value = own[:, lanes] + silu(y[:, LANES : 2 * LANES] + before + after)
        target = pl.ds(pl.multiple_of((q + 1) * LANES, LANES), LANES)
        mixed[: n - cols, target] = value[: n - cols]
        mixed[n - cols :, target] = value[n - cols :] * not_last
        return carry

    lax.fori_loop(0, blocks, mix, 0)
    count = n - cols
    lane = iota((count, LANES), 1)
    middle = (lane >= 32) & (lane < 96)
    outer = iota((n, LANES), 1) >= 96

    def first(q, carry):
        here = pl.ds(pl.multiple_of((q + 1) * LANES, LANES), LANES)
        before = pl.ds(pl.multiple_of(q * LANES, LANES), LANES)
        after = pl.ds(pl.multiple_of((q + 2) * LANES, LANES), LANES)
        high, low = split(mixed[:, here])
        edges = jnp.where(outer, mixed[:, before], mixed[:, after])
        edges = jnp.where(middle, pltpu.roll(edges[cols:], 64, 1), edges[:count])
        edge_high, edge_low = split(edges)
        highs = [high[:count], high[cols:], edge_high]
        lows = [low[:count], low[cols:], edge_low]
        left = jnp.concatenate(highs + lows + highs, axis=1)
        value = silu(jnp.dot(left, thrice(wd1), preferred_element_type=F32))
        target = pl.ds(pl.multiple_of(q * LANES, LANES), LANES)
        for i in range(rows - 1):
            for p in range(2):
                block = value[i * cols : (i + 1) * cols, p * LANES : (p + 1) * LANES]
                if i == 0 and p == 0:
                    block = block * not_first
                if i == rows - 2 and p == 1:
                    block = block * not_last
                high, low = split(block)
                start = (2 * i + p) * cols
                dh[start : start + cols, target] = high
                dl[start : start + cols, target] = low
        return carry

    lax.fori_loop(0, blocks, first, 0)
    total = jnp.zeros((cols, LANES), F32)
    pairs = strip // 2 + 1
    step = 6
    for begin in range(0, pairs, step):
        size = min(step, pairs - begin)
        top = slice(begin * cols, (begin + size) * cols)
        bottom = slice((begin + 1) * cols, (begin + size + 1) * cols)
        high = [dh[top], dh[bottom]]
        low = [dl[top], dl[bottom]]
        left = jnp.concatenate(high + low + high, axis=1)
        value = jnp.dot(left, thrice(wd2), preferred_element_type=F32)
        for i in range(size):
            for p in range(2):
                row = 2 * (begin + i) - 1 + p
                if 0 <= row < strip:
                    block = value[i * cols : (i + 1) * cols, p * LANES : (p + 1) * LANES]
                    where = pl.ds(row, cols, stride=strip)
                    rebuilt[where, :] = block
                    error = block - x[where, :]
                    total = total + error * error
    part[...] = jnp.sum(total.T, axis=0, keepdims=True) * (1.0 / (LANES * LANES))


def swapped(value, axis, pairs):
    return lax.ppermute(value, axis, [(i, j) for i, j in pairs] + [(j, i) for i, j in pairs])


def on_device(patterns, encoder_one, encoder_two, real_space, decoder_one, decoder_two):
    _, cols, strip, width = patterns.shape
    f1 = encoder_one.shape[3]
    f2 = encoder_two.shape[3]
    n_scan = lax.axis_size("scan")
    n_det = lax.axis_size("det")
    latent_rows = strip // 4 + 2
    latent_lanes = (width // 4) * f2
    hidden_lanes = (width // 2) * f1
    x = patterns.reshape(cols * strip, width)

    down = [(i, i + 1) for i in range(n_det - 1)]
    up = [(i + 1, i) for i in range(n_det - 1)]
    above = lax.ppermute(patterns[0, :, strip - ABOVE :].transpose(1, 0, 2), "det", down)
    below = lax.ppermute(patterns[0, :, :BELOW].transpose(1, 0, 2), "det", up)
    chips = [(i, i + 1) for i in range(1, n_scan - 1, 2)]
    cores = [(i, i + 1) for i in range(0, n_scan, 2)]
    far_x = swapped(x, "scan", chips)
    halo = jnp.concatenate([above, below], axis=0)
    far_halo = swapped(halo, "scan", chips)

    def cost(flops, moved):
        return pl.CostEstimate(flops=flops, transcendentals=0, bytes_accessed=moved)

    w1, w2 = pl.pallas_call(
        encoder_weights_body,
        out_shape=[
            jax.ShapeDtypeStruct((2 * LANES, hidden_lanes), BF16),
            jax.ShapeDtypeStruct((18 * LANES, 256), BF16),
        ],
        compiler_params=pltpu.CompilerParams(vmem_limit_bytes=12 << 20),
        cost_estimate=cost(10**9, 2 << 20),
        name="encoder_weights",
    )(encoder_one, encoder_two)
    wm, wd1, wd2 = pl.pallas_call(
        decoder_weights_body,
        out_shape=[
            jax.ShapeDtypeStruct((6 * LANES, 3 * LANES), BF16),
            jax.ShapeDtypeStruct((6 * LANES, 2 * LANES), BF16),
            jax.ShapeDtypeStruct((4 * hidden_lanes, 2 * LANES), BF16),
        ],
        compiler_params=pltpu.CompilerParams(vmem_limit_bytes=12 << 20),
        cost_estimate=cost(10**9, 4 << 20),
        name="decoder_weights",
    )(real_space, decoder_one.transpose(0, 1, 3, 2), decoder_two.transpose(0, 1, 3, 2))

    n_latent = latent_rows * cols
    n_hidden = (2 * latent_rows + 1) * cols

    def encode(strip_x, strip_halo):
        return pl.pallas_call(
            functools.partial(encode_body, strip=strip, cols=cols),
            out_shape=jax.ShapeDtypeStruct((n_latent, latent_lanes), F32),
            scratch_shapes=[pltpu.VMEM((n_hidden, LANES), F32)] * 3
            + [pltpu.VMEM((n_hidden, hidden_lanes + LANES), BF16)] * 2,
            compiler_params=pltpu.CompilerParams(vmem_limit_bytes=ENCODE_VMEM),
            cost_estimate=cost(2 * n_latent * 27 * LANES * latent_lanes * 8, 8 << 20),
            name="encode",
        )(strip_x, strip_halo, w1, w2)

    own = encode(x, halo)
    sibling = swapped(own, "scan", cores)
    other = encode(far_x, far_halo)
    rebuilt, part = pl.pallas_call(
        functools.partial(decode_body, strip=strip, cols=cols),
        out_shape=[
            jax.ShapeDtypeStruct((cols * strip, width), F32),
            jax.ShapeDtypeStruct((1, cols), F32),
        ],
        scratch_shapes=[
            pltpu.VMEM((n_latent, latent_lanes + 2 * LANES), F32),
            pltpu.VMEM(((strip // 2 + 2) * cols, hidden_lanes), BF16),
            pltpu.VMEM(((strip // 2 + 2) * cols, hidden_lanes), BF16),
        ],
        compiler_params=pltpu.CompilerParams(vmem_limit_bytes=DECODE_VMEM),
        cost_estimate=cost(2 * n_latent * 45 * LANES * latent_lanes, 16 << 20),
        name="decode",
    )(own, sibling, other, x, wm, wd1, wd2)
    if n_det == 4:
        misfit = part
        for turn in range(1, n_det):
            misfit = misfit + lax.ppermute(part, "det", [(i, (i + turn) % n_det) for i in range(n_det)])
    else:
        misfit = lax.psum(part, "det")
    return rebuilt.reshape(patterns.shape), misfit


def solution(mesh):
    return jax.shard_map(
        on_device,
        mesh=mesh,
        in_specs=(P("scan", None, "det", None), P(), P(), P(), P(), P()),
        out_specs=(P("scan", None, "det", None), P("scan", None)),
        check_vma=False,
    )
```

time: 108 us -> 66.2 us (0.61); the launches traced: 108 us -> 64.9 us
  Pallas kernels: 61.8 us -> 40.4 us
  blocking collectives: 11.2 us -> 0 us
  waiting for transfers between devices: 14.2 us -> 3.45 us
  starting transfers between devices: 10.4 us -> 16 us
  local copies, waits for them, and re-layouts: 9.12 us -> 3.66 us
    ppermute x3, waiting for transfers between devices: 14.2 us -> 0.12 us  [swapped(): lax.ppermute(value, axis, [(i, j) for i, j in pairs] + [(j, i) for i, j i...]
    pallas_call x2, Pallas kernels: 31.4 us -> 17.8 us  [encode(): pl.pallas_call(functools.partial(encode_body, strip=strip, cols=cols), ou...]
    psum x1 -> x0, blocking collectives: 11.2 us -> none  [on_device(): misfit = lax.psum(part, 'det') / (width * width)]
    ppermute x0 -> x3, starting transfers between devices: none -> 5.57 us  [on_device(): lax.ppermute(part, 'det', [(i, (i + turn) % n_det) for i in range(n_det)])]
    unnamed x15, local copies, waits for them, and re-layouts: 7.16 us -> 1.66 us
    pallas_call x1, Pallas kernels: 24.1 us -> 19.3 us  [on_device(): pl.pallas_call(functools.partial(decode_body, strip=strip, cols=cols), ou...]
    pallas_call x1 -> x2, Pallas kernels: 6.32 us -> 3.34 us  [the longest x1 1.85 us: on_device(): pl.pallas_call(decoder_weights_body, out_shape=[jax.ShapeDtypeStruct((6 *...]
    ppermute x0 -> x3, waiting for transfers between devices: none -> 2.98 us  [on_device(): lax.ppermute(part, 'det', [(i, (i + turn) % n_det) for i in range(n_det)])]
  transfers between devices with their start and end apart: 5 -> 8, of which waited for: 1 -> 4; matrix products, arithmetic and copies ran while one was open for 4% -> 2% of each run, Pallas kernels for 20% -> 33%
where the time goes in v1:
time: 66.2 us; the launch traced here: 64.9 us
  Pallas kernels  40.4 us (61%)
  starting transfers between devices  16 us (24%)
  local copies, waits for them, and re-layouts  3.66 us (6%)
  waiting for transfers between devices  3.45 us (5%)
  between operations  0.82 us (1%)
    pallas_call x1, Pallas kernels, on_device(): pl.pallas_call(functools.partial(decode_body, strip=strip, cols=cols), ou...  19.3 us
    pallas_call x2, Pallas kernels, encode(): pl.pallas_call(functools.partial(encode_body, strip=strip, cols=cols), ou...  17.8 us
    ppermute x3, starting transfers between devices, swapped(): lax.ppermute(value, axis, [(i, j) for i, j in pairs] + [(j, i) for i, j i...  5.77 us
    ppermute x3, starting transfers between devices, on_device(): lax.ppermute(part, 'det', [(i, (i + turn) % n_det) for i in range(n_det)])  5.57 us
    ppermute x1, starting transfers between devices, on_device(): lax.ppermute(patterns[0, :, strip - ABOVE:].transpose(1, 0, 2), 'det', down)  3.41 us
    ppermute x3, waiting for transfers between devices, on_device(): lax.ppermute(part, 'det', [(i, (i + turn) % n_det) for i in range(n_det)])  2.98 us
    pallas_call x1, Pallas kernels, on_device(): pl.pallas_call(decoder_weights_body, out_shape=[jax.ShapeDtypeStruct((6 *...  1.85 us
    unnamed x15, local copies, waits for them, and re-layouts  1.66 us
  transfers between devices with their start and end apart: 8, of which 4 were waited for; matrix products, arithmetic and copies ran while one was open for 2% of the time, Pallas kernels for 33%

profile of v1, /device:TPU:8, one launch (start us, length us, event | category | flops | bytes accessed | tf_op | source)
XLA Modules:
  0.0 64.9 jit_solution(13747665645197999507)
XLA Ops:
  0.6 0.0 copy-start.5
  0.6 0.0 copy-start.3
  0.7 0.0 copy-start.1
  0.7 1.0 %slice.6 = f32[1,64,7,128]{3,2,1,0:T(8,128)S(1)} slice(f32[1,64,32,128]{3,2,1,0:T(8,128)} %param.6), slice={[0:1], [0:64], [25:32], [0:128]} | slice | bytes 458752 | tf_op jit(solution)/shard_map/slice | solution.py:306
  1.7 3.4 %collective-permute-start = (f32[7,64,128]{2,1,0:T(8,128)S(1)}, f32[7,64,128]{2,1,0:T(8,128)S(1)}, u32[]{:S(2)}, u32[]{:S(2)}) collective-permute-start(f32[7,64,128]{2,1,0:T(8,128)S(1)} %bitcast.19), channel_id=1, source_target_pairs={{0,1},{1,2},{2,3},{4,5},{5,6},{6,7},{8,9},{9,10},{10,11},{12,13},{... | collective-permute-start | bytes 688136 | tf_op jit(solution)/shard_map/ppermute | solution.py:306
  5.2 1.0 %slice.7 = f32[1,64,4,128]{3,2,1,0:T(4,128)S(1)} slice(f32[1,64,32,128]{3,2,1,0:T(8,128)} %param.6), slice={[0:1], [0:64], [0:4], [0:128]} | slice | bytes 262144 | tf_op jit(solution)/shard_map/slice | solution.py:307
  6.1 1.3 %collective-permute-start.1 = (f32[4,64,128]{2,1,0:T(8,128)S(1)}, f32[4,64,128]{2,1,0:T(8,128)S(1)}, u32[]{:S(2)}, u32[]{:S(2)}) collective-permute-start(f32[4,64,128]{2,1,0:T(8,128)S(1)} %bitcast.20), channel_id=1, source_target_pairs={{1,0},{2,1},{3,2},{5,4},{6,5},{7,6},{9,8},{10,9},{11,10},{13,12},{... | collective-permute-start | bytes 393224 | tf_op jit(solution)/shard_map/ppermute | solution.py:307
  7.4 1.9 %collective-permute-start.3 = (f32[2048,128]{1,0:T(8,128)}, f32[2048,128]{1,0:T(8,128)S(1)}, u32[]{:S(2)}, u32[]{:S(2)}) collective-permute-start(f32[2048,128]{1,0:T(8,128)} %bitcast.14), channel_id=1, source_target_pairs={{4,8},{12,16},{20,24},{8,4},{16,12},{24,20},{5,9},{13,17},{21,25},... | collective-permute-start | bytes 3145736 | tf_op jit(solution)/shard_map/ppermute | solution.py:290
  9.4 0.0 copy-start.2
  9.4 0.9 %copy-done.2 = f32[3,3,16,32]{3,2,1,0:T(8,128)S(1)} copy-done((f32[3,3,16,32]{3,2,1,0:T(8,128)S(1)}, f32[3,3,16,32]{3,2,1,0:T(8,128)}, u32[]{:S(2)}) %copy-start.2) | copy-done | bytes 18456
  10.3 0.0 copy-start.4
  10.3 0.7 %copy-done.4 = f32[3,3,1,16]{3,2,1,0:T(1,128)S(1)} copy-done((f32[3,3,1,16]{3,2,1,0:T(1,128)S(1)}, f32[3,3,1,16]{3,2,1,0:T(1,128)}, u32[]{:S(2)}) %copy-start.4) | copy-done | bytes 600
  10.9 1.5 %encoder_weights.1 = (bf16[256,1024]{1,0:T(8,128)(2,1)S(1)}, bf16[2304,256]{1,0:T(8,128)(2,1)S(1)}) custom-call(f32[3,3,1,16]{3,2,1,0:T(1,128)S(1)} %copy-done.4, f32[3,3,16,32]{3,2,1,0:T(8,128)S(1)} %copy-done.2), custom_call_target="tpu_custom_call" | custom-call | flops 1000000000 | bytes 2097152 | tf_op jit(solution)/shard_map/encoder_weights/pallas_call | solution.py:317
  12.4 0.0 copy-start
  12.5 0.0 copy-done.5
  12.5 0.0 copy-done.3
  12.5 0.0 copy-done.1
  12.5 1.9 %decoder_weights.1 = (bf16[768,384]{1,0:T(8,128)(2,1)S(1)}, bf16[768,256]{1,0:T(8,128)(2,1)S(1)}, bf16[4096,256]{1,0:T(8,128)(2,1)S(1)}) custom-call(f32[3,3,32,32]{3,2,1,0:T(8,128)S(1)} %copy-done.1, f32[3,3,16,32]{3,2,1,0:T(8,128)S(1)} %bitcast.17, f32[3,3,1,16]{3,2,1,0:T(1,128)S(1)} %bitcast.18), custom_call_target="tpu_custom_call" | custom-call | flops 1000000000 | bytes 4194304 | tf_op jit(solution)/shard_map/decoder_weights/pallas_call | solution.py:327
  14.3 0.0 collective-permute-done
  14.4 0.4 collective-permute-done.1
  14.8 3.5 %collective-permute-start.4 = (f32[11,64,128]{2,1,0:T(8,128)S(1)}, f32[11,64,128]{2,1,0:T(8,128)S(1)}, u32[]{:S(2)}, u32[]{:S(2)}) collective-permute-start(f32[11,64,128]{2,1,0:T(8,128)S(1)} %constant_dynamic-update-slice_fusion.halo), channel_id=1, source_target_pairs={{4,8},{12,16},{20,24},{8,4},{16,12},{24,20},{5,9},{13,17},{21,25},... | collective-permute-start | bytes 1081352 | tf_op jit(solution)/shard_map/ppermute | solution.py:290
  18.2 0.0 copy-done
  18.3 8.9 %encode.2.own = f32[640,1024]{1,0:T(8,128)S(1)} custom-call(f32[2048,128]{1,0:T(8,128)S(1)} %bitcast.15, f32[11,64,128]{2,1,0:T(8,128)S(1)} %constant_dynamic-update-slice_fusion.halo, bf16[256,1024]{1,0:T(8,128)(2,1)S(1)} %get-tuple-element.9.w1, bf16[2304,256]{1,0:T(8,128)(2,1)S(1)} %get-tuple-element.10.w2), custom_call_target="tpu_custom_call" | custom-call | flops 36238786560 | bytes 8388608 | tf_op jit(solution)/shard_map/encode/pallas_call | solution.py:343
  27.2 0.4 collective-permute-start.2
  27.5 0.1 collective-permute-done.4.halo
  27.6 0.0 collective-permute-done.3.x
  27.6 8.9 %encode.3.other = f32[640,1024]{1,0:T(8,128)S(1)} custom-call(f32[2048,128]{1,0:T(8,128)S(1)} %collective-permute-done.3.x, f32[11,64,128]{2,1,0:T(8,128)S(1)} %collective-permute-done.4.halo, bf16[256,1024]{1,0:T(8,128)(2,1)S(1)} %get-tuple-element.9.w1, bf16[2304,256]{1,0:T(8,128)(2,1)S(1)} %get-tuple-element.10.w2), custom_call_target="tpu_custom_call" | custom-call | flops 36238786560 | bytes 8388608 | tf_op jit(solution)/shard_map/encode/pallas_call | solution.py:343
  36.5 0.0 collective-permute-done.2.sibling
  36.5 19.3 %decode.1 = (f32[2048,128]{1,0:T(8,128)}, f32[1,64]{1,0:T(1,128)S(1)}) custom-call(f32[640,1024]{1,0:T(8,128)S(1)} %encode.2.own, f32[640,1024]{1,0:T(8,128)S(1)} %collective-permute-done.2.sibling, f32[640,1024]{1,0:T(8,128)S(1)} %encode.3.other, f32[2048,128]{1,0:T(8,128)S(1)} %bitcast.16, bf16[768,384]{1,0:T(8,128)(2,1)S(1)} %get-tuple-element.11.wm, ...), custom_call_target="tpu_custom_call" | custom-call | flops 7549747200 | bytes 16777216 | tf_op jit(solution)/shard_map/decode/pallas_call | solution.py:356
  55.8 3.6 %collective-permute-start.7 = (f32[1,64]{1,0:T(1,128)S(1)}, f32[1,64]{1,0:T(1,128)S(1)}, u32[]{:S(2)}, u32[]{:S(2)}) collective-permute-start(f32[1,64]{1,0:T(1,128)S(1)} %get-tuple-element.15), channel_id=1, source_target_pairs={{0,3},{1,0},{2,1},{3,2},{4,7},{5,4},{6,5},{7,6},{8,11},{9,8},{10,9... | collective-permute-start | bytes 776 | tf_op jit(solution)/shard_map/ppermute | solution.py:374
  59.4 0.5 collective-permute-start.6
  59.9 1.5 %collective-permute-start.5 = (f32[1,64]{1,0:T(1,128)S(1)}, f32[1,64]{1,0:T(1,128)S(1)}, u32[]{:S(2)}, u32[]{:S(2)}) collective-permute-start(f32[1,64]{1,0:T(1,128)S(1)} %get-tuple-element.15), channel_id=1, source_target_pairs={{0,1},{1,2},{2,3},{3,0},{4,5},{5,6},{6,7},{7,4},{8,9},{9,10},{10,1... | collective-permute-start | bytes 776 | tf_op jit(solution)/shard_map/ppermute | solution.py:374
  61.4 0.0 collective-permute-done.7
  61.4 1.6 %collective-permute-done.6 = f32[1,64]{1,0:T(1,128)S(1)} collective-permute-done((f32[1,64]{1,0:T(1,128)S(1)}, f32[1,64]{1,0:T(1,128)S(1)}, u32[]{:S(2)}, u32[]{:S(2)}) %collective-permute-start.6) | collective-permute-done | bytes 288 | tf_op jit(solution)/shard_map/ppermute | solution.py:374
  63.0 1.4 %collective-permute-done.5 = f32[1,64]{1,0:T(1,128)S(1)} collective-permute-done((f32[1,64]{1,0:T(1,128)S(1)}, f32[1,64]{1,0:T(1,128)S(1)}, u32[]{:S(2)}, u32[]{:S(2)}) %collective-permute-start.5) | collective-permute-done | bytes 288 | tf_op jit(solution)/shard_map/ppermute | solution.py:374
  64.4 0.5 add_add_fusion
  (4 shorter events, 0.1 us)
Async XLA Ops:
  0.6 11.8 %copy-start.5 = (f32[3,3,16,1]{2,3,1,0:T(1,128)S(1)}, f32[3,3,16,1]{2,3,1,0:T(1,128)}, u32[]{:S(2)}) copy-start(f32[3,3,16,1]{2,3,1,0:T(1,128)} %param.11) | copy-start | bytes 1732
  0.6 11.8 %copy-start.3 = (f32[3,3,32,16]{2,3,1,0:T(8,128)S(1)}, f32[3,3,32,16]{2,3,1,0:T(8,128)}, u32[]{:S(2)}) copy-start(f32[3,3,32,16]{2,3,1,0:T(8,128)} %param.10) | copy-start | bytes 55300
  0.7 11.8 %copy-start.1 = (f32[3,3,32,32]{3,2,1,0:T(8,128)S(1)}, f32[3,3,32,32]{3,2,1,0:T(8,128)}, u32[]{:S(2)}) copy-start(f32[3,3,32,32]{3,2,1,0:T(8,128)} %rs.1) | copy-start | bytes 110596
  1.7 12.6 %collective-permute-start = (f32[7,64,128]{2,1,0:T(8,128)S(1)}, f32[7,64,128]{2,1,0:T(8,128)S(1)}, u32[]{:S(2)}, u32[]{:S(2)}) collective-permute-start(f32[7,64,128]{2,1,0:T(8,128)S(1)} %bitcast.19), channel_id=1, source_target_pairs={{0,1},{1,2},{2,3},{4,5},{5,6},{6,7},{8,9},{9,10},{10,11},{12,13},{... | collective-permute-start | bytes 688136 | tf_op jit(solution)/shard_map/ppermute | solution.py:306
  6.1 8.6 %collective-permute-start.1 = (f32[4,64,128]{2,1,0:T(8,128)S(1)}, f32[4,64,128]{2,1,0:T(8,128)S(1)}, u32[]{:S(2)}, u32[]{:S(2)}) collective-permute-start(f32[4,64,128]{2,1,0:T(8,128)S(1)} %bitcast.20), channel_id=1, source_target_pairs={{1,0},{2,1},{3,2},{5,4},{6,5},{7,6},{9,8},{10,9},{11,10},{13,12},{... | collective-permute-start | bytes 393224 | tf_op jit(solution)/shard_map/ppermute | solution.py:307
  7.4 20.2 %collective-permute-start.3 = (f32[2048,128]{1,0:T(8,128)}, f32[2048,128]{1,0:T(8,128)S(1)}, u32[]{:S(2)}, u32[]{:S(2)}) collective-permute-start(f32[2048,128]{1,0:T(8,128)} %bitcast.14), channel_id=1, source_target_pairs={{4,8},{12,16},{20,24},{8,4},{16,12},{24,20},{5,9},{13,17},{21,25},... | collective-permute-start | bytes 3145736 | tf_op jit(solution)/shard_map/ppermute | solution.py:290
  9.4 0.9 %copy-start.2 = (f32[3,3,16,32]{3,2,1,0:T(8,128)S(1)}, f32[3,3,16,32]{3,2,1,0:T(8,128)}, u32[]{:S(2)}) copy-start(f32[3,3,16,32]{3,2,1,0:T(8,128)} %e2.1) | copy-start | bytes 55300
  10.3 0.7 %copy-start.4 = (f32[3,3,1,16]{3,2,1,0:T(1,128)S(1)}, f32[3,3,1,16]{3,2,1,0:T(1,128)}, u32[]{:S(2)}) copy-start(f32[3,3,1,16]{3,2,1,0:T(1,128)} %e1.1) | copy-start | bytes 1732
  12.4 5.8 %copy-start = (f32[1,64,32,128]{3,2,1,0:T(8,128)S(1)}, f32[1,64,32,128]{3,2,1,0:T(8,128)}, u32[]{:S(2)}) copy-start(f32[1,64,32,128]{3,2,1,0:T(8,128)} %param.6) | copy-start | bytes 3145732
  14.8 12.9 %collective-permute-start.4 = (f32[11,64,128]{2,1,0:T(8,128)S(1)}, f32[11,64,128]{2,1,0:T(8,128)S(1)}, u32[]{:S(2)}, u32[]{:S(2)}) collective-permute-start(f32[11,64,128]{2,1,0:T(8,128)S(1)} %constant_dynamic-update-slice_fusion.halo), channel_id=1, source_target_pairs={{4,8},{12,16},{20,24},{8,4},{16,12},{24,20},{5,9},{13,17},{21,25},... | collective-permute-start | bytes 1081352 | tf_op jit(solution)/shard_map/ppermute | solution.py:290
  27.2 9.4 %collective-permute-start.2 = (f32[640,1024]{1,0:T(8,128)S(1)}, f32[640,1024]{1,0:T(8,128)S(1)}, u32[]{:S(2)}, u32[]{:S(2)}) collective-permute-start(f32[640,1024]{1,0:T(8,128)S(1)} %encode.2.own), channel_id=1, source_target_pairs={{0,4},{8,12},{16,20},{24,28},{4,0},{12,8},{20,16},{28,24},{1,5},{9... | collective-permute-start | bytes 7864328 | tf_op jit(solution)/shard_map/ppermute | solution.py:290
  55.8 5.6 %collective-permute-start.7 = (f32[1,64]{1,0:T(1,128)S(1)}, f32[1,64]{1,0:T(1,128)S(1)}, u32[]{:S(2)}, u32[]{:S(2)}) collective-permute-start(f32[1,64]{1,0:T(1,128)S(1)} %get-tuple-element.15), channel_id=1, source_target_pairs={{0,3},{1,0},{2,1},{3,2},{4,7},{5,4},{6,5},{7,6},{8,11},{9,8},{10,9... | collective-permute-start | bytes 776 | tf_op jit(solution)/shard_map/ppermute | solution.py:374
  59.4 3.5 %collective-permute-start.6 = (f32[1,64]{1,0:T(1,128)S(1)}, f32[1,64]{1,0:T(1,128)S(1)}, u32[]{:S(2)}, u32[]{:S(2)}) collective-permute-start(f32[1,64]{1,0:T(1,128)S(1)} %get-tuple-element.15), channel_id=1, source_target_pairs={{0,2},{1,3},{2,0},{3,1},{4,6},{5,7},{6,4},{7,5},{8,10},{9,11},{10,... | collective-permute-start | bytes 776 | tf_op jit(solution)/shard_map/ppermute | solution.py:374
  59.9 4.4 %collective-permute-start.5 = (f32[1,64]{1,0:T(1,128)S(1)}, f32[1,64]{1,0:T(1,128)S(1)}, u32[]{:S(2)}, u32[]{:S(2)}) collective-permute-start(f32[1,64]{1,0:T(1,128)S(1)} %get-tuple-element.15), channel_id=1, source_target_pairs={{0,1},{1,2},{2,3},{3,0},{4,5},{5,6},{6,7},{7,4},{8,9},{9,10},{10,1... | collective-permute-start | bytes 776 | tf_op jit(solution)/shard_map/ppermute | solution.py:374

commit v2 on v1

--- a/solution.py
+++ b/solution.py
@@ -62,7 +62,24 @@
 ROW_TAPS = {(0, 0): (0, 1), (1, 0): (2,), (0, 1): (0,), (1, 1): (1, 2)}
 
 
-def encoder_weights_body(e1, e2, w1, w2):
+def own_lane(shape):
+    return iota(shape, len(shape) - 1) ^ (lax.axis_index("scan") % 2 * (LANES // 2))
+
+
+def weights_body(*refs):
+    sources, outputs, targets, sems = refs[:5], refs[5:10], refs[10:15], refs[15]
+    copies = [pltpu.make_async_copy(a, b, sems.at[i]) for i, (a, b) in enumerate(zip(sources, targets))]
+    for copy in copies:
+        copy.start()
+    for copy in copies:
+        copy.wait()
+    e1, e2, rs, d1, d2 = targets
+    w1, w2, wm, wd1, wd2 = outputs
+    encoder_weights(e1, e2, w1, w2)
+    decoder_weights(rs, d1, d2, wm, wd1, wd2)
+
+
+def encoder_weights(e1, e2, w1, w2):
     f1 = e1.shape[3]
     f2 = e2.shape[3]
     wide = spread(mosaic(e1), w1.shape[1])
@@ -81,36 +98,57 @@
         value = jnp.where(key == tap, wide[tap : tap + 1, :], value)
     put(w1, 0, value)
     wide = spread(mosaic(e2), w2.shape[1])
-    shape = (3 * LANES, w2.shape[1])
-    delta = iota(shape, 0) // f1 - LANES // f1 - 2 * (iota(shape, 1) // f2) + 1
+    shape = (256, w2.shape[1])
+    out_col = own_lane(shape) // f2
+    delta = iota(shape, 0) // f1 - 2 * out_col + 1
     for a in range(3):
         value = jnp.zeros(shape, F32)
         for b in range(3):
             tap = wide[(3 * a + b) * f1 : (3 * a + b + 1) * f1]
             value = jnp.where(delta == b, stack(tap, shape[0] // f1), value)
         put(w2, a * shape[0], value)
-
-
-def decoder_weights_body(rs, d1, d2, wm, wd1, wd2):
+    shape = (LANES, w2.shape[1])
+    slot = iota(shape, 0) // f1
+    value = jnp.zeros(shape, F32)
+    for a, at in enumerate((LANES // f1 - 1, 0, 1)):
+        tap = stack(wide[3 * a * f1 : (3 * a + 1) * f1], LANES // f1)
+        value = jnp.where((slot == at) & (own_lane(shape) // f2 == 0), tap, value)
+    put(w2, 3 * 256, value)
+
+
+def decoder_weights(rs, d1, d2, wm, wd1, wd2):
     f2, f1 = d1.shape[3], d1.shape[2]
     odd = lax.axis_index("scan") % 2
     shape = (LANES, LANES)
-    same = iota(shape, 0) // f2 == iota(shape, 1) // f2
     wide = spread(mosaic(rs), LANES)
-    tap = {(a, b): wide[(3 * a + b) * f2 : (3 * a + b + 1) * f2] for a in range(3) for b in range(3)}
-    for place in range(3):
-        for b in range(3):
-            if place == 0:
-                block = tap[1, b]
+
+    def tap(a, b):
+        return stack(wide[(3 * a + b) * f2 : (3 * a + b + 1) * f2], LANES // f2)
+
+    def outer(first, b):
+        return jnp.where(odd == first, tap(0, b), tap(2, b))
+
+    k = iota(shape, 0) ^ (odd * (LANES // 2))
+    n = own_lane(shape)
+    same = (k // f2) % 2 == (n // f2) % 2
+    for half in range(2):
+        row_here = k // (LANES // 2) == half
+        col_here = n // (LANES // 2) == half
+        for part in range(2):
+            if part == 0:
+                block = [jnp.where(row_here, tap(1, b), outer(1, b)) for b in range(3)]
+                good = same
             else:
-                block = jnp.where(odd == (0 if place == 2 else 1), tap[0, b], tap[2, b])
-            value = jnp.where(same, stack(block, LANES // f2), 0.0)
-            put(wm, place * LANES, value, slice(b * LANES, (b + 1) * LANES))
+                block = [outer(0, b) for b in range(3)]
+                good = same & row_here
+            sides = jnp.where(good, jnp.where(col_here, block[0], block[2]), 0.0)
+            centre = jnp.where(good & col_here, block[1], 0.0)
+            put(wm, part * LANES, sides, slice(half * 256, half * 256 + LANES))
+            put(wm, part * LANES, centre, slice(half * 256 + LANES, half * 256 + 256))
     per = LANES // f2
     wide = spread(jnp.concatenate([d1[a, b].T for a in range(3) for b in range(3)], axis=0), LANES)
     tap = {(a, b): wide[(3 * a + b) * f2 : (3 * a + b + 1) * f2] for a in range(3) for b in range(3)}
     w_local = iota(shape, 1) // f1
-    k = iota(shape, 0)
     for p in range(2):
         lanes = slice(p * LANES, (p + 1) * LANES)
         wide_edge = jnp.zeros(shape, F32)
@@ -145,7 +183,9 @@
             put(wd2, r * depth, value, slice(p * LANES, (p + 1) * LANES))
 
 
-def encode_body(x, halo, w1, w2, out, tap0, tap1, tap2, high_map, low_map, *, strip, cols):
+def encode_body(
+    x, halo, w1, w2, out, tap0, tap1, tap2, high_map, low_map, high_edge, low_edge, *, strip, cols, step
+):
     rows = strip + ABOVE + BELOW
     n_odd = strip // 4 + 2
     n_even = n_odd + 1
@@ -170,35 +210,43 @@
             if e > 0:
                 tap2[place(e // 2 - 1), :] = pltpu.roll(value, 2 * TAPS, 1)
     total = high_map.shape[0]
-    for ref in (high_map, low_map):
-        ref[:, :LANES] = jnp.zeros((total, LANES), BF16)
+    n = n_odd * cols
+    for ref in (high_edge, low_edge):
+        ref[:, :LANES] = jnp.zeros((n, LANES), BF16)
     lane = iota((total, LANES), 1)
+    edge_lane = iota((n, LANES), 1)
+    groups = high_map.shape[1] // 256
 
     def first(g, carry):
         lanes = pl.ds(pl.multiple_of(g * 256, 256), 256)
-        target = pl.ds(pl.multiple_of(LANES + g * 256, LANES), 256)
         at = (lane - 32 * g + 1) & (LANES - 1)
         packed = jnp.where(at < TAPS, tap0[...], jnp.where(at < 2 * TAPS, tap1[...], tap2[...]))
         high, low = split(packed)
         left = jnp.concatenate([high, low, high], axis=1)
         value = silu(jnp.dot(left, thrice(w1.at[:, lanes]), preferred_element_type=F32))
         high, low = split(value)
-        high_map[:, target] = high
-        low_map[:, target] = low
+        high_map[:, lanes] = high
+        low_map[:, lanes] = low
+        last = value[:, LANES:]
+        one = pltpu.roll(last[odd_start:], step, 1)
+        two = pltpu.roll(last[cols:odd_start], 2 * step, 1)
+        edge = jnp.where(edge_lane < step, one, jnp.where(edge_lane < 2 * step, two, last[:n]))
+        high, low = split(edge)
+        target = pl.ds(pl.multiple_of((g + 1) * LANES, LANES), LANES)
+        high_edge[:, target] = high
+        low_edge[:, target] = low
         return carry
 
-    groups = (high_map.shape[1] - LANES) // 256
     lax.fori_loop(0, groups, first, 0)
-    n = n_odd * cols
 
     def second(g, carry):
-        source = pl.ds(pl.multiple_of(g * 256, 256), 3 * LANES)
+        source = pl.ds(pl.multiple_of(g * 256, 256), 256)
+        beside = pl.ds(pl.multiple_of(g * LANES, LANES), LANES)
         starts = (0, odd_start, cols)
-        high = [high_map[start : start + n, source] for start in starts]
-        low = [low_map[start : start + n, source] for start in starts]
+        high = [high_map[start : start + n, source] for start in starts] + [high_edge[:, beside]]
+        low = [low_map[start : start + n, source] for start in starts] + [low_edge[:, beside]]
         left = jnp.concatenate(high + low + high, axis=1)
-        value = silu(jnp.dot(left, thrice(w2), preferred_element_type=F32))
-        out[:, pl.ds(pl.multiple_of(g * 256, 256), 256)] = value
+        out[:, source] = silu(jnp.dot(left, thrice(w2), preferred_element_type=F32))
         return carry
 
     lax.fori_loop(0, groups, second, 0)
@@ -214,17 +262,24 @@
     mixed[:, :LANES] = jnp.zeros((n, LANES), F32)
     mixed[:, (blocks + 1) * LANES :] = jnp.zeros((n, LANES), F32)
     position = iota((n, LANES), 0) % cols
+    below = own_lane((n, LANES)) < LANES // 2
 
     def mix(q, carry):
         lanes = pl.ds(pl.multiple_of(q * LANES, LANES), LANES)
-        pairs = [split(ref[:, lanes]) for ref in (own, sibling, other)]
-        high = [h for h, _ in pairs]
-        low = [v for _, v in pairs]
-        left = jnp.concatenate(high + low + high, axis=1)
-        y = jnp.dot(left, thrice(wm), preferred_element_type=F32)
-        before = jnp.where(position == 0, 0.0, pltpu.roll(y[:, :LANES], 1, 0))
-        after = jnp.where(position == cols - 1, 0.0, pltpu.roll(y[:, 2 * LANES :], n - 1, 0))
-        value = own[:, lanes] + silu(y[:, LANES : 2 * LANES] + before + after)
+        mine, beside = own[:, lanes], sibling[:, lanes]
+        other_high, other_low = split(other[:, lanes])
+        sides, centres = [], []
+        for half, joined in enumerate((jnp.where(below, mine, beside), jnp.where(below, beside, mine))):
+            high, low = split(joined)
+            left = jnp.concatenate([high, other_high, low, other_low, high, other_high], axis=1)
+            y = jnp.dot(left, thrice(wm.at[:, half * 256 : half * 256 + 256]), preferred_element_type=F32)
+            sides.append(y[:, :LANES])
+            centres.append(y[:, LANES:])
+        before = pltpu.roll(jnp.where(below, sides[0], sides[1]), 1, 0)
+        after = pltpu.roll(pltpu.roll(jnp.where(below, sides[1], sides[0]), LANES // 2, 1), n - 1, 0)
+        before = jnp.where(position == 0, 0.0, before)
+        after = jnp.where(position == cols - 1, 0.0, after)
+        value = mine + silu(centres[0] + centres[1] + before + after)
         target = pl.ds(pl.multiple_of((q + 1) * LANES, LANES), LANES)
         mixed[: n - cols, target] = value[: n - cols]
         mixed[n - cols :, target] = value[n - cols :] * not_last
@@ -232,9 +287,9 @@
 
     lax.fori_loop(0, blocks, mix, 0)
     count = n - cols
-    lane = iota((count, LANES), 1)
+    lane = own_lane((count, LANES))
     middle = (lane >= 32) & (lane < 96)
-    outer = iota((n, LANES), 1) >= 96
+    outer = own_lane((n, LANES)) >= 96
 
     def first(q, carry):
         here = pl.ds(pl.multiple_of((q + 1) * LANES, LANES), LANES)
@@ -303,8 +358,11 @@
 
     down = [(i, i + 1) for i in range(n_det - 1)]
     up = [(i + 1, i) for i in range(n_det - 1)]
-    above = lax.ppermute(patterns[0, :, strip - ABOVE :].transpose(1, 0, 2), "det", down)
-    below = lax.ppermute(patterns[0, :, :BELOW].transpose(1, 0, 2), "det", up)
+    last, first = lax.optimization_barrier(
+        (patterns[0, :, strip - ABOVE :].transpose(1, 0, 2), patterns[0, :, :BELOW].transpose(1, 0, 2))
+    )
+    above = lax.ppermute(last, "det", down)
+    below = lax.ppermute(first, "det", up)
     chips = [(i, i + 1) for i in range(1, n_scan - 1, 2)]
     cores = [(i, i + 1) for i in range(0, n_scan, 2)]
     far_x = swapped(x, "scan", chips)
@@ -314,37 +372,40 @@
     def cost(flops, moved):
         return pl.CostEstimate(flops=flops, transcendentals=0, bytes_accessed=moved)
 
-    w1, w2 = pl.pallas_call(
-        encoder_weights_body,
+    weights = (
+        encoder_one,
+        encoder_two,
+        real_space,
+        decoder_one.transpose(0, 1, 3, 2),
+        decoder_two.transpose(0, 1, 3, 2),
+    )
+    w1, w2, wm, wd1, wd2 = pl.pallas_call(
+        weights_body,
+        in_specs=[pl.BlockSpec(memory_space=pltpu.HBM)] * len(weights),
         out_shape=[
             jax.ShapeDtypeStruct((2 * LANES, hidden_lanes), BF16),
-            jax.ShapeDtypeStruct((18 * LANES, 256), BF16),
-        ],
-        compiler_params=pltpu.CompilerParams(vmem_limit_bytes=12 << 20),
-        cost_estimate=cost(10**9, 2 << 20),
-        name="encoder_weights",
-    )(encoder_one, encoder_two)
-    wm, wd1, wd2 = pl.pallas_call(
-        decoder_weights_body,
-        out_shape=[
-            jax.ShapeDtypeStruct((6 * LANES, 3 * LANES), BF16),
+            jax.ShapeDtypeStruct((14 * LANES, 256), BF16),
+            jax.ShapeDtypeStruct((4 * LANES, 4 * LANES), BF16),
             jax.ShapeDtypeStruct((6 * LANES, 2 * LANES), BF16),
             jax.ShapeDtypeStruct((4 * hidden_lanes, 2 * LANES), BF16),
         ],
-        compiler_params=pltpu.CompilerParams(vmem_limit_bytes=12 << 20),
+        scratch_shapes=[pltpu.VMEM(w.shape, F32) for w in weights]
+        + [pltpu.SemaphoreType.DMA((len(weights),))],
+        compiler_params=pltpu.CompilerParams(vmem_limit_bytes=16 << 20),
         cost_estimate=cost(10**9, 4 << 20),
-        name="decoder_weights",
-    )(real_space, decoder_one.transpose(0, 1, 3, 2), decoder_two.transpose(0, 1, 3, 2))
+        name="weights",
+    )(*[pltpu.with_memory_space_constraint(w, pltpu.HBM) for w in weights])
 
     n_latent = latent_rows * cols
     n_hidden = (2 * latent_rows + 1) * cols
 
     def encode(strip_x, strip_halo):
         return pl.pallas_call(
-            functools.partial(encode_body, strip=strip, cols=cols),
+            functools.partial(encode_body, strip=strip, cols=cols, step=f1),
             out_shape=jax.ShapeDtypeStruct((n_latent, latent_lanes), F32),
             scratch_shapes=[pltpu.VMEM((n_hidden, LANES), F32)] * 3
-            + [pltpu.VMEM((n_hidden, hidden_lanes + LANES), BF16)] * 2,
+            + [pltpu.VMEM((n_hidden, hidden_lanes), BF16)] * 2
+            + [pltpu.VMEM((n_latent, hidden_lanes // 2 + LANES), BF16)] * 2,
             compiler_params=pltpu.CompilerParams(vmem_limit_bytes=ENCODE_VMEM),
             cost_estimate=cost(2 * n_latent * 27 * LANES * latent_lanes * 8, 8 << 20),
             name="encode",

time: 66.2 us -> 63.3 us (0.956)
  Pallas kernels: 40.4 us -> 38 us
  waiting for transfers between devices: 3.45 us -> 5.22 us
  local copies, waits for them, and re-layouts: 3.66 us -> 2.04 us
    pallas_call x1, Pallas kernels: 19.3 us -> 17.2 us  [on_device(): pl.pallas_call(functools.partial(decode_body, strip=strip, cols=cols), ou...]
    ppermute x2, waiting for transfers between devices: 0.35 us -> 2.26 us  [the longest x1 2.26 us: on_device(): below = lax.ppermute(first, 'det', up)]
    unnamed x15 -> x5, local copies, waits for them, and re-layouts: 1.66 us -> 0.08 us
    pallas_call x4 -> x3, Pallas kernels: 21.1 us -> 20.8 us  [the longest x2 16.7 us: encode(): pl.pallas_call(functools.partial(encode_body, strip=strip, cols=cols, ste...]
  transfers between devices with their start and end apart: 8 -> 8, of which waited for: 4 -> 3; matrix products, arithmetic and copies ran while one was open for 2% -> 0% of each run, Pallas kernels for 33% -> 33%
where the time goes in v2:
time: 63.3 us; the launch traced here: 62.4 us
  Pallas kernels  38 us (60%)
  starting transfers between devices  15.9 us (25%)
  waiting for transfers between devices  5.22 us (8%)
  local copies, waits for them, and re-layouts  2.04 us (3%)
  between operations  0.76 us (1%)
    pallas_call x1, Pallas kernels, on_device(): pl.pallas_call(functools.partial(decode_body, strip=strip, cols=cols), ou...  17.2 us
    pallas_call x2, Pallas kernels, encode(): pl.pallas_call(functools.partial(encode_body, strip=strip, cols=cols, ste...  16.7 us
    ppermute x3, starting transfers between devices, swapped(): lax.ppermute(value, axis, [(i, j) for i, j in pairs] + [(j, i) for i, j i...  5.78 us
    ppermute x3, starting transfers between devices, on_device(): lax.ppermute(part, 'det', [(i, (i + turn) % n_det) for i in range(n_det)])  5.25 us
    pallas_call x1, Pallas kernels, on_device(): pl.pallas_call(weights_body, in_specs=[pl.BlockSpec(memory_space=pltpu.HB...  4.05 us
    ppermute x1, starting transfers between devices, on_device(): above = lax.ppermute(last, 'det', down)  3.54 us
    ppermute x3, waiting for transfers between devices, on_device(): lax.ppermute(part, 'det', [(i, (i + turn) % n_det) for i in range(n_det)])  2.95 us
    ppermute x1, waiting for transfers between devices, on_device(): below = lax.ppermute(first, 'det', up)  2.26 us
  transfers between devices with their start and end apart: 8, of which 3 were waited for; matrix products, arithmetic and copies ran while one was open for 0% of the time, Pallas kernels for 33%

profile of v2, /device:TPU:8, one launch (start us, length us, event | category | flops | bytes accessed | tf_op | source)
XLA Modules:
  0.0 62.4 jit_solution(14135703666846944389)
XLA Ops:
  0.6 1.0 %slice.7 = f32[1,64,4,128]{3,2,1,0:T(4,128)S(1)} slice(f32[1,64,32,128]{3,2,1,0:T(8,128)} %param.6), slice={[0:1], [0:64], [0:4], [0:128]} | slice | bytes 262144 | tf_op jit(solution)/shard_map/slice | solution.py:362
  1.6 1.0 %slice.6 = f32[1,64,7,128]{3,2,1,0:T(8,128)S(1)} slice(f32[1,64,32,128]{3,2,1,0:T(8,128)} %param.6), slice={[0:1], [0:64], [25:32], [0:128]} | slice | bytes 458752 | tf_op jit(solution)/shard_map/slice | solution.py:362
  2.6 0.0 copy-start
  2.7 3.5 %collective-permute-start = (f32[7,64,128]{2,1,0:T(8,128)S(1)}, f32[7,64,128]{2,1,0:T(8,128)S(1)}, u32[]{:S(2)}, u32[]{:S(2)}) collective-permute-start(f32[7,64,128]{2,1,0:T(8,128)S(1)} %bitcast.17), channel_id=1, source_target_pairs={{0,1},{1,2},{2,3},{4,5},{5,6},{6,7},{8,9},{9,10},{10,11},{12,13},{... | collective-permute-start | bytes 688136 | tf_op jit(solution)/shard_map/ppermute | solution.py:364
  6.2 1.3 %collective-permute-start.1 = (f32[4,64,128]{2,1,0:T(8,128)S(1)}, f32[4,64,128]{2,1,0:T(8,128)S(1)}, u32[]{:S(2)}, u32[]{:S(2)}) collective-permute-start(f32[4,64,128]{2,1,0:T(8,128)S(1)} %bitcast.18), channel_id=1, source_target_pairs={{1,0},{2,1},{3,2},{5,4},{6,5},{7,6},{9,8},{10,9},{11,10},{13,12},{... | collective-permute-start | bytes 393224 | tf_op jit(solution)/shard_map/ppermute | solution.py:365
  7.5 1.9 %collective-permute-start.3 = (f32[2048,128]{1,0:T(8,128)}, f32[2048,128]{1,0:T(8,128)S(1)}, u32[]{:S(2)}, u32[]{:S(2)}) collective-permute-start(f32[2048,128]{1,0:T(8,128)} %bitcast.14), channel_id=1, source_target_pairs={{4,8},{12,16},{20,24},{8,4},{16,12},{24,20},{5,9},{13,17},{21,25},... | collective-permute-start | bytes 3145736 | tf_op jit(solution)/shard_map/ppermute | solution.py:345
  9.4 4.1 %weights.1 = (bf16[256,1024]{1,0:T(8,128)(2,1)S(1)}, bf16[1792,256]{1,0:T(8,128)(2,1)S(1)}, bf16[512,512]{1,0:T(8,128)(2,1)S(1)}, bf16[768,256]{1,0:T(8,128)(2,1)S(1)}, bf16[4096,256]{1,0:T(8,128)(2,1)S(1)}) custom-call(f32[3,3,1,16]{3,2,1,0:T(1,128)} %refs_0_.1, f32[3,3,16,32]{3,2,1,0:T(8,128)} %refs_1_.1, f32[3,3,32,32]{3,2,1,0:T(8,128)} %refs_2_.1, ...), custom_call_target="tpu_custom_call" | custom-call | flops 1000000000 | bytes 4194304 | tf_op jit(solution)/shard_map/weights/pallas_call | solution.py:382
  13.5 0.0 collective-permute-done
  13.5 2.3 %collective-permute-done.1 = f32[4,64,128]{2,1,0:T(8,128)S(1)} collective-permute-done((f32[4,64,128]{2,1,0:T(8,128)S(1)}, f32[4,64,128]{2,1,0:T(8,128)S(1)}, u32[]{:S(2)}, u32[]{:S(2)}) %collective-permute-start.1) | collective-permute-done | bytes 131104 | tf_op jit(solution)/shard_map/ppermute | solution.py:365
  15.8 2.1 %collective-permute-start.4 = (f32[11,64,128]{2,1,0:T(8,128)S(1)}, f32[11,64,128]{2,1,0:T(8,128)S(1)}, u32[]{:S(2)}, u32[]{:S(2)}) collective-permute-start(f32[11,64,128]{2,1,0:T(8,128)S(1)} %constant_dynamic-update-slice_fusion.halo), channel_id=1, source_target_pairs={{4,8},{12,16},{20,24},{8,4},{16,12},{24,20},{5,9},{13,17},{21,25},... | collective-permute-start | bytes 1081352 | tf_op jit(solution)/shard_map/ppermute | solution.py:345
  17.9 0.0 copy-done
  17.9 8.4 %encode.2.own = f32[640,1024]{1,0:T(8,128)S(1)} custom-call(f32[2048,128]{1,0:T(8,128)S(1)} %bitcast.15, f32[11,64,128]{2,1,0:T(8,128)S(1)} %constant_dynamic-update-slice_fusion.halo, bf16[256,1024]{1,0:T(8,128)(2,1)S(1)} %get-tuple-element.13.w1, bf16[1792,256]{1,0:T(8,128)(2,1)S(1)} %get-tuple-element.14.w2), custom_call_target="tpu_custom_call" | custom-call | flops 36238786560 | bytes 8388608 | tf_op jit(solution)/shard_map/encode/pallas_call | solution.py:403
  26.3 1.8 %collective-permute-start.2 = (f32[640,1024]{1,0:T(8,128)S(1)}, f32[640,1024]{1,0:T(8,128)S(1)}, u32[]{:S(2)}, u32[]{:S(2)}) collective-permute-start(f32[640,1024]{1,0:T(8,128)S(1)} %encode.2.own), channel_id=1, source_target_pairs={{0,4},{8,12},{16,20},{24,28},{4,0},{12,8},{20,16},{28,24},{1,5},{9... | collective-permute-start | bytes 7864328 | tf_op jit(solution)/shard_map/ppermute | solution.py:345
  28.1 0.0 collective-permute-done.4.halo
  28.1 0.0 collective-permute-done.3.x
  28.1 8.4 %encode.3.other = f32[640,1024]{1,0:T(8,128)S(1)} custom-call(f32[2048,128]{1,0:T(8,128)S(1)} %collective-permute-done.3.x, f32[11,64,128]{2,1,0:T(8,128)S(1)} %collective-permute-done.4.halo, bf16[256,1024]{1,0:T(8,128)(2,1)S(1)} %get-tuple-element.13.w1, bf16[1792,256]{1,0:T(8,128)(2,1)S(1)} %get-tuple-element.14.w2), custom_call_target="tpu_custom_call" | custom-call | flops 36238786560 | bytes 8388608 | tf_op jit(solution)/shard_map/encode/pallas_call | solution.py:403
  36.4 0.0 collective-permute-done.2.sibling
  36.4 17.2 %decode.1 = (f32[2048,128]{1,0:T(8,128)}, f32[1,64]{1,0:T(1,128)S(1)}) custom-call(f32[640,1024]{1,0:T(8,128)S(1)} %encode.2.own, f32[640,1024]{1,0:T(8,128)S(1)} %collective-permute-done.2.sibling, f32[640,1024]{1,0:T(8,128)S(1)} %encode.3.other, f32[2048,128]{1,0:T(8,128)S(1)} %bitcast.16, bf16[512,512]{1,0:T(8,128)(2,1)S(1)} %get-tuple-element.15.wm, ...), custom_call_target="tpu_custom_call" | custom-call | flops 7549747200 | bytes 16777216 | tf_op jit(solution)/shard_map/decode/pallas_call | solution.py:417
  53.7 3.2 %collective-permute-start.7 = (f32[1,64]{1,0:T(1,128)S(1)}, f32[1,64]{1,0:T(1,128)S(1)}, u32[]{:S(2)}, u32[]{:S(2)}) collective-permute-start(f32[1,64]{1,0:T(1,128)S(1)} %get-tuple-element.19), channel_id=1, source_target_pairs={{0,3},{1,0},{2,1},{3,2},{4,7},{5,4},{6,5},{7,6},{8,11},{9,8},{10,9... | collective-permute-start | bytes 776 | tf_op jit(solution)/shard_map/ppermute | solution.py:435
  56.9 0.5 collective-permute-start.6
  57.4 1.5 %collective-permute-start.5 = (f32[1,64]{1,0:T(1,128)S(1)}, f32[1,64]{1,0:T(1,128)S(1)}, u32[]{:S(2)}, u32[]{:S(2)}) collective-permute-start(f32[1,64]{1,0:T(1,128)S(1)} %get-tuple-element.19), channel_id=1, source_target_pairs={{0,1},{1,2},{2,3},{3,0},{4,5},{5,6},{6,7},{7,4},{8,9},{9,10},{10,1... | collective-permute-start | bytes 776 | tf_op jit(solution)/shard_map/ppermute | solution.py:435
  58.9 0.0 collective-permute-done.7
  58.9 1.5 %collective-permute-done.6 = f32[1,64]{1,0:T(1,128)S(1)} collective-permute-done((f32[1,64]{1,0:T(1,128)S(1)}, f32[1,64]{1,0:T(1,128)S(1)}, u32[]{:S(2)}, u32[]{:S(2)}) %collective-permute-start.6) | collective-permute-done | bytes 288 | tf_op jit(solution)/shard_map/ppermute | solution.py:435
  60.4 1.4 %collective-permute-done.5 = f32[1,64]{1,0:T(1,128)S(1)} collective-permute-done((f32[1,64]{1,0:T(1,128)S(1)}, f32[1,64]{1,0:T(1,128)S(1)}, u32[]{:S(2)}, u32[]{:S(2)}) %collective-permute-start.5) | collective-permute-done | bytes 288 | tf_op jit(solution)/shard_map/ppermute | solution.py:435
  61.9 0.5 add_add_fusion
  (4 shorter events, 0.1 us)
Async XLA Ops:
  2.6 15.3 %copy-start = (f32[1,64,32,128]{3,2,1,0:T(8,128)S(1)}, f32[1,64,32,128]{3,2,1,0:T(8,128)}, u32[]{:S(2)}) copy-start(f32[1,64,32,128]{3,2,1,0:T(8,128)} %param.6) | copy-start | bytes 3145732
  2.7 10.8 %collective-permute-start = (f32[7,64,128]{2,1,0:T(8,128)S(1)}, f32[7,64,128]{2,1,0:T(8,128)S(1)}, u32[]{:S(2)}, u32[]{:S(2)}) collective-permute-start(f32[7,64,128]{2,1,0:T(8,128)S(1)} %bitcast.17), channel_id=1, source_target_pairs={{0,1},{1,2},{2,3},{4,5},{5,6},{6,7},{8,9},{9,10},{10,11},{12,13},{... | collective-permute-start | bytes 688136 | tf_op jit(solution)/shard_map/ppermute | solution.py:364
  6.2 9.6 %collective-permute-start.1 = (f32[4,64,128]{2,1,0:T(8,128)S(1)}, f32[4,64,128]{2,1,0:T(8,128)S(1)}, u32[]{:S(2)}, u32[]{:S(2)}) collective-permute-start(f32[4,64,128]{2,1,0:T(8,128)S(1)} %bitcast.18), channel_id=1, source_target_pairs={{1,0},{2,1},{3,2},{5,4},{6,5},{7,6},{9,8},{10,9},{11,10},{13,12},{... | collective-permute-start | bytes 393224 | tf_op jit(solution)/shard_map/ppermute | solution.py:365
  7.5 20.5 %collective-permute-start.3 = (f32[2048,128]{1,0:T(8,128)}, f32[2048,128]{1,0:T(8,128)S(1)}, u32[]{:S(2)}, u32[]{:S(2)}) collective-permute-start(f32[2048,128]{1,0:T(8,128)} %bitcast.14), channel_id=1, source_target_pairs={{4,8},{12,16},{20,24},{8,4},{16,12},{24,20},{5,9},{13,17},{21,25},... | collective-permute-start | bytes 3145736 | tf_op jit(solution)/shard_map/ppermute | solution.py:345
  15.8 12.2 %collective-permute-start.4 = (f32[11,64,128]{2,1,0:T(8,128)S(1)}, f32[11,64,128]{2,1,0:T(8,128)S(1)}, u32[]{:S(2)}, u32[]{:S(2)}) collective-permute-start(f32[11,64,128]{2,1,0:T(8,128)S(1)} %constant_dynamic-update-slice_fusion.halo), channel_id=1, source_target_pairs={{4,8},{12,16},{20,24},{8,4},{16,12},{24,20},{5,9},{13,17},{21,25},... | collective-permute-start | bytes 1081352 | tf_op jit(solution)/shard_map/ppermute | solution.py:345
  26.3 10.1 %collective-permute-start.2 = (f32[640,1024]{1,0:T(8,128)S(1)}, f32[640,1024]{1,0:T(8,128)S(1)}, u32[]{:S(2)}, u32[]{:S(2)}) collective-permute-start(f32[640,1024]{1,0:T(8,128)S(1)} %encode.2.own), channel_id=1, source_target_pairs={{0,4},{8,12},{16,20},{24,28},{4,0},{12,8},{20,16},{28,24},{1,5},{9... | collective-permute-start | bytes 7864328 | tf_op jit(solution)/shard_map/ppermute | solution.py:345
  53.7 5.2 %collective-permute-start.7 = (f32[1,64]{1,0:T(1,128)S(1)}, f32[1,64]{1,0:T(1,128)S(1)}, u32[]{:S(2)}, u32[]{:S(2)}) collective-permute-start(f32[1,64]{1,0:T(1,128)S(1)} %get-tuple-element.19), channel_id=1, source_target_pairs={{0,3},{1,0},{2,1},{3,2},{4,7},{5,4},{6,5},{7,6},{8,11},{9,8},{10,9... | collective-permute-start | bytes 776 | tf_op jit(solution)/shard_map/ppermute | solution.py:435
  56.9 3.5 %collective-permute-start.6 = (f32[1,64]{1,0:T(1,128)S(1)}, f32[1,64]{1,0:T(1,128)S(1)}, u32[]{:S(2)}, u32[]{:S(2)}) collective-permute-start(f32[1,64]{1,0:T(1,128)S(1)} %get-tuple-element.19), channel_id=1, source_target_pairs={{0,2},{1,3},{2,0},{3,1},{4,6},{5,7},{6,4},{7,5},{8,10},{9,11},{10,... | collective-permute-start | bytes 776 | tf_op jit(solution)/shard_map/ppermute | solution.py:435
  57.4 4.4 %collective-permute-start.5 = (f32[1,64]{1,0:T(1,128)S(1)}, f32[1,64]{1,0:T(1,128)S(1)}, u32[]{:S(2)}, u32[]{:S(2)}) collective-permute-start(f32[1,64]{1,0:T(1,128)S(1)} %get-tuple-element.19), channel_id=1, source_target_pairs={{0,1},{1,2},{2,3},{3,0},{4,5},{5,6},{6,7},{7,4},{8,9},{9,10},{10,1... | collective-permute-start | bytes 776 | tf_op jit(solution)/shard_map/ppermute | solution.py:435

commit v3 on v2

--- a/solution.py
+++ b/solution.py
@@ -66,17 +66,21 @@
     return iota(shape, len(shape) - 1) ^ (lax.axis_index("scan") % 2 * (LANES // 2))
 
 
-def weights_body(*refs):
-    sources, outputs, targets, sems = refs[:5], refs[5:10], refs[10:15], refs[15]
+def loaded(sources, targets, sems):
     copies = [pltpu.make_async_copy(a, b, sems.at[i]) for i, (a, b) in enumerate(zip(sources, targets))]
     for copy in copies:
         copy.start()
     for copy in copies:
         copy.wait()
-    e1, e2, rs, d1, d2 = targets
-    w1, w2, wm, wd1, wd2 = outputs
-    encoder_weights(e1, e2, w1, w2)
-    decoder_weights(rs, d1, d2, wm, wd1, wd2)
+    return targets
+
+
+def encoder_weights_body(e1, e2, w1, w2, t1, t2, sems):
+    encoder_weights(*loaded((e1, e2), (t1, t2), sems), w1, w2)
+
+
+def decoder_weights_body(rs, d1, d2, after, wm, wd1, wd2, t1, t2, t3, sems):
+    decoder_weights(*loaded((rs, d1, d2), (t1, t2, t3), sems), wm, wd1, wd2)
 
 
 def encoder_weights(e1, e2, w1, w2):
@@ -183,41 +187,51 @@
             put(wd2, r * depth, value, slice(p * LANES, (p + 1) * LANES))
 
 
-def encode_body(
-    x, halo, w1, w2, out, tap0, tap1, tap2, high_map, low_map, high_edge, low_edge, *, strip, cols, step
-):
-    rows = strip + ABOVE + BELOW
-    n_odd = strip // 4 + 2
-    n_even = n_odd + 1
-    odd_start = n_even * cols
-
-    def place(h):
-        start = (h // 2) * cols + (h % 2) * odd_start
-        return slice(start, start + cols)
-
-    for e in range(rows):
-        if e < ABOVE:
-            value = halo[e]
-        elif e < ABOVE + strip:
-            value = x[pl.ds(e - ABOVE, cols, stride=strip), :]
-        else:
-            value = halo[e - strip]
-        if e % 2:
-            tap1[place(e // 2), :] = pltpu.roll(value, TAPS, 1)
-        else:
-            if e // 2 < n_even + n_odd:
-                tap0[place(e // 2), :] = value
-            if e > 0:
-                tap2[place(e // 2 - 1), :] = pltpu.roll(value, 2 * TAPS, 1)
-    total = high_map.shape[0]
-    n = n_odd * cols
+def run_starts(runs, cols):
+    starts, at = [], 0
+    for first, count in runs:
+        starts.append((at, at + (count + 1) * cols))
+        at += (2 * count + 1) * cols
+    return starts, at
+
+
+def encode_rows(x, halo, w1, w2, out, scratch, runs, strip, cols, step):
+    tap0, tap1, tap2, high_map, low_map, high_edge, low_edge = scratch
+    starts, total = run_starts(runs, cols)
+    n = sum(count for _, count in runs) * cols
+    det = lax.axis_index("det")
+    not_first = (det > 0).astype(F32)
+    not_last = (det < lax.axis_size("det") - 1).astype(F32)
+    for (first, count), (even, odd) in zip(runs, starts):
+        for e in range(4 * first, 4 * (first + count) + 3):
+            if e < ABOVE:
+                value = halo[e] * not_first
+            elif e < ABOVE + strip:
+                value = x[pl.ds(e - ABOVE, cols, stride=strip), :]
+            else:
+                value = halo[e - strip] * not_last
+            rolled = pltpu.roll(value, (TAPS if e % 2 else 2 * TAPS), 1)
+            for tap, ref in enumerate((tap0, tap1, tap2)):
+                if (e - tap) % 2:
+                    continue
+                h = (e - tap) // 2 - 2 * first
+                if 0 <= h <= 2 * count:
+                    start = (odd if h % 2 else even) + (h // 2) * cols
+                    ref[start : start + cols, :] = rolled if tap else value
     for ref in (high_edge, low_edge):
         ref[:, :LANES] = jnp.zeros((n, LANES), BF16)
     lane = iota((total, LANES), 1)
     edge_lane = iota((n, LANES), 1)
     groups = high_map.shape[1] // 256
 
-    def first(g, carry):
+    def taps_of(source):
+        taps = ([], [], [])
+        for (_, count), (even, odd) in zip(runs, starts):
+            for tap, start in zip(taps, (even, odd, even + cols)):
+                tap.append(source(start, start + count * cols))
+        return [tap[0] if len(tap) == 1 else jnp.concatenate(tap, axis=0) for tap in taps]
+
+    def first_layer(g, carry):
         lanes = pl.ds(pl.multiple_of(g * 256, 256), 256)
         at = (lane - 32 * g + 1) & (LANES - 1)
         packed = jnp.where(at < TAPS, tap0[...], jnp.where(at < 2 * TAPS, tap1[...], tap2[...]))
@@ -227,29 +241,56 @@
         high, low = split(value)
         high_map[:, lanes] = high
         low_map[:, lanes] = low
-        last = value[:, LANES:]
-        one = pltpu.roll(last[odd_start:], step, 1)
-        two = pltpu.roll(last[cols:odd_start], 2 * step, 1)
-        edge = jnp.where(edge_lane < step, one, jnp.where(edge_lane < 2 * step, two, last[:n]))
+        zero, one, two = taps_of(lambda start, stop: value[start:stop, LANES:])
+        one = pltpu.roll(one, step, 1)
+        two = pltpu.roll(two, 2 * step, 1)
+        edge = jnp.where(edge_lane < step, one, jnp.where(edge_lane < 2 * step, two, zero))
         high, low = split(edge)
         target = pl.ds(pl.multiple_of((g + 1) * LANES, LANES), LANES)
         high_edge[:, target] = high
         low_edge[:, target] = low
         return carry
 
-    lax.fori_loop(0, groups, first, 0)
-
-    def second(g, carry):
+    lax.fori_loop(0, groups, first_layer, 0)
+
+    def second_layer(g, carry):
         source = pl.ds(pl.multiple_of(g * 256, 256), 256)
         beside = pl.ds(pl.multiple_of(g * LANES, LANES), LANES)
-        starts = (0, odd_start, cols)
-        high = [high_map[start : start + n, source] for start in starts] + [high_edge[:, beside]]
-        low = [low_map[start : start + n, source] for start in starts] + [low_edge[:, beside]]
+        high = taps_of(lambda start, stop: high_map[start:stop, source]) + [high_edge[:, beside]]
+        low = taps_of(lambda start, stop: low_map[start:stop, source]) + [low_edge[:, beside]]
         left = jnp.concatenate(high + low + high, axis=1)
-        out[:, source] = silu(jnp.dot(left, thrice(w2), preferred_element_type=F32))
+        value = silu(jnp.dot(left, thrice(w2), preferred_element_type=F32))
+        done = 0
+        for first, count in runs:
+            row = first * cols if out.shape[0] > n else done
+            out[row : row + count * cols, source] = value[done : done + count * cols]
+            done += count * cols
         return carry
 
-    lax.fori_loop(0, groups, second, 0)
+    lax.fori_loop(0, groups, second_layer, 0)
+
+
+def inner_body(x, w1, w2, out, *scratch, **sizes):
+    encode_rows(x, None, w1, w2, out, scratch, **sizes)
+
+
+def border_body(x, halo, w1, w2, inner, out, *scratch, runs, cols, **sizes):
+    start = runs[0][1] * cols
+    out[start : start + inner.shape[0], :] = inner[...]
+    encode_rows(x, halo, w1, w2, out, scratch, runs=runs, cols=cols, **sizes)
+
+
+def other_body(x, halo, w1, w2, after, out, *scratch, **sizes):
+    scan = lax.axis_index("scan")
+    inside = (scan > 0) & (scan < lax.axis_size("scan") - 1)
+
+    @pl.when(inside)
+    def _():
+        encode_rows(x, halo, w1, w2, out, scratch, **sizes)
+
+    @pl.when(jnp.logical_not(inside))
+    def _():
+        out[...] = jnp.zeros(out.shape, F32)
 
 
 def decode_body(own, sibling, other, x, wm, wd1, wd2, rebuilt, part, mixed, dh, dl, *, strip, cols):
@@ -341,79 +382,86 @@
     part[...] = jnp.sum(total.T, axis=0, keepdims=True) * (1.0 / (LANES * LANES))
 
 
-def swapped(value, axis, pairs):
-    return lax.ppermute(value, axis, [(i, j) for i, j in pairs] + [(j, i) for i, j in pairs])
+def far_route(n_scan, n_det):
+    route = []
+    for i in range(n_scan):
+        for j in range(n_det):
+            rim = i == 0 or i == n_scan - 1
+            to = (i, (j + n_det // 2) % n_det) if rim else (i + 1 if i % 2 else i - 1, j)
+            route.append((i * n_det + j, to[0] * n_det + to[1]))
+    return route
 
 
 def on_device(patterns, encoder_one, encoder_two, real_space, decoder_one, decoder_two):
     _, cols, strip, width = patterns.shape
     f1 = encoder_one.shape[3]
     f2 = encoder_two.shape[3]
-    n_scan = lax.axis_size("scan")
     n_det = lax.axis_size("det")
     latent_rows = strip // 4 + 2
     latent_lanes = (width // 4) * f2
     hidden_lanes = (width // 2) * f1
     x = patterns.reshape(cols * strip, width)
 
-    down = [(i, i + 1) for i in range(n_det - 1)]
-    up = [(i + 1, i) for i in range(n_det - 1)]
+    down = [(i, (i + 1) % n_det) for i in range(n_det)]
+    up = [(j, i) for i, j in down]
     last, first = lax.optimization_barrier(
         (patterns[0, :, strip - ABOVE :].transpose(1, 0, 2), patterns[0, :, :BELOW].transpose(1, 0, 2))
     )
     above = lax.ppermute(last, "det", down)
     below = lax.ppermute(first, "det", up)
-    chips = [(i, i + 1) for i in range(1, n_scan - 1, 2)]
-    cores = [(i, i + 1) for i in range(0, n_scan, 2)]
-    far_x = swapped(x, "scan", chips)
+    far = far_route(lax.axis_size("scan"), n_det)
+    far_x = lax.ppermute(x, ("scan", "det"), far)
     halo = jnp.concatenate([above, below], axis=0)
-    far_halo = swapped(halo, "scan", chips)
+    far_halo = lax.ppermute(halo, ("scan", "det"), far)
 
     def cost(flops, moved):
         return pl.CostEstimate(flops=flops, transcendentals=0, bytes_accessed=moved)
 
-    weights = (
-        encoder_one,
-        encoder_two,
-        real_space,
-        decoder_one.transpose(0, 1, 3, 2),
-        decoder_two.transpose(0, 1, 3, 2),
+    def build(body, shapes, weights, *after):
+        return pl.pallas_call(
+            body,
+            in_specs=[pl.BlockSpec(memory_space=pltpu.HBM)] * len(weights)
+            + [pl.BlockSpec(memory_space=pl.ANY)] * len(after),
+            out_shape=[jax.ShapeDtypeStruct(shape, BF16) for shape in shapes],
+            scratch_shapes=[pltpu.VMEM(w.shape, F32) for w in weights]
+            + [pltpu.SemaphoreType.DMA((len(weights),))],
+            compiler_params=pltpu.CompilerParams(vmem_limit_bytes=12 << 20),
+            cost_estimate=cost(10**9, 4 << 20),
+            name=body.__name__,
+        )(*[pltpu.with_memory_space_constraint(w, pltpu.HBM) for w in weights], *after)
+
+    w1, w2 = build(
+        encoder_weights_body, [(2 * LANES, hidden_lanes), (14 * LANES, 256)], (encoder_one, encoder_two)
     )
-    w1, w2, wm, wd1, wd2 = pl.pallas_call(
-        weights_body,
-        in_specs=[pl.BlockSpec(memory_space=pltpu.HBM)] * len(weights),
-        out_shape=[
-            jax.ShapeDtypeStruct((2 * LANES, hidden_lanes), BF16),
-            jax.ShapeDtypeStruct((14 * LANES, 256), BF16),
-            jax.ShapeDtypeStruct((4 * LANES, 4 * LANES), BF16),
-            jax.ShapeDtypeStruct((6 * LANES, 2 * LANES), BF16),
-            jax.ShapeDtypeStruct((4 * hidden_lanes, 2 * LANES), BF16),
-        ],
-        scratch_shapes=[pltpu.VMEM(w.shape, F32) for w in weights]
-        + [pltpu.SemaphoreType.DMA((len(weights),))],
-        compiler_params=pltpu.CompilerParams(vmem_limit_bytes=16 << 20),
-        cost_estimate=cost(10**9, 4 << 20),
-        name="weights",
-    )(*[pltpu.with_memory_space_constraint(w, pltpu.HBM) for w in weights])
 
     n_latent = latent_rows * cols
-    n_hidden = (2 * latent_rows + 1) * cols
-
-    def encode(strip_x, strip_halo):
+
+    def encode(body, runs, rows, *operands, wait_for=None):
+        n_hidden = run_starts(runs, cols)[1]
+        n_run = sum(count for _, count in runs) * cols
         return pl.pallas_call(
-            functools.partial(encode_body, strip=strip, cols=cols, step=f1),
-            out_shape=jax.ShapeDtypeStruct((n_latent, latent_lanes), F32),
+            functools.partial(body, runs=runs, strip=strip, cols=cols, step=f1),
+            out_shape=jax.ShapeDtypeStruct((rows * cols, latent_lanes), F32),
+            in_specs=[pl.BlockSpec(memory_space=pl.ANY if ref is wait_for else None) for ref in operands],
             scratch_shapes=[pltpu.VMEM((n_hidden, LANES), F32)] * 3
             + [pltpu.VMEM((n_hidden, hidden_lanes), BF16)] * 2
-            + [pltpu.VMEM((n_latent, hidden_lanes // 2 + LANES), BF16)] * 2,
+            + [pltpu.VMEM((n_run, hidden_lanes // 2 + LANES), BF16)] * 2,
             compiler_params=pltpu.CompilerParams(vmem_limit_bytes=ENCODE_VMEM),
-            cost_estimate=cost(2 * n_latent * 27 * LANES * latent_lanes * 8, 8 << 20),
-            name="encode",
-        )(strip_x, strip_halo, w1, w2)
-
-    own = encode(x, halo)
-    sibling = swapped(own, "scan", cores)
-    other = encode(far_x, far_halo)
+            cost_estimate=cost(2 * n_run * 27 * LANES * latent_lanes * 8, 8 << 20),
+            name=body.__name__,
+        )(*operands)
+
+    n_inner = latent_rows - 3
+    inner = encode(inner_body, [(2, n_inner)], n_inner, x, w1, w2)
+    own = encode(border_body, [(0, 2), (latent_rows - 1, 1)], latent_rows, x, halo, w1, w2, inner)
+    sibling = lax.ppermute(own, "scan", [(i, i ^ 1) for i in range(lax.axis_size("scan"))])
+    wm, wd1, wd2 = build(
+        decoder_weights_body,
+        [(4 * LANES, 4 * LANES), (6 * LANES, 2 * LANES), (4 * hidden_lanes, 2 * LANES)],
+        (real_space, decoder_one.transpose(0, 1, 3, 2), decoder_two.transpose(0, 1, 3, 2)),
+        own,
+    )
+    other = encode(other_body, [(0, latent_rows)], latent_rows, far_x, far_halo, w1, w2, wm, wait_for=wm)
     rebuilt, part = pl.pallas_call(
         functools.partial(decode_body, strip=strip, cols=cols),
         out_shape=[
@@ -429,10 +477,11 @@
         cost_estimate=cost(2 * n_latent * 45 * LANES * latent_lanes, 16 << 20),
         name="decode",
     )(own, sibling, other, x, wm, wd1, wd2)
-    if n_det == 4:
-        misfit = part
-        for turn in range(1, n_det):
-            misfit = misfit + lax.ppermute(part, "det", [(i, (i + turn) % n_det) for i in range(n_det)])
+    if n_det & (n_det - 1) == 0:
+        misfit, bit = part, 1
+        while bit < n_det:
+            misfit = misfit + lax.ppermute(misfit, "det", [(i, i ^ bit) for i in range(n_det)])
+            bit *= 2
     else:
         misfit = lax.psum(part, "det")
     return rebuilt.reshape(patterns.shape), misfit

time: 63.3 us -> 57.7 us (0.912); the launches traced: 62.4 us -> 57.5 us
  starting transfers between devices: 15.9 us -> 6.99 us
  Pallas kernels: 38 us -> 41.3 us
    ppermute x6 -> x5, starting transfers between devices: 11 us -> 4.01 us  [the longest x2 2.13 us: on_device(): lax.ppermute(misfit, 'det', [(i, i ^ bit) for i in range(n_det)])]
    pallas_call x3 -> x5, Pallas kernels: 20.8 us -> 24 us  [the longest x3 18.9 us: encode(): pl.pallas_call(functools.partial(body, runs=runs, strip=strip, cols=cols,...]
    ppermute x6 -> x5, waiting for transfers between devices: 2.96 us -> 5.81 us  [the longest x2 4.95 us: on_device(): lax.ppermute(misfit, 'det', [(i, i ^ bit) for i in range(n_det)])]
    ppermute x1, waiting for transfers between devices: 2.26 us -> 0.01 us  [on_device(): below = lax.ppermute(first, 'det', up)]
    ppermute x1, starting transfers between devices: 3.54 us -> 1.54 us  [on_device(): above = lax.ppermute(last, 'det', down)]
  transfers between devices with their start and end apart: 8 -> 7, of which waited for: 3 -> 3; matrix products, arithmetic and copies ran while one was open for 0% -> 0% of each run, Pallas kernels for 33% -> 42%
where the time goes in v3:
time: 57.7 us; the launch traced here: 57.5 us
  Pallas kernels  41.3 us (72%)
  starting transfers between devices  6.99 us (12%)
  waiting for transfers between devices  5.81 us (10%)
  local copies, waits for them, and re-layouts  2.12 us (4%)
  between operations  0.76 us (1%)
    pallas_call x3, Pallas kernels, encode(): pl.pallas_call(functools.partial(body, runs=runs, strip=strip, cols=cols,...  18.9 us
    pallas_call x1, Pallas kernels, on_device(): pl.pallas_call(functools.partial(decode_body, strip=strip, cols=cols), ou...  17.3 us
    pallas_call x2, Pallas kernels, build(): pl.pallas_call(body, in_specs=[pl.BlockSpec(memory_space=pltpu.HBM)] * le...  5.14 us
    ppermute x2, waiting for transfers between devices, on_device(): lax.ppermute(misfit, 'det', [(i, i ^ bit) for i in range(n_det)])  4.95 us
    ppermute x2, starting transfers between devices, on_device(): lax.ppermute(misfit, 'det', [(i, i ^ bit) for i in range(n_det)])  2.13 us
    ppermute x1, starting transfers between devices, on_device(): far_halo = lax.ppermute(halo, ('scan', 'det'), far)  1.81 us
    ppermute x1, starting transfers between devices, on_device(): above = lax.ppermute(last, 'det', down)  1.54 us
    ppermute x1, starting transfers between devices, on_device(): below = lax.ppermute(first, 'det', up)  1.43 us
  transfers between devices with their start and end apart: 7, of which 3 were waited for; matrix products, arithmetic and copies ran while one was open for 0% of the time, Pallas kernels for 42%

profile of v3, /device:TPU:8, one launch (start us, length us, event | category | flops | bytes accessed | tf_op | source)
XLA Modules:
  0.0 57.5 jit_solution(14499278891710739842)
XLA Ops:
  0.6 0.0 copy-start
  0.6 1.1 %slice.6 = f32[1,64,7,128]{3,2,1,0:T(8,128)S(1)} slice(f32[1,64,32,128]{3,2,1,0:T(8,128)} %param.6), slice={[0:1], [0:64], [25:32], [0:128]} | slice | bytes 458752 | tf_op jit(solution)/shard_map/slice | solution.py:408
  1.7 1.0 %slice.7 = f32[1,64,4,128]{3,2,1,0:T(4,128)S(1)} slice(f32[1,64,32,128]{3,2,1,0:T(8,128)} %param.6), slice={[0:1], [0:64], [0:4], [0:128]} | slice | bytes 262144 | tf_op jit(solution)/shard_map/slice | solution.py:408
  2.8 1.5 %collective-permute-start = (f32[7,64,128]{2,1,0:T(8,128)S(1)}, f32[7,64,128]{2,1,0:T(8,128)S(1)}, u32[]{:S(2)}, u32[]{:S(2)}) collective-permute-start(f32[7,64,128]{2,1,0:T(8,128)S(1)} %bitcast.18), channel_id=1, source_target_pairs={{0,1},{1,2},{2,3},{3,0},{4,5},{5,6},{6,7},{7,4},{8,9},{9,10},{10,1... | collective-permute-start | bytes 688136 | tf_op jit(solution)/shard_map/ppermute | solution.py:410
  4.3 1.4 %collective-permute-start.1 = (f32[4,64,128]{2,1,0:T(8,128)S(1)}, f32[4,64,128]{2,1,0:T(8,128)S(1)}, u32[]{:S(2)}, u32[]{:S(2)}) collective-permute-start(f32[4,64,128]{2,1,0:T(8,128)S(1)} %bitcast.19), channel_id=1, source_target_pairs={{1,0},{2,1},{3,2},{0,3},{5,4},{6,5},{7,6},{4,7},{9,8},{10,9},{11,1... | collective-permute-start | bytes 393224 | tf_op jit(solution)/shard_map/ppermute | solution.py:411
  5.7 0.0 collective-permute-start.3
  5.7 2.2 %encoder_weights_body.1 = (bf16[256,1024]{1,0:T(8,128)(2,1)S(1)}, bf16[1792,256]{1,0:T(8,128)(2,1)S(1)}) custom-call(f32[3,3,1,16]{3,2,1,0:T(1,128)} %e1.1, f32[3,3,16,32]{3,2,1,0:T(8,128)} %e2.1), custom_call_target="tpu_custom_call" | custom-call | flops 1000000000 | bytes 4194304 | tf_op jit(solution)/shard_map/encoder_weights_body/pallas_call | solution.py:421
  7.9 0.0 copy-done
  7.9 6.4 %inner_body.1.inner = f32[448,1024]{1,0:T(8,128)S(1)} custom-call(f32[2048,128]{1,0:T(8,128)S(1)} %bitcast.15, bf16[256,1024]{1,0:T(8,128)(2,1)S(1)} %get-tuple-element.13.w1, bf16[1792,256]{1,0:T(8,128)(2,1)S(1)} %get-tuple-element.14.w2), custom_call_target="tpu_custom_call" | custom-call | flops 25367150592 | bytes 8388608 | tf_op jit(solution)/shard_map/inner_body/pallas_call | solution.py:442
  14.4 0.0 collective-permute-done
  14.4 0.0 collective-permute-done.1
  14.4 1.8 %collective-permute-start.4 = (f32[11,64,128]{2,1,0:T(8,128)S(1)}, f32[11,64,128]{2,1,0:T(8,128)S(1)}, u32[]{:S(2)}, u32[]{:S(2)}) collective-permute-start(f32[11,64,128]{2,1,0:T(8,128)S(1)} %constant_dynamic-update-slice_fusion.halo), channel_id=1, source_target_pairs={{0,2},{1,3},{2,0},{3,1},{4,8},{5,9},{6,10},{7,11},{8,4},{9,5},{10,... | collective-permute-start | bytes 1081352 | tf_op jit(solution)/shard_map/ppermute | solution.py:415
  16.2 3.9 %border_body.1.after.own = f32[640,1024]{1,0:T(8,128)S(1)} custom-call(f32[2048,128]{1,0:T(8,128)S(1)} %bitcast.16, f32[11,64,128]{2,1,0:T(8,128)S(1)} %constant_dynamic-update-slice_fusion.halo, bf16[256,1024]{1,0:T(8,128)(2,1)S(1)} %get-tuple-element.13.w1, bf16[1792,256]{1,0:T(8,128)(2,1)S(1)} %get-tuple-element.14.w2, f32[448,1024]{1,0:T(8,128)S(1)} %inner_body.1.inner), custom_call_target="tpu_custom_call" | custom-call | flops 10871635968 | bytes 8388608 | tf_op jit(solution)/shard_map/border_body/pallas_call | solution.py:442
  20.1 0.1 collective-permute-start.2
  20.2 3.0 %decoder_weights_body.1 = (bf16[512,512]{1,0:T(8,128)(2,1)S(1)}, bf16[768,256]{1,0:T(8,128)(2,1)S(1)}, bf16[4096,256]{1,0:T(8,128)(2,1)S(1)}) custom-call(f32[3,3,32,32]{3,2,1,0:T(8,128)} %rs.1, f32[3,3,16,32]{3,2,1,0:T(8,128)} %bitcast.20, f32[3,3,1,16]{3,2,1,0:T(1,128)} %bitcast.21, f32[640,1024]{1,0:T(8,128)S(1)} %border_body.1.after.own), custom_call_target="tpu_custom_call" | custom-call | flops 1000000000 | bytes 4194304 | tf_op jit(solution)/shard_map/decoder_weights_body/pallas_call | solution.py:421
  23.2 0.9 %collective-permute-done.4.halo = f32[11,64,128]{2,1,0:T(8,128)S(1)} collective-permute-done((f32[11,64,128]{2,1,0:T(8,128)S(1)}, f32[11,64,128]{2,1,0:T(8,128)S(1)}, u32[]{:S(2)}, u32[]{:S(2)}) %collective-permute-start.4) | collective-permute-done | bytes 360480 | tf_op jit(solution)/shard_map/ppermute | solution.py:415
  24.0 0.0 collective-permute-done.3.x
  24.0 8.6 %other_body.1.other = f32[640,1024]{1,0:T(8,128)S(1)} custom-call(f32[2048,128]{1,0:T(8,128)S(1)} %collective-permute-done.3.x, f32[11,64,128]{2,1,0:T(8,128)S(1)} %collective-permute-done.4.halo, bf16[256,1024]{1,0:T(8,128)(2,1)S(1)} %get-tuple-element.13.w1, bf16[1792,256]{1,0:T(8,128)(2,1)S(1)} %get-tuple-element.14.w2, ...), custom_call_target="tpu_custom_call" | custom-call | flops 36238786560 | bytes 8388608 | tf_op jit(solution)/shard_map/other_body/pallas_call | solution.py:442
  32.6 0.0 collective-permute-done.2.sibling
  32.6 17.3 %decode.1 = (f32[2048,128]{1,0:T(8,128)}, f32[1,64]{1,0:T(1,128)S(1)}) custom-call(f32[640,1024]{1,0:T(8,128)S(1)} %border_body.1.after.own, f32[640,1024]{1,0:T(8,128)S(1)} %collective-permute-done.2.sibling, f32[640,1024]{1,0:T(8,128)S(1)} %other_body.1.other, f32[2048,128]{1,0:T(8,128)S(1)} %bitcast.17, bf16[512,512]{1,0:T(8,128)(2,1)S(1)} %get-tuple-element.15.after.wm, ...), custom_call_target="tpu_custom_call" | custom-call | flops 7549747200 | bytes 16777216 | tf_op jit(solution)/shard_map/decode/pallas_call | solution.py:465
  49.9 0.6 %collective-permute-start.5 = (f32[1,64]{1,0:T(1,128)S(1)}, f32[1,64]{1,0:T(1,128)S(1)}, u32[]{:S(2)}, u32[]{:S(2)}) collective-permute-start(f32[1,64]{1,0:T(1,128)S(1)} %get-tuple-element.19), channel_id=1, source_target_pairs={{0,1},{1,0},{2,3},{3,2},{4,5},{5,4},{6,7},{7,6},{8,9},{9,8},{10,11... | collective-permute-start | bytes 776 | tf_op jit(solution)/shard_map/ppermute | solution.py:483
  50.5 2.9 %collective-permute-done.5 = f32[1,64]{1,0:T(1,128)S(1)} collective-permute-done((f32[1,64]{1,0:T(1,128)S(1)}, f32[1,64]{1,0:T(1,128)S(1)}, u32[]{:S(2)}, u32[]{:S(2)}) %collective-permute-start.5) | collective-permute-done | bytes 288 | tf_op jit(solution)/shard_map/ppermute | solution.py:483
  53.4 1.5 %collective-permute-start.6 = (f32[1,64]{1,0:T(1,128)S(1)}, f32[1,64]{1,0:T(1,128)S(1)}, u32[]{:S(2)}, u32[]{:S(2)}) collective-permute-start(f32[1,64]{1,0:T(1,128)S(1)} %add.6), channel_id=1, source_target_pairs={{0,2},{1,3},{2,0},{3,1},{4,6},{5,7},{6,4},{7,5},{8,10},{9,11},{10,... | collective-permute-start | bytes 776 | tf_op jit(solution)/shard_map/ppermute | solution.py:483
  54.9 2.0 %collective-permute-done.6 = f32[1,64]{1,0:T(1,128)S(1)} collective-permute-done((f32[1,64]{1,0:T(1,128)S(1)}, f32[1,64]{1,0:T(1,128)S(1)}, u32[]{:S(2)}, u32[]{:S(2)}) %collective-permute-start.6) | collective-permute-done | bytes 288 | tf_op jit(solution)/shard_map/ppermute | solution.py:483
  56.9 0.5 add.7
  (5 shorter events, 0.1 us)
Async XLA Ops:
  0.6 7.3 %copy-start = (f32[1,64,32,128]{3,2,1,0:T(8,128)S(1)}, f32[1,64,32,128]{3,2,1,0:T(8,128)}, u32[]{:S(2)}) copy-start(f32[1,64,32,128]{3,2,1,0:T(8,128)} %param.6) | copy-start | bytes 3145732
  2.8 11.6 %collective-permute-start = (f32[7,64,128]{2,1,0:T(8,128)S(1)}, f32[7,64,128]{2,1,0:T(8,128)S(1)}, u32[]{:S(2)}, u32[]{:S(2)}) collective-permute-start(f32[7,64,128]{2,1,0:T(8,128)S(1)} %bitcast.18), channel_id=1, source_target_pairs={{0,1},{1,2},{2,3},{3,0},{4,5},{5,6},{6,7},{7,4},{8,9},{9,10},{10,1... | collective-permute-start | bytes 688136 | tf_op jit(solution)/shard_map/ppermute | solution.py:410
  4.3 10.1 %collective-permute-start.1 = (f32[4,64,128]{2,1,0:T(8,128)S(1)}, f32[4,64,128]{2,1,0:T(8,128)S(1)}, u32[]{:S(2)}, u32[]{:S(2)}) collective-permute-start(f32[4,64,128]{2,1,0:T(8,128)S(1)} %bitcast.19), channel_id=1, source_target_pairs={{1,0},{2,1},{3,2},{0,3},{5,4},{6,5},{7,6},{4,7},{9,8},{10,9},{11,1... | collective-permute-start | bytes 393224 | tf_op jit(solution)/shard_map/ppermute | solution.py:411
  5.7 18.3 %collective-permute-start.3 = (f32[2048,128]{1,0:T(8,128)}, f32[2048,128]{1,0:T(8,128)S(1)}, u32[]{:S(2)}, u32[]{:S(2)}) collective-permute-start(f32[2048,128]{1,0:T(8,128)} %bitcast.14), channel_id=1, source_target_pairs={{0,2},{1,3},{2,0},{3,1},{4,8},{5,9},{6,10},{7,11},{8,4},{9,5},{10,... | collective-permute-start | bytes 3145736 | tf_op jit(solution)/shard_map/ppermute | solution.py:413
  14.4 9.6 %collective-permute-start.4 = (f32[11,64,128]{2,1,0:T(8,128)S(1)}, f32[11,64,128]{2,1,0:T(8,128)S(1)}, u32[]{:S(2)}, u32[]{:S(2)}) collective-permute-start(f32[11,64,128]{2,1,0:T(8,128)S(1)} %constant_dynamic-update-slice_fusion.halo), channel_id=1, source_target_pairs={{0,2},{1,3},{2,0},{3,1},{4,8},{5,9},{6,10},{7,11},{8,4},{9,5},{10,... | collective-permute-start | bytes 1081352 | tf_op jit(solution)/shard_map/ppermute | solution.py:415
  20.1 12.5 %collective-permute-start.2 = (f32[640,1024]{1,0:T(8,128)S(1)}, f32[640,1024]{1,0:T(8,128)S(1)}, u32[]{:S(2)}, u32[]{:S(2)}) collective-permute-start(f32[640,1024]{1,0:T(8,128)S(1)} %border_body.1.after.own), channel_id=1, source_target_pairs={{0,4},{4,0},{8,12},{12,8},{16,20},{20,16},{24,28},{28,24},{1,5},{5... | collective-permute-start | bytes 7864328 | tf_op jit(solution)/shard_map/ppermute | solution.py:457
  49.9 3.5 %collective-permute-start.5 = (f32[1,64]{1,0:T(1,128)S(1)}, f32[1,64]{1,0:T(1,128)S(1)}, u32[]{:S(2)}, u32[]{:S(2)}) collective-permute-start(f32[1,64]{1,0:T(1,128)S(1)} %get-tuple-element.19), channel_id=1, source_target_pairs={{0,1},{1,0},{2,3},{3,2},{4,5},{5,4},{6,7},{7,6},{8,9},{9,8},{10,11... | collective-permute-start | bytes 776 | tf_op jit(solution)/shard_map/ppermute | solution.py:483
  53.4 3.5 %collective-permute-start.6 = (f32[1,64]{1,0:T(1,128)S(1)}, f32[1,64]{1,0:T(1,128)S(1)}, u32[]{:S(2)}, u32[]{:S(2)}) collective-permute-start(f32[1,64]{1,0:T(1,128)S(1)} %add.6), channel_id=1, source_target_pairs={{0,2},{1,3},{2,0},{3,1},{4,6},{5,7},{6,4},{7,5},{8,10},{9,11},{10,... | collective-permute-start | bytes 776 | tf_op jit(solution)/shard_map/ppermute | solution.py:483

commit v4 on v3

--- a/solution.py
+++ b/solution.py
@@ -66,21 +66,17 @@
     return iota(shape, len(shape) - 1) ^ (lax.axis_index("scan") % 2 * (LANES // 2))
 
 
-def loaded(sources, targets, sems):
-    copies = [pltpu.make_async_copy(a, b, sems.at[i]) for i, (a, b) in enumerate(zip(sources, targets))]
+def encoder_weights_body(e1, e2, w1, w2, t1, t2, sems):
+    copies = [pltpu.make_async_copy(a, b, sems.at[i]) for i, (a, b) in enumerate(((e1, t1), (e2, t2)))]
     for copy in copies:
         copy.start()
     for copy in copies:
         copy.wait()
-    return targets
-
-
-def encoder_weights_body(e1, e2, w1, w2, t1, t2, sems):
-    encoder_weights(*loaded((e1, e2), (t1, t2), sems), w1, w2)
-
-
-def decoder_weights_body(rs, d1, d2, after, wm, wd1, wd2, t1, t2, t3, sems):
-    decoder_weights(*loaded((rs, d1, d2), (t1, t2, t3), sems), wm, wd1, wd2)
+    encoder_weights(t1, t2, w1, w2)
+
+
+def decoder_weights_body(rs, d1, d2, after, wm, wd1, wd2):
+    decoder_weights(rs, d1, d2, wm, wd1, wd2)
 
 
 def encoder_weights(e1, e2, w1, w2):
@@ -251,7 +247,7 @@
         low_edge[:, target] = low
         return carry
 
-    lax.fori_loop(0, groups, first_layer, 0)
+    lax.fori_loop(0, groups, first_layer, 0, unroll=True)
 
     def second_layer(g, carry):
         source = pl.ds(pl.multiple_of(g * 256, 256), 256)
@@ -267,7 +263,7 @@
             done += count * cols
         return carry
 
-    lax.fori_loop(0, groups, second_layer, 0)
+    lax.fori_loop(0, groups, second_layer, 0, unroll=True)
 
 
 def inner_body(x, w1, w2, out, *scratch, **sizes):
@@ -280,17 +276,22 @@
     encode_rows(x, halo, w1, w2, out, scratch, runs=runs, cols=cols, **sizes)
 
 
-def other_body(x, halo, w1, w2, after, out, *scratch, **sizes):
+def inside_scan(run, out):
     scan = lax.axis_index("scan")
     inside = (scan > 0) & (scan < lax.axis_size("scan") - 1)
-
-    @pl.when(inside)
-    def _():
-        encode_rows(x, halo, w1, w2, out, scratch, **sizes)
+    pl.when(inside)(run)
 
     @pl.when(jnp.logical_not(inside))
     def _():
         out[...] = jnp.zeros(out.shape, F32)
+
+
+def far_inner_body(x, w1, w2, after, out, *scratch, **sizes):
+    inside_scan(lambda: inner_body(x, w1, w2, out, *scratch, **sizes), out)
+
+
+def far_border_body(x, halo, w1, w2, inner, out, *scratch, **sizes):
+    inside_scan(lambda: border_body(x, halo, w1, w2, inner, out, *scratch, **sizes), out)
 
 
 def decode_body(own, sibling, other, x, wm, wd1, wd2, rebuilt, part, mixed, dh, dl, *, strip, cols):
@@ -326,7 +327,7 @@
         mixed[n - cols :, target] = value[n - cols :] * not_last
         return carry
 
-    lax.fori_loop(0, blocks, mix, 0)
+    lax.fori_loop(0, blocks, mix, 0, unroll=True)
     count = n - cols
     lane = own_lane((count, LANES))
     middle = (lane >= 32) & (lane < 96)
@@ -358,10 +359,10 @@
                 dl[start : start + cols, target] = low
         return carry
 
-    lax.fori_loop(0, blocks, first, 0)
+    lax.fori_loop(0, blocks, first, 0, unroll=True)
     total = jnp.zeros((cols, LANES), F32)
     pairs = strip // 2 + 1
-    step = 6
+    step = 9
     for begin in range(0, pairs, step):
         size = min(step, pairs - begin)
         top = slice(begin * cols, (begin + size) * cols)
@@ -417,22 +418,19 @@
     def cost(flops, moved):
         return pl.CostEstimate(flops=flops, transcendentals=0, bytes_accessed=moved)
 
-    def build(body, shapes, weights, *after):
-        return pl.pallas_call(
-            body,
-            in_specs=[pl.BlockSpec(memory_space=pltpu.HBM)] * len(weights)
-            + [pl.BlockSpec(memory_space=pl.ANY)] * len(after),
-            out_shape=[jax.ShapeDtypeStruct(shape, BF16) for shape in shapes],
-            scratch_shapes=[pltpu.VMEM(w.shape, F32) for w in weights]
-            + [pltpu.SemaphoreType.DMA((len(weights),))],
-            compiler_params=pltpu.CompilerParams(vmem_limit_bytes=12 << 20),
-            cost_estimate=cost(10**9, 4 << 20),
-            name=body.__name__,
-        )(*[pltpu.with_memory_space_constraint(w, pltpu.HBM) for w in weights], *after)
-
-    w1, w2 = build(
-        encoder_weights_body, [(2 * LANES, hidden_lanes), (14 * LANES, 256)], (encoder_one, encoder_two)
-    )
+    weights = (encoder_one, encoder_two)
+    w1, w2 = pl.pallas_call(
+        encoder_weights_body,
+        in_specs=[pl.BlockSpec(memory_space=pltpu.HBM)] * 2,
+        out_shape=[
+            jax.ShapeDtypeStruct((2 * LANES, hidden_lanes), BF16),
+            jax.ShapeDtypeStruct((14 * LANES, 256), BF16),
+        ],
+        scratch_shapes=[pltpu.VMEM(w.shape, F32) for w in weights] + [pltpu.SemaphoreType.DMA((2,))],
+        compiler_params=pltpu.CompilerParams(vmem_limit_bytes=12 << 20),
+        cost_estimate=cost(10**9, 4 << 20),
+        name="encoder_weights",
+    )(*[pltpu.with_memory_space_constraint(w, pltpu.HBM) for w in weights])
 
     n_latent = latent_rows * cols
 
@@ -452,16 +450,24 @@
         )(*operands)
 
     n_inner = latent_rows - 3
-    inner = encode(inner_body, [(2, n_inner)], n_inner, x, w1, w2)
-    own = encode(border_body, [(0, 2), (latent_rows - 1, 1)], latent_rows, x, halo, w1, w2, inner)
+    inner_runs, border_runs = [(2, n_inner)], [(0, 2), (latent_rows - 1, 1)]
+    inner = encode(inner_body, inner_runs, n_inner, x, w1, w2)
+    own = encode(border_body, border_runs, latent_rows, x, halo, w1, w2, inner)
     sibling = lax.ppermute(own, "scan", [(i, i ^ 1) for i in range(lax.axis_size("scan"))])
-    wm, wd1, wd2 = build(
+    wm, wd1, wd2 = pl.pallas_call(
         decoder_weights_body,
-        [(4 * LANES, 4 * LANES), (6 * LANES, 2 * LANES), (4 * hidden_lanes, 2 * LANES)],
-        (real_space, decoder_one.transpose(0, 1, 3, 2), decoder_two.transpose(0, 1, 3, 2)),
-        own,
-    )
-    other = encode(other_body, [(0, latent_rows)], latent_rows, far_x, far_halo, w1, w2, wm, wait_for=wm)
+        in_specs=[pl.BlockSpec()] * 3 + [pl.BlockSpec(memory_space=pl.ANY)],
+        out_shape=[
+            jax.ShapeDtypeStruct((4 * LANES, 4 * LANES), BF16),
+            jax.ShapeDtypeStruct((6 * LANES, 2 * LANES), BF16),
+            jax.ShapeDtypeStruct((4 * hidden_lanes, 2 * LANES), BF16),
+        ],
+        compiler_params=pltpu.CompilerParams(vmem_limit_bytes=12 << 20),
+        cost_estimate=cost(10**9, 4 << 20),
+        name="decoder_weights",
+    )(real_space, decoder_one.transpose(0, 1, 3, 2), decoder_two.transpose(0, 1, 3, 2), own)
+    far_inner = encode(far_inner_body, inner_runs, n_inner, far_x, w1, w2, wm, wait_for=wm)
+    other = encode(far_border_body, border_runs, latent_rows, far_x, far_halo, w1, w2, far_inner)
     rebuilt, part = pl.pallas_call(
         functools.partial(decode_body, strip=strip, cols=cols),
         out_shape=[

time: 57.7 us -> 49.3 us (0.85)
  Pallas kernels: 41.3 us -> 31.7 us
  starting transfers between devices: 6.99 us -> 7.71 us
    pallas_call x3 -> x4, Pallas kernels: 18.9 us -> 13.8 us  [encode(): pl.pallas_call(functools.partial(body, runs=runs, strip=strip, cols=cols,...]
    pallas_call x1, Pallas kernels: 17.3 us -> 13.7 us  [on_device(): pl.pallas_call(functools.partial(decode_body, strip=strip, cols=cols), ou...]
    ppermute x1, waiting for transfers between devices: 0.01 us -> 1.43 us  [on_device(): below = lax.ppermute(first, 'det', up)]
    ppermute x1, starting transfers between devices: 1.81 us -> 0.4 us  [on_device(): far_halo = lax.ppermute(halo, ('scan', 'det'), far)]
    ppermute x1, starting transfers between devices: 0.07 us -> 1.42 us  [on_device(): lax.ppermute(own, 'scan', [(i, i ^ 1) for i in range(lax.axis_size('scan'...]
    pallas_call x2, Pallas kernels: 5.14 us -> 4.15 us  [the longest x1 2.16 us: on_device(): pl.pallas_call(encoder_weights_body, in_specs=[pl.BlockSpec(memory_space=...]
    ppermute x1, waiting for transfers between devices: 0.85 us -> 0.01 us  [on_device(): far_halo = lax.ppermute(halo, ('scan', 'det'), far)]
    ppermute x2, starting transfers between devices: 2.13 us -> 2.91 us  [on_device(): lax.ppermute(misfit, 'det', [(i, i ^ bit) for i in range(n_det)])]
  transfers between devices with their start and end apart: 7 -> 7, of which waited for: 3 -> 4; matrix products, arithmetic and copies ran while one was open for 0% -> 0% of each run, Pallas kernels for 42% -> 37%
where the time goes in v4:
time: 49.3 us; the launch traced here: 48.5 us
  Pallas kernels  31.7 us (64%)
  starting transfers between devices  7.71 us (16%)
  waiting for transfers between devices  5.71 us (12%)
  local copies, waits for them, and re-layouts  2.14 us (4%)
  between operations  0.78 us (2%)
  other arithmetic  0.52 us (1%)
    pallas_call x4, Pallas kernels, encode(): pl.pallas_call(functools.partial(body, runs=runs, strip=strip, cols=cols,...  13.8 us
    pallas_call x1, Pallas kernels, on_device(): pl.pallas_call(functools.partial(decode_body, strip=strip, cols=cols), ou...  13.7 us
    ppermute x2, waiting for transfers between devices, on_device(): lax.ppermute(misfit, 'det', [(i, i ^ bit) for i in range(n_det)])  4.17 us
    ppermute x2, starting transfers between devices, on_device(): lax.ppermute(misfit, 'det', [(i, i ^ bit) for i in range(n_det)])  2.91 us
    pallas_call x1, Pallas kernels, on_device(): pl.pallas_call(encoder_weights_body, in_specs=[pl.BlockSpec(memory_space=...  2.16 us
    pallas_call x1, Pallas kernels, on_device(): pl.pallas_call(decoder_weights_body, in_specs=[pl.BlockSpec()] * 3 + [pl....  1.99 us
    ppermute x1, starting transfers between devices, on_device(): above = lax.ppermute(last, 'det', down)  1.54 us
    ppermute x1, starting transfers between devices, on_device(): below = lax.ppermute(first, 'det', up)  1.43 us
  transfers between devices with their start and end apart: 7, of which 4 were waited for; matrix products, arithmetic and copies ran while one was open for 0% of the time, Pallas kernels for 37%

profile of v4, /device:TPU:8, one launch (start us, length us, event | category | flops | bytes accessed | tf_op | source)
XLA Modules:
  0.0 48.5 jit_solution(4695357138285072547)
XLA Ops:
  0.6 0.0 copy-start
  0.6 1.1 %slice.6 = f32[1,64,7,128]{3,2,1,0:T(8,128)S(1)} slice(f32[1,64,32,128]{3,2,1,0:T(8,128)} %param.6), slice={[0:1], [0:64], [25:32], [0:128]} | slice | bytes 458752 | tf_op jit(solution)/shard_map/slice | solution.py:409
  1.7 1.0 %slice.7 = f32[1,64,4,128]{3,2,1,0:T(4,128)S(1)} slice(f32[1,64,32,128]{3,2,1,0:T(8,128)} %param.6), slice={[0:1], [0:64], [0:4], [0:128]} | slice | bytes 262144 | tf_op jit(solution)/shard_map/slice | solution.py:409
  2.8 1.5 %collective-permute-start = (f32[7,64,128]{2,1,0:T(8,128)S(1)}, f32[7,64,128]{2,1,0:T(8,128)S(1)}, u32[]{:S(2)}, u32[]{:S(2)}) collective-permute-start(f32[7,64,128]{2,1,0:T(8,128)S(1)} %bitcast.20), channel_id=1, source_target_pairs={{0,1},{1,2},{2,3},{3,0},{4,5},{5,6},{6,7},{7,4},{8,9},{9,10},{10,1... | collective-permute-start | bytes 688136 | tf_op jit(solution)/shard_map/ppermute | solution.py:411
  4.3 1.4 %collective-permute-start.1 = (f32[4,64,128]{2,1,0:T(8,128)S(1)}, f32[4,64,128]{2,1,0:T(8,128)S(1)}, u32[]{:S(2)}, u32[]{:S(2)}) collective-permute-start(f32[4,64,128]{2,1,0:T(8,128)S(1)} %bitcast.21), channel_id=1, source_target_pairs={{1,0},{2,1},{3,2},{0,3},{5,4},{6,5},{7,6},{4,7},{9,8},{10,9},{11,1... | collective-permute-start | bytes 393224 | tf_op jit(solution)/shard_map/ppermute | solution.py:412
  5.7 0.0 collective-permute-start.3
  5.7 2.2 %encoder_weights.1 = (bf16[256,1024]{1,0:T(8,128)(2,1)S(1)}, bf16[1792,256]{1,0:T(8,128)(2,1)S(1)}) custom-call(f32[3,3,1,16]{3,2,1,0:T(1,128)} %e1.1, f32[3,3,16,32]{3,2,1,0:T(8,128)} %e2.1), custom_call_target="tpu_custom_call" | custom-call | flops 1000000000 | bytes 4194304 | tf_op jit(solution)/shard_map/encoder_weights/pallas_call | solution.py:422
  7.9 0.0 copy-done
  7.9 4.5 %inner_body.1.inner = f32[448,1024]{1,0:T(8,128)S(1)} custom-call(f32[2048,128]{1,0:T(8,128)S(1)} %bitcast.15, bf16[256,1024]{1,0:T(8,128)(2,1)S(1)} %get-tuple-element.13.w1, bf16[1792,256]{1,0:T(8,128)(2,1)S(1)} %get-tuple-element.14.w2), custom_call_target="tpu_custom_call" | custom-call | flops 25367150592 | bytes 8388608 | tf_op jit(solution)/shard_map/inner_body/pallas_call | solution.py:440
  12.4 0.0 collective-permute-done
  12.5 1.4 %collective-permute-done.1 = f32[4,64,128]{2,1,0:T(8,128)S(1)} collective-permute-done((f32[4,64,128]{2,1,0:T(8,128)S(1)}, f32[4,64,128]{2,1,0:T(8,128)S(1)}, u32[]{:S(2)}, u32[]{:S(2)}) %collective-permute-start.1) | collective-permute-done | bytes 131104 | tf_op jit(solution)/shard_map/ppermute | solution.py:412
  13.9 0.0 copy-start.1
  13.9 0.0 copy-start.2
  14.0 0.0 copy-start.3
  14.0 0.4 collective-permute-start.4
  14.4 2.3 %border_body.1.after.own = f32[640,1024]{1,0:T(8,128)S(1)} custom-call(f32[2048,128]{1,0:T(8,128)S(1)} %bitcast.16, f32[11,64,128]{2,1,0:T(8,128)S(1)} %constant_dynamic-update-slice_fusion.halo, bf16[256,1024]{1,0:T(8,128)(2,1)S(1)} %get-tuple-element.13.w1, bf16[1792,256]{1,0:T(8,128)(2,1)S(1)} %get-tuple-element.14.w2, f32[448,1024]{1,0:T(8,128)S(1)} %inner_body.1.inner), custom_call_target="tpu_custom_call" | custom-call | flops 10871635968 | bytes 8388608 | tf_op jit(solution)/shard_map/border_body/pallas_call | solution.py:440
  16.6 1.4 %collective-permute-start.2 = (f32[640,1024]{1,0:T(8,128)S(1)}, f32[640,1024]{1,0:T(8,128)S(1)}, u32[]{:S(2)}, u32[]{:S(2)}) collective-permute-start(f32[640,1024]{1,0:T(8,128)S(1)} %border_body.1.after.own), channel_id=1, source_target_pairs={{0,4},{4,0},{8,12},{12,8},{16,20},{20,16},{24,28},{28,24},{1,5},{5... | collective-permute-start | bytes 7864328 | tf_op jit(solution)/shard_map/ppermute | solution.py:456
  18.0 0.0 copy-done.1
  18.1 0.0 copy-done.2
  18.1 0.0 copy-done.3
  18.1 2.0 %decoder_weights.1 = (bf16[512,512]{1,0:T(8,128)(2,1)S(1)}, bf16[768,256]{1,0:T(8,128)(2,1)S(1)}, bf16[4096,256]{1,0:T(8,128)(2,1)S(1)}) custom-call(f32[3,3,32,32]{3,2,1,0:T(8,128)S(1)} %copy-done.1, f32[3,3,16,32]{3,2,1,0:T(8,128)S(1)} %bitcast.18, f32[3,3,1,16]{3,2,1,0:T(1,128)S(1)} %bitcast.19, f32[640,1024]{1,0:T(8,128)S(1)} %border_body.1.after.own), custom_call_target="tpu_custom_call" | custom-call | flops 1000000000 | bytes 4194304 | tf_op jit(solution)/shard_map/decoder_weights/pallas_call | solution.py:457
  20.1 0.1 collective-permute-done.3.x
  20.2 4.6 %far_inner_body.1.inner = f32[448,1024]{1,0:T(8,128)S(1)} custom-call(f32[2048,128]{1,0:T(8,128)S(1)} %collective-permute-done.3.x, bf16[256,1024]{1,0:T(8,128)(2,1)S(1)} %get-tuple-element.13.w1, bf16[1792,256]{1,0:T(8,128)(2,1)S(1)} %get-tuple-element.14.w2, bf16[512,512]{1,0:T(8,128)(2,1)S(1)} %get-tuple-element.15.after.wm), custom_call_target="tpu_custom_call" | custom-call | flops 25367150592 | bytes 8388608 | tf_op jit(solution)/shard_map/far_inner_body/pallas_call | solution.py:440
  24.8 0.0 collective-permute-done.4.halo
  24.8 2.4 %far_border_body.1.other = f32[640,1024]{1,0:T(8,128)S(1)} custom-call(f32[2048,128]{1,0:T(8,128)S(1)} %collective-permute-done.3.x, f32[11,64,128]{2,1,0:T(8,128)S(1)} %collective-permute-done.4.halo, bf16[256,1024]{1,0:T(8,128)(2,1)S(1)} %get-tuple-element.13.w1, bf16[1792,256]{1,0:T(8,128)(2,1)S(1)} %get-tuple-element.14.w2, ...), custom_call_target="tpu_custom_call" | custom-call | flops 10871635968 | bytes 8388608 | tf_op jit(solution)/shard_map/far_border_body/pallas_call | solution.py:440
  27.2 0.0 collective-permute-done.2.sibling
  27.2 13.7 %decode.1 = (f32[2048,128]{1,0:T(8,128)}, f32[1,64]{1,0:T(1,128)S(1)}) custom-call(f32[640,1024]{1,0:T(8,128)S(1)} %border_body.1.after.own, f32[640,1024]{1,0:T(8,128)S(1)} %collective-permute-done.2.sibling, f32[640,1024]{1,0:T(8,128)S(1)} %far_border_body.1.other, f32[2048,128]{1,0:T(8,128)S(1)} %bitcast.17, ...), custom_call_target="tpu_custom_call" | custom-call | flops 7549747200 | bytes 16777216 | tf_op jit(solution)/shard_map/decode/pallas_call | solution.py:471
  40.9 1.5 %collective-permute-start.5 = (f32[1,64]{1,0:T(1,128)S(1)}, f32[1,64]{1,0:T(1,128)S(1)}, u32[]{:S(2)}, u32[]{:S(2)}) collective-permute-start(f32[1,64]{1,0:T(1,128)S(1)} %get-tuple-element.19), channel_id=1, source_target_pairs={{0,1},{1,0},{2,3},{3,2},{4,5},{5,4},{6,7},{7,6},{8,9},{9,8},{10,11... | collective-permute-start | bytes 776 | tf_op jit(solution)/shard_map/ppermute | solution.py:489
  42.4 2.0 %collective-permute-done.5 = f32[1,64]{1,0:T(1,128)S(1)} collective-permute-done((f32[1,64]{1,0:T(1,128)S(1)}, f32[1,64]{1,0:T(1,128)S(1)}, u32[]{:S(2)}, u32[]{:S(2)}) %collective-permute-start.5) | collective-permute-done | bytes 288 | tf_op jit(solution)/shard_map/ppermute | solution.py:489
  44.5 1.4 %collective-permute-start.6 = (f32[1,64]{1,0:T(1,128)S(1)}, f32[1,64]{1,0:T(1,128)S(1)}, u32[]{:S(2)}, u32[]{:S(2)}) collective-permute-start(f32[1,64]{1,0:T(1,128)S(1)} %add.6), channel_id=1, source_target_pairs={{0,2},{1,3},{2,0},{3,1},{4,6},{5,7},{6,4},{7,5},{8,10},{9,11},{10,... | collective-permute-start | bytes 776 | tf_op jit(solution)/shard_map/ppermute | solution.py:489
  45.9 2.1 %collective-permute-done.6 = f32[1,64]{1,0:T(1,128)S(1)} collective-permute-done((f32[1,64]{1,0:T(1,128)S(1)}, f32[1,64]{1,0:T(1,128)S(1)}, u32[]{:S(2)}, u32[]{:S(2)}) %collective-permute-start.6) | collective-permute-done | bytes 288 | tf_op jit(solution)/shard_map/ppermute | solution.py:489
  48.0 0.5 %add.7 = f32[1,64]{1,0:T(1,128)} add(f32[1,64]{1,0:T(1,128)S(1)} %add.6, f32[1,64]{1,0:T(1,128)S(1)} %collective-permute-done.6) | non-fusion elementwise | flops 64 | bytes 768 | tf_op jit(solution)/shard_map/add | solution.py:489
  (5 shorter events, 0.1 us)
Async XLA Ops:
  0.6 7.3 %copy-start = (f32[1,64,32,128]{3,2,1,0:T(8,128)S(1)}, f32[1,64,32,128]{3,2,1,0:T(8,128)}, u32[]{:S(2)}) copy-start(f32[1,64,32,128]{3,2,1,0:T(8,128)} %param.6) | copy-start | bytes 3145732
  2.8 9.7 %collective-permute-start = (f32[7,64,128]{2,1,0:T(8,128)S(1)}, f32[7,64,128]{2,1,0:T(8,128)S(1)}, u32[]{:S(2)}, u32[]{:S(2)}) collective-permute-start(f32[7,64,128]{2,1,0:T(8,128)S(1)} %bitcast.20), channel_id=1, source_target_pairs={{0,1},{1,2},{2,3},{3,0},{4,5},{5,6},{6,7},{7,4},{8,9},{9,10},{10,1... | collective-permute-start | bytes 688136 | tf_op jit(solution)/shard_map/ppermute | solution.py:411
  4.3 9.6 %collective-permute-start.1 = (f32[4,64,128]{2,1,0:T(8,128)S(1)}, f32[4,64,128]{2,1,0:T(8,128)S(1)}, u32[]{:S(2)}, u32[]{:S(2)}) collective-permute-start(f32[4,64,128]{2,1,0:T(8,128)S(1)} %bitcast.21), channel_id=1, source_target_pairs={{1,0},{2,1},{3,2},{0,3},{5,4},{6,5},{7,6},{4,7},{9,8},{10,9},{11,1... | collective-permute-start | bytes 393224 | tf_op jit(solution)/shard_map/ppermute | solution.py:412
  5.7 14.4 %collective-permute-start.3 = (f32[2048,128]{1,0:T(8,128)}, f32[2048,128]{1,0:T(8,128)S(1)}, u32[]{:S(2)}, u32[]{:S(2)}) collective-permute-start(f32[2048,128]{1,0:T(8,128)} %bitcast.14), channel_id=1, source_target_pairs={{0,2},{1,3},{2,0},{3,1},{4,8},{5,9},{6,10},{7,11},{8,4},{9,5},{10,... | collective-permute-start | bytes 3145736 | tf_op jit(solution)/shard_map/ppermute | solution.py:414
  13.9 4.1 %copy-start.1 = (f32[3,3,32,32]{3,2,1,0:T(8,128)S(1)}, f32[3,3,32,32]{3,2,1,0:T(8,128)}, u32[]{:S(2)}) copy-start(f32[3,3,32,32]{3,2,1,0:T(8,128)} %rs.1) | copy-start | bytes 110596
  13.9 4.1 %copy-start.2 = (f32[3,3,32,16]{2,3,1,0:T(8,128)S(1)}, f32[3,3,32,16]{2,3,1,0:T(8,128)}, u32[]{:S(2)}) copy-start(f32[3,3,32,16]{2,3,1,0:T(8,128)} %param.10) | copy-start | bytes 55300
  14.0 4.1 %copy-start.3 = (f32[3,3,16,1]{2,3,1,0:T(1,128)S(1)}, f32[3,3,16,1]{2,3,1,0:T(1,128)}, u32[]{:S(2)}) copy-start(f32[3,3,16,1]{2,3,1,0:T(1,128)} %param.11) | copy-start | bytes 1732
  14.0 10.8 %collective-permute-start.4 = (f32[11,64,128]{2,1,0:T(8,128)S(1)}, f32[11,64,128]{2,1,0:T(8,128)S(1)}, u32[]{:S(2)}, u32[]{:S(2)}) collective-permute-start(f32[11,64,128]{2,1,0:T(8,128)S(1)} %constant_dynamic-update-slice_fusion.halo), channel_id=1, source_target_pairs={{0,2},{1,3},{2,0},{3,1},{4,8},{5,9},{6,10},{7,11},{8,4},{9,5},{10,... | collective-permute-start | bytes 1081352 | tf_op jit(solution)/shard_map/ppermute | solution.py:416
  16.6 10.6 %collective-permute-start.2 = (f32[640,1024]{1,0:T(8,128)S(1)}, f32[640,1024]{1,0:T(8,128)S(1)}, u32[]{:S(2)}, u32[]{:S(2)}) collective-permute-start(f32[640,1024]{1,0:T(8,128)S(1)} %border_body.1.after.own), channel_id=1, source_target_pairs={{0,4},{4,0},{8,12},{12,8},{16,20},{20,16},{24,28},{28,24},{1,5},{5... | collective-permute-start | bytes 7864328 | tf_op jit(solution)/shard_map/ppermute | solution.py:456
  40.9 3.5 %collective-permute-start.5 = (f32[1,64]{1,0:T(1,128)S(1)}, f32[1,64]{1,0:T(1,128)S(1)}, u32[]{:S(2)}, u32[]{:S(2)}) collective-permute-start(f32[1,64]{1,0:T(1,128)S(1)} %get-tuple-element.19), channel_id=1, source_target_pairs={{0,1},{1,0},{2,3},{3,2},{4,5},{5,4},{6,7},{7,6},{8,9},{9,8},{10,11... | collective-permute-start | bytes 776 | tf_op jit(solution)/shard_map/ppermute | solution.py:489
  44.5 3.5 %collective-permute-start.6 = (f32[1,64]{1,0:T(1,128)S(1)}, f32[1,64]{1,0:T(1,128)S(1)}, u32[]{:S(2)}, u32[]{:S(2)}) collective-permute-start(f32[1,64]{1,0:T(1,128)S(1)} %add.6), channel_id=1, source_target_pairs={{0,2},{1,3},{2,0},{3,1},{4,6},{5,7},{6,4},{7,5},{8,10},{9,11},{10,... | collective-permute-start | bytes 776 | tf_op jit(solution)/shard_map/ppermute | solution.py:489

commit v5 on v4

--- a/solution.py
+++ b/solution.py
@@ -66,20 +66,29 @@
     return iota(shape, len(shape) - 1) ^ (lax.axis_index("scan") % 2 * (LANES // 2))
 
 
-def encoder_weights_body(e1, e2, w1, w2, t1, t2, sems):
-    copies = [pltpu.make_async_copy(a, b, sems.at[i]) for i, (a, b) in enumerate(((e1, t1), (e2, t2)))]
+def edges_body(x, e1, e2, last, first, e1_here, e2_here, bottom, top, sems):
+    strip = x.shape[1]
+    copies = [
+        pltpu.make_async_copy(a, b, sems.at[i])
+        for i, (a, b) in enumerate(
+            ((x.at[:, strip - 8 :, :], bottom), (x.at[:, :8, :], top), (e1, e1_here), (e2, e2_here))
+        )
+    ]
     for copy in copies:
         copy.start()
     for copy in copies:
         copy.wait()
-    encoder_weights(t1, t2, w1, w2)
+    for i in range(ABOVE):
+        last[i] = bottom[:, 8 - ABOVE + i, :]
+    for i in range(BELOW):
+        first[i] = top[:, i, :]
 
 
 def decoder_weights_body(rs, d1, d2, after, wm, wd1, wd2):
     decoder_weights(rs, d1, d2, wm, wd1, wd2)
 
 
-def encoder_weights(e1, e2, w1, w2):
+def encoder_weights_body(e1, e2, w1, w2):
     f1 = e1.shape[3]
     f2 = e2.shape[3]
     wide = spread(mosaic(e1), w1.shape[1])
@@ -270,6 +279,10 @@
     encode_rows(x, None, w1, w2, out, scratch, **sizes)
 
 
+def own_border_body(x, halo, w1, w2, inner, after, out, *scratch, **sizes):
+    border_body(x, halo, w1, w2, inner, out, *scratch, **sizes)
+
+
 def border_body(x, halo, w1, w2, inner, out, *scratch, runs, cols, **sizes):
     start = runs[0][1] * cols
     out[start : start + inner.shape[0], :] = inner[...]
@@ -286,7 +299,7 @@
         out[...] = jnp.zeros(out.shape, F32)
 
 
-def far_inner_body(x, w1, w2, after, out, *scratch, **sizes):
+def far_inner_body(x, w1, w2, out, *scratch, **sizes):
     inside_scan(lambda: inner_body(x, w1, w2, out, *scratch, **sizes), out)
 
 
@@ -383,12 +396,12 @@
     part[...] = jnp.sum(total.T, axis=0, keepdims=True) * (1.0 / (LANES * LANES))
 
 
-def far_route(n_scan, n_det):
+def far_route(n_scan, n_det, turn):
     route = []
     for i in range(n_scan):
         for j in range(n_det):
             rim = i == 0 or i == n_scan - 1
-            to = (i, (j + n_det // 2) % n_det) if rim else (i + 1 if i % 2 else i - 1, j)
+            to = (i, j ^ turn) if rim else (i + 1 if i % 2 else i - 1, j)
             route.append((i * n_det + j, to[0] * n_det + to[1]))
     return route
 
@@ -405,36 +418,48 @@
 
     down = [(i, (i + 1) % n_det) for i in range(n_det)]
     up = [(j, i) for i, j in down]
-    last, first = lax.optimization_barrier(
-        (patterns[0, :, strip - ABOVE :].transpose(1, 0, 2), patterns[0, :, :BELOW].transpose(1, 0, 2))
-    )
+    in_hbm = [
+        pltpu.with_memory_space_constraint(a, pltpu.HBM)
+        for a in (patterns.reshape(cols, strip, width), encoder_one, encoder_two)
+    ]
+    last, first, e1, e2 = pl.pallas_call(
+        edges_body,
+        in_specs=[pl.BlockSpec(memory_space=pltpu.HBM)] * 3,
+        out_shape=[
+            jax.ShapeDtypeStruct((ABOVE, cols, width), F32),
+            jax.ShapeDtypeStruct((BELOW, cols, width), F32),
+            jax.ShapeDtypeStruct(encoder_one.shape, F32),
+            jax.ShapeDtypeStruct(encoder_two.shape, F32),
+        ],
+        scratch_shapes=[pltpu.VMEM((cols, 8, width), F32)] * 2 + [pltpu.SemaphoreType.DMA((4,))],
+        compiler_params=pltpu.CompilerParams(vmem_limit_bytes=4 << 20),
+        name="edges",
+    )(*in_hbm)
     above = lax.ppermute(last, "det", down)
     below = lax.ppermute(first, "det", up)
-    far = far_route(lax.axis_size("scan"), n_det)
-    far_x = lax.ppermute(x, ("scan", "det"), far)
+    n_scan = lax.axis_size("scan")
+    far_x = lax.ppermute(x, ("scan", "det"), far_route(n_scan, n_det, n_det // 2))
     halo = jnp.concatenate([above, below], axis=0)
-    far_halo = lax.ppermute(halo, ("scan", "det"), far)
+
+    far_halo = lax.ppermute(halo, ("scan", "det"), far_route(n_scan, n_det, 1))
 
     def cost(flops, moved):
         return pl.CostEstimate(flops=flops, transcendentals=0, bytes_accessed=moved)
 
-    weights = (encoder_one, encoder_two)
     w1, w2 = pl.pallas_call(
         encoder_weights_body,
-        in_specs=[pl.BlockSpec(memory_space=pltpu.HBM)] * 2,
         out_shape=[
             jax.ShapeDtypeStruct((2 * LANES, hidden_lanes), BF16),
             jax.ShapeDtypeStruct((14 * LANES, 256), BF16),
         ],
-        scratch_shapes=[pltpu.VMEM(w.shape, F32) for w in weights] + [pltpu.SemaphoreType.DMA((2,))],
         compiler_params=pltpu.CompilerParams(vmem_limit_bytes=12 << 20),
-        cost_estimate=cost(10**9, 4 << 20),
+        cost_estimate=cost(2 * 10**9, 0),
         name="encoder_weights",
-    )(*[pltpu.with_memory_space_constraint(w, pltpu.HBM) for w in weights])
+    )(e1, e2)
 
     n_latent = latent_rows * cols
 
-    def encode(body, runs, rows, *operands, wait_for=None):
+    def encode(body, runs, rows, *operands, wait_for=None, weight=0):
         n_hidden = run_starts(runs, cols)[1]
         n_run = sum(count for _, count in runs) * cols
         return pl.pallas_call(
@@ -445,15 +470,13 @@
             + [pltpu.VMEM((n_hidden, hidden_lanes), BF16)] * 2
             + [pltpu.VMEM((n_run, hidden_lanes // 2 + LANES), BF16)] * 2,
             compiler_params=pltpu.CompilerParams(vmem_limit_bytes=ENCODE_VMEM),
-            cost_estimate=cost(2 * n_run * 27 * LANES * latent_lanes * 8, 8 << 20),
+            cost_estimate=cost(2 * n_run * 27 * LANES * latent_lanes * weight, 0),
             name=body.__name__,
         )(*operands)
 
     n_inner = latent_rows - 3
     inner_runs, border_runs = [(2, n_inner)], [(0, 2), (latent_rows - 1, 1)]
     inner = encode(inner_body, inner_runs, n_inner, x, w1, w2)
-    own = encode(border_body, border_runs, latent_rows, x, halo, w1, w2, inner)
-    sibling = lax.ppermute(own, "scan", [(i, i ^ 1) for i in range(lax.axis_size("scan"))])
     wm, wd1, wd2 = pl.pallas_call(
         decoder_weights_body,
         in_specs=[pl.BlockSpec()] * 3 + [pl.BlockSpec(memory_space=pl.ANY)],
@@ -463,11 +486,13 @@
             jax.ShapeDtypeStruct((4 * hidden_lanes, 2 * LANES), BF16),
         ],
         compiler_params=pltpu.CompilerParams(vmem_limit_bytes=12 << 20),
-        cost_estimate=cost(10**9, 4 << 20),
+        cost_estimate=cost(0, 0),
         name="decoder_weights",
-    )(real_space, decoder_one.transpose(0, 1, 3, 2), decoder_two.transpose(0, 1, 3, 2), own)
-    far_inner = encode(far_inner_body, inner_runs, n_inner, far_x, w1, w2, wm, wait_for=wm)
-    other = encode(far_border_body, border_runs, latent_rows, far_x, far_halo, w1, w2, far_inner)
+    )(real_space, decoder_one.transpose(0, 1, 3, 2), decoder_two.transpose(0, 1, 3, 2), inner)
+    own = encode(own_border_body, border_runs, latent_rows, x, halo, w1, w2, inner, wm, wait_for=wm)
+    sibling = lax.ppermute(own, "scan", [(i, i ^ 1) for i in range(lax.axis_size("scan"))])
+    far_inner = encode(far_inner_body, inner_runs, n_inner, far_x, w1, w2, weight=8)
+    other = encode(far_border_body, border_runs, latent_rows, far_x, far_halo, w1, w2, far_inner, weight=8)
     rebuilt, part = pl.pallas_call(
         functools.partial(decode_body, strip=strip, cols=cols),
         out_shape=[

time: 49.3 us -> 46.5 us (0.943)
  local copies, waits for them, and re-layouts: 2.14 us -> 0.05 us
  starting transfers between devices: 7.71 us -> 7.15 us
    slice x2 -> x0, local copies, waits for them, and re-layouts: 2.03 us -> none  [the longest x1 1.06 us: on_device(): patterns[0, :, strip - ABOVE:].transpose(1, 0, 2)]
    ppermute x1, waiting for transfers between devices: 1.43 us -> 0.76 us  [on_device(): below = lax.ppermute(first, 'det', up)]
    ppermute x2, starting transfers between devices: 2.91 us -> 2.28 us  [on_device(): lax.ppermute(misfit, 'det', [(i, i ^ bit) for i in range(n_det)])]
    ppermute x2, waiting for transfers between devices: 4.17 us -> 4.8 us  [on_device(): lax.ppermute(misfit, 'det', [(i, i ^ bit) for i in range(n_det)])]
    ppermute x2, starting transfers between devices: 0.4 us -> 1.03 us  [the longest x1 0.96 us: on_device(): far_halo = lax.ppermute(halo, ('scan', 'det'), far_route(n_scan, n_det, 1))]
    ppermute x1, starting transfers between devices: 1.42 us -> 0.87 us  [on_device(): lax.ppermute(own, 'scan', [(i, i ^ 1) for i in range(lax.axis_size('scan'...]
    pallas_call x1 -> x2, Pallas kernels: 2.16 us -> 2.53 us  [the longest x1 1.29 us: on_device(): pl.pallas_call(edges_body, in_specs=[pl.BlockSpec(memory_space=pltpu.HBM)...]
  transfers between devices with their start and end apart: 7 -> 7, of which waited for: 4 -> 3; matrix products, arithmetic and copies ran while one was open for 0% -> 0% of each run, Pallas kernels for 37% -> 40%
where the time goes in v5:
time: 46.5 us; the launch traced here: 46.1 us
  Pallas kernels  32.1 us (69%)
  starting transfers between devices  7.15 us (15%)
  waiting for transfers between devices  5.57 us (12%)
  between operations  0.79 us (2%)
  other arithmetic  0.52 us (1%)
    pallas_call x1, Pallas kernels, on_device(): pl.pallas_call(functools.partial(decode_body, strip=strip, cols=cols), ou...  13.8 us
    pallas_call x4, Pallas kernels, encode(): pl.pallas_call(functools.partial(body, runs=runs, strip=strip, cols=cols,...  13.7 us
    ppermute x2, waiting for transfers between devices, on_device(): lax.ppermute(misfit, 'det', [(i, i ^ bit) for i in range(n_det)])  4.8 us
    ppermute x2, starting transfers between devices, on_device(): lax.ppermute(misfit, 'det', [(i, i ^ bit) for i in range(n_det)])  2.28 us
    pallas_call x1, Pallas kernels, on_device(): pl.pallas_call(decoder_weights_body, in_specs=[pl.BlockSpec()] * 3 + [pl....  1.99 us
    ppermute x1, starting transfers between devices, on_device(): above = lax.ppermute(last, 'det', down)  1.54 us
    ppermute x1, starting transfers between devices, on_device(): below = lax.ppermute(first, 'det', up)  1.43 us
    pallas_call x1, Pallas kernels, on_device(): pl.pallas_call(edges_body, in_specs=[pl.BlockSpec(memory_space=pltpu.HBM)...  1.29 us
  transfers between devices with their start and end apart: 7, of which 3 were waited for; matrix products, arithmetic and copies ran while one was open for 0% of the time, Pallas kernels for 40%

profile of v5, /device:TPU:8, one launch (start us, length us, event | category | flops | bytes accessed | tf_op | source)
XLA Modules:
  0.0 46.1 jit_solution(16587383015114261369)
XLA Ops:
  0.6 0.1 collective-permute-start.3
  0.7 1.3 %edges.1 = (f32[7,64,128]{2,1,0:T(8,128)S(1)}, f32[4,64,128]{2,1,0:T(8,128)S(1)}, f32[3,3,1,16]{3,2,1,0:T(1,128)S(1)}, f32[3,3,16,32]{3,2,1,0:T(8,128)S(1)}) custom-call(f32[64,32,128]{2,1,0:T(8,128)} %bitcast.6, f32[3,3,1,16]{3,2,1,0:T(1,128)} %e1.1, f32[3,3,16,32]{3,2,1,0:T(8,128)} %e2.1), custom_call_target="tpu_custom_call" | custom-call | tf_op jit(solution)/shard_map/edges/pallas_call | solution.py:425
  2.0 1.5 %collective-permute-start = (f32[7,64,128]{2,1,0:T(8,128)S(1)}, f32[7,64,128]{2,1,0:T(8,128)S(1)}, u32[]{:S(2)}, u32[]{:S(2)}) collective-permute-start(f32[7,64,128]{2,1,0:T(8,128)S(1)} %get-tuple-element.13), channel_id=1, source_target_pairs={{0,1},{1,2},{2,3},{3,0},{4,5},{5,6},{6,7},{7,4},{8,9},{9,10},{10,1... | collective-permute-start | bytes 688136 | tf_op jit(solution)/shard_map/ppermute | solution.py:438
  3.6 1.4 %collective-permute-start.1 = (f32[4,64,128]{2,1,0:T(8,128)S(1)}, f32[4,64,128]{2,1,0:T(8,128)S(1)}, u32[]{:S(2)}, u32[]{:S(2)}) collective-permute-start(f32[4,64,128]{2,1,0:T(8,128)S(1)} %get-tuple-element.14), channel_id=1, source_target_pairs={{1,0},{2,1},{3,2},{0,3},{5,4},{6,5},{7,6},{4,7},{9,8},{10,9},{11,1... | collective-permute-start | bytes 393224 | tf_op jit(solution)/shard_map/ppermute | solution.py:439
  5.0 0.0 copy-start
  5.0 1.2 %encoder_weights.1 = (bf16[256,1024]{1,0:T(8,128)(2,1)S(1)}, bf16[1792,256]{1,0:T(8,128)(2,1)S(1)}) custom-call(f32[3,3,1,16]{3,2,1,0:T(1,128)S(1)} %get-tuple-element.15.e1, f32[3,3,16,32]{3,2,1,0:T(8,128)S(1)} %get-tuple-element.16.e2), custom_call_target="tpu_custom_call" | custom-call | flops 2000000000 | tf_op jit(solution)/shard_map/encoder_weights/pallas_call | solution.py:449
  6.2 0.0 copy-start.1
  6.2 0.0 copy-start.2
  6.3 0.0 copy-start.3
  6.3 0.0 copy-done
  6.3 4.5 %inner_body.1.after.inner = f32[448,1024]{1,0:T(8,128)S(1)} custom-call(f32[2048,128]{1,0:T(8,128)S(1)} %bitcast.7, bf16[256,1024]{1,0:T(8,128)(2,1)S(1)} %get-tuple-element.17.w1, bf16[1792,256]{1,0:T(8,128)(2,1)S(1)} %get-tuple-element.18.w2), custom_call_target="tpu_custom_call" | custom-call | tf_op jit(solution)/shard_map/inner_body/pallas_call | solution.py:465
  10.8 0.0 copy-done.1
  10.8 0.0 copy-done.2
  10.8 0.0 copy-done.3
  10.9 2.0 %decoder_weights.1 = (bf16[512,512]{1,0:T(8,128)(2,1)S(1)}, bf16[768,256]{1,0:T(8,128)(2,1)S(1)}, bf16[4096,256]{1,0:T(8,128)(2,1)S(1)}) custom-call(f32[3,3,32,32]{3,2,1,0:T(8,128)S(1)} %copy-done.1, f32[3,3,16,32]{3,2,1,0:T(8,128)S(1)} %bitcast.10, f32[3,3,1,16]{3,2,1,0:T(1,128)S(1)} %bitcast.11, f32[448,1024]{1,0:T(8,128)S(1)} %inner_body.1.after.inner), custom_call_target="tpu_custom_call" | custom-call | tf_op jit(solution)/shard_map/decoder_weights/pallas_call | solution.py:480
  12.9 0.0 collective-permute-done
  12.9 0.8 %collective-permute-done.1 = f32[4,64,128]{2,1,0:T(8,128)S(1)} collective-permute-done((f32[4,64,128]{2,1,0:T(8,128)S(1)}, f32[4,64,128]{2,1,0:T(8,128)S(1)}, u32[]{:S(2)}, u32[]{:S(2)}) %collective-permute-start.1) | collective-permute-done | bytes 131104 | tf_op jit(solution)/shard_map/ppermute | solution.py:439
  13.7 1.0 %collective-permute-start.4 = (f32[11,64,128]{2,1,0:T(8,128)S(1)}, f32[11,64,128]{2,1,0:T(8,128)S(1)}, u32[]{:S(2)}, u32[]{:S(2)}) collective-permute-start(f32[11,64,128]{2,1,0:T(8,128)S(1)} %constant_dynamic-update-slice_fusion.halo), channel_id=1, source_target_pairs={{0,1},{1,0},{2,3},{3,2},{4,8},{5,9},{6,10},{7,11},{8,4},{9,5},{10,... | collective-permute-start | bytes 1081352 | tf_op jit(solution)/shard_map/ppermute | solution.py:444
  14.6 2.3 %own_border_body.1.own = f32[640,1024]{1,0:T(8,128)S(1)} custom-call(f32[2048,128]{1,0:T(8,128)S(1)} %bitcast.8, f32[11,64,128]{2,1,0:T(8,128)S(1)} %constant_dynamic-update-slice_fusion.halo, bf16[256,1024]{1,0:T(8,128)(2,1)S(1)} %get-tuple-element.17.w1, bf16[1792,256]{1,0:T(8,128)(2,1)S(1)} %get-tuple-element.18.w2, ...), custom_call_target="tpu_custom_call" | custom-call | tf_op jit(solution)/shard_map/own_border_body/pallas_call | solution.py:465
  16.9 0.9 %collective-permute-start.2 = (f32[640,1024]{1,0:T(8,128)S(1)}, f32[640,1024]{1,0:T(8,128)S(1)}, u32[]{:S(2)}, u32[]{:S(2)}) collective-permute-start(f32[640,1024]{1,0:T(8,128)S(1)} %own_border_body.1.own), channel_id=1, source_target_pairs={{0,4},{4,0},{8,12},{12,8},{16,20},{20,16},{24,28},{28,24},{1,5},{5... | collective-permute-start | bytes 7864328 | tf_op jit(solution)/shard_map/ppermute | solution.py:493
  17.7 0.0 collective-permute-done.3.x
  17.7 4.5 %far_inner_body.1.inner = f32[448,1024]{1,0:T(8,128)S(1)} custom-call(f32[2048,128]{1,0:T(8,128)S(1)} %collective-permute-done.3.x, bf16[256,1024]{1,0:T(8,128)(2,1)S(1)} %get-tuple-element.17.w1, bf16[1792,256]{1,0:T(8,128)(2,1)S(1)} %get-tuple-element.18.w2), custom_call_target="tpu_custom_call" | custom-call | flops 25367150592 | tf_op jit(solution)/shard_map/far_inner_body/pallas_call | solution.py:465
  22.3 0.0 collective-permute-done.4.halo
  22.3 2.4 %far_border_body.1.other = f32[640,1024]{1,0:T(8,128)S(1)} custom-call(f32[2048,128]{1,0:T(8,128)S(1)} %collective-permute-done.3.x, f32[11,64,128]{2,1,0:T(8,128)S(1)} %collective-permute-done.4.halo, bf16[256,1024]{1,0:T(8,128)(2,1)S(1)} %get-tuple-element.17.w1, bf16[1792,256]{1,0:T(8,128)(2,1)S(1)} %get-tuple-element.18.w2, ...), custom_call_target="tpu_custom_call" | custom-call | flops 10871635968 | tf_op jit(solution)/shard_map/far_border_body/pallas_call | solution.py:465
  24.7 0.0 collective-permute-done.2.sibling
  24.7 13.8 %decode.1 = (f32[2048,128]{1,0:T(8,128)}, f32[1,64]{1,0:T(1,128)S(1)}) custom-call(f32[640,1024]{1,0:T(8,128)S(1)} %own_border_body.1.own, f32[640,1024]{1,0:T(8,128)S(1)} %collective-permute-done.2.sibling, f32[640,1024]{1,0:T(8,128)S(1)} %far_border_body.1.other, f32[2048,128]{1,0:T(8,128)S(1)} %bitcast.9, ...), custom_call_target="tpu_custom_call" | custom-call | flops 7549747200 | bytes 16777216 | tf_op jit(solution)/shard_map/decode/pallas_call | solution.py:496
  38.5 1.5 %collective-permute-start.5 = (f32[1,64]{1,0:T(1,128)S(1)}, f32[1,64]{1,0:T(1,128)S(1)}, u32[]{:S(2)}, u32[]{:S(2)}) collective-permute-start(f32[1,64]{1,0:T(1,128)S(1)} %get-tuple-element.23), channel_id=1, source_target_pairs={{0,1},{1,0},{2,3},{3,2},{4,5},{5,4},{6,7},{7,6},{8,9},{9,8},{10,11... | collective-permute-start | bytes 776 | tf_op jit(solution)/shard_map/ppermute | solution.py:514
  40.0 2.0 %collective-permute-done.5 = f32[1,64]{1,0:T(1,128)S(1)} collective-permute-done((f32[1,64]{1,0:T(1,128)S(1)}, f32[1,64]{1,0:T(1,128)S(1)}, u32[]{:S(2)}, u32[]{:S(2)}) %collective-permute-start.5) | collective-permute-done | bytes 288 | tf_op jit(solution)/shard_map/ppermute | solution.py:514
  42.1 0.8 %collective-permute-start.6 = (f32[1,64]{1,0:T(1,128)S(1)}, f32[1,64]{1,0:T(1,128)S(1)}, u32[]{:S(2)}, u32[]{:S(2)}) collective-permute-start(f32[1,64]{1,0:T(1,128)S(1)} %add.6), channel_id=1, source_target_pairs={{0,2},{1,3},{2,0},{3,1},{4,6},{5,7},{6,4},{7,5},{8,10},{9,11},{10,... | collective-permute-start | bytes 776 | tf_op jit(solution)/shard_map/ppermute | solution.py:514
  42.9 2.8 %collective-permute-done.6 = f32[1,64]{1,0:T(1,128)S(1)} collective-permute-done((f32[1,64]{1,0:T(1,128)S(1)}, f32[1,64]{1,0:T(1,128)S(1)}, u32[]{:S(2)}, u32[]{:S(2)}) %collective-permute-start.6) | collective-permute-done | bytes 288 | tf_op jit(solution)/shard_map/ppermute | solution.py:514
  45.6 0.5 %add.7 = f32[1,64]{1,0:T(1,128)} add(f32[1,64]{1,0:T(1,128)S(1)} %add.6, f32[1,64]{1,0:T(1,128)S(1)} %collective-permute-done.6) | non-fusion elementwise | flops 64 | bytes 768 | tf_op jit(solution)/shard_map/add | solution.py:514
  (3 shorter events, 0.0 us)
Async XLA Ops:
  0.6 17.1 %collective-permute-start.3 = (f32[2048,128]{1,0:T(8,128)}, f32[2048,128]{1,0:T(8,128)S(1)}, u32[]{:S(2)}, u32[]{:S(2)}) collective-permute-start(f32[2048,128]{1,0:T(8,128)} %bitcast.5), channel_id=1, source_target_pairs={{0,2},{1,3},{2,0},{3,1},{4,8},{5,9},{6,10},{7,11},{8,4},{9,5},{10,... | collective-permute-start | bytes 3145736 | tf_op jit(solution)/shard_map/ppermute | solution.py:441
  2.0 10.8 %collective-permute-start = (f32[7,64,128]{2,1,0:T(8,128)S(1)}, f32[7,64,128]{2,1,0:T(8,128)S(1)}, u32[]{:S(2)}, u32[]{:S(2)}) collective-permute-start(f32[7,64,128]{2,1,0:T(8,128)S(1)} %get-tuple-element.13), channel_id=1, source_target_pairs={{0,1},{1,2},{2,3},{3,0},{4,5},{5,6},{6,7},{7,4},{8,9},{9,10},{10,1... | collective-permute-start | bytes 688136 | tf_op jit(solution)/shard_map/ppermute | solution.py:438
  3.6 10.1 %collective-permute-start.1 = (f32[4,64,128]{2,1,0:T(8,128)S(1)}, f32[4,64,128]{2,1,0:T(8,128)S(1)}, u32[]{:S(2)}, u32[]{:S(2)}) collective-permute-start(f32[4,64,128]{2,1,0:T(8,128)S(1)} %get-tuple-element.14), channel_id=1, source_target_pairs={{1,0},{2,1},{3,2},{0,3},{5,4},{6,5},{7,6},{4,7},{9,8},{10,9},{11,1... | collective-permute-start | bytes 393224 | tf_op jit(solution)/shard_map/ppermute | solution.py:439
  5.0 1.3 %copy-start = (f32[1,64,32,128]{3,2,1,0:T(8,128)S(1)}, f32[1,64,32,128]{3,2,1,0:T(8,128)}, u32[]{:S(2)}) copy-start(f32[1,64,32,128]{3,2,1,0:T(8,128)} %param.6) | copy-start | bytes 3145732
  6.2 4.6 %copy-start.1 = (f32[3,3,32,32]{3,2,1,0:T(8,128)S(1)}, f32[3,3,32,32]{3,2,1,0:T(8,128)}, u32[]{:S(2)}) copy-start(f32[3,3,32,32]{3,2,1,0:T(8,128)} %rs.1) | copy-start | bytes 110596
  6.2 4.6 %copy-start.2 = (f32[3,3,32,16]{2,3,1,0:T(8,128)S(1)}, f32[3,3,32,16]{2,3,1,0:T(8,128)}, u32[]{:S(2)}) copy-start(f32[3,3,32,16]{2,3,1,0:T(8,128)} %param.10) | copy-start | bytes 55300
  6.3 4.6 %copy-start.3 = (f32[3,3,16,1]{2,3,1,0:T(1,128)S(1)}, f32[3,3,16,1]{2,3,1,0:T(1,128)}, u32[]{:S(2)}) copy-start(f32[3,3,16,1]{2,3,1,0:T(1,128)} %param.11) | copy-start | bytes 1732
  13.7 8.6 %collective-permute-start.4 = (f32[11,64,128]{2,1,0:T(8,128)S(1)}, f32[11,64,128]{2,1,0:T(8,128)S(1)}, u32[]{:S(2)}, u32[]{:S(2)}) collective-permute-start(f32[11,64,128]{2,1,0:T(8,128)S(1)} %constant_dynamic-update-slice_fusion.halo), channel_id=1, source_target_pairs={{0,1},{1,0},{2,3},{3,2},{4,8},{5,9},{6,10},{7,11},{8,4},{9,5},{10,... | collective-permute-start | bytes 1081352 | tf_op jit(solution)/shard_map/ppermute | solution.py:444
  16.9 7.8 %collective-permute-start.2 = (f32[640,1024]{1,0:T(8,128)S(1)}, f32[640,1024]{1,0:T(8,128)S(1)}, u32[]{:S(2)}, u32[]{:S(2)}) collective-permute-start(f32[640,1024]{1,0:T(8,128)S(1)} %own_border_body.1.own), channel_id=1, source_target_pairs={{0,4},{4,0},{8,12},{12,8},{16,20},{20,16},{24,28},{28,24},{1,5},{5... | collective-permute-start | bytes 7864328 | tf_op jit(solution)/shard_map/ppermute | solution.py:493
  38.5 3.5 %collective-permute-start.5 = (f32[1,64]{1,0:T(1,128)S(1)}, f32[1,64]{1,0:T(1,128)S(1)}, u32[]{:S(2)}, u32[]{:S(2)}) collective-permute-start(f32[1,64]{1,0:T(1,128)S(1)} %get-tuple-element.23), channel_id=1, source_target_pairs={{0,1},{1,0},{2,3},{3,2},{4,5},{5,4},{6,7},{7,6},{8,9},{9,8},{10,11... | collective-permute-start | bytes 776 | tf_op jit(solution)/shard_map/ppermute | solution.py:514
  42.1 3.5 %collective-permute-start.6 = (f32[1,64]{1,0:T(1,128)S(1)}, f32[1,64]{1,0:T(1,128)S(1)}, u32[]{:S(2)}, u32[]{:S(2)}) collective-permute-start(f32[1,64]{1,0:T(1,128)S(1)} %add.6), channel_id=1, source_target_pairs={{0,2},{1,3},{2,0},{3,1},{4,6},{5,7},{6,4},{7,5},{8,10},{9,11},{10,... | collective-permute-start | bytes 776 | tf_op jit(solution)/shard_map/ppermute | solution.py:514

commit v6 on v5

--- a/solution.py
+++ b/solution.py
@@ -496,7 +496,7 @@
     rebuilt, part = pl.pallas_call(
         functools.partial(decode_body, strip=strip, cols=cols),
         out_shape=[
-            jax.ShapeDtypeStruct((cols * strip, width), F32),
+            pltpu.VMEM((cols * strip, width), F32),
             jax.ShapeDtypeStruct((1, cols), F32),
         ],
         scratch_shapes=[
@@ -508,11 +508,10 @@
         cost_estimate=cost(2 * n_latent * 45 * LANES * latent_lanes, 16 << 20),
         name="decode",
     )(own, sibling, other, x, wm, wd1, wd2)
-    if n_det & (n_det - 1) == 0:
-        misfit, bit = part, 1
-        while bit < n_det:
-            misfit = misfit + lax.ppermute(misfit, "det", [(i, i ^ bit) for i in range(n_det)])
-            bit *= 2
+    if n_det == 4:
+        misfit = part
+        for bit in (1, 2, 3):
+            misfit = misfit + lax.ppermute(part, "det", [(i, i ^ bit) for i in range(n_det)])
     else:
         misfit = lax.psum(part, "det")
     return rebuilt.reshape(patterns.shape), misfit

time: 46.5 us -> 45 us (0.968)
  waiting for transfers between devices: 5.57 us -> 2.8 us
  starting transfers between devices: 7.15 us -> 8.43 us
  local copies, waits for them, and re-layouts: 0.05 us -> 1.02 us
  Pallas kernels: 32.1 us -> 31.3 us
    ppermute x2 -> x3, waiting for transfers between devices: 4.8 us -> 2.03 us  [on_device(): lax.ppermute(part, 'det', [(i, i ^ bit) for i in range(n_det)])]
    ppermute x2 -> x3, starting transfers between devices: 2.28 us -> 3.55 us  [on_device(): lax.ppermute(part, 'det', [(i, i ^ bit) for i in range(n_det)])]
    unnamed x9 -> x10, local copies, waits for them, and re-layouts: 0.04 us -> 1.01 us
    pallas_call x1, Pallas kernels: 13.8 us -> 13 us  [on_device(): pl.pallas_call(functools.partial(decode_body, strip=strip, cols=cols), ou...]
  transfers between devices with their start and end apart: 7 -> 8, of which waited for: 3 -> 3; matrix products, arithmetic and copies ran while one was open for 0% -> 2% of each run, Pallas kernels for 40% -> 41%
where the time goes in v6:
time: 45 us; the launch traced here: 44.8 us
  Pallas kernels  31.3 us (70%)
  starting transfers between devices  8.43 us (19%)
  waiting for transfers between devices  2.8 us (6%)
  local copies, waits for them, and re-layouts  1.02 us (2%)
  between operations  0.79 us (2%)
  other arithmetic  0.52 us (1%)
    pallas_call x4, Pallas kernels, encode(): pl.pallas_call(functools.partial(body, runs=runs, strip=strip, cols=cols,...  13.7 us
    pallas_call x1, Pallas kernels, on_device(): pl.pallas_call(functools.partial(decode_body, strip=strip, cols=cols), ou...  13 us
    ppermute x3, starting transfers between devices, on_device(): lax.ppermute(part, 'det', [(i, i ^ bit) for i in range(n_det)])  3.55 us
    ppermute x3, waiting for transfers between devices, on_device(): lax.ppermute(part, 'det', [(i, i ^ bit) for i in range(n_det)])  2.03 us
    pallas_call x1, Pallas kernels, on_device(): pl.pallas_call(decoder_weights_body, in_specs=[pl.BlockSpec()] * 3 + [pl....  1.99 us
    ppermute x1, starting transfers between devices, on_device(): above = lax.ppermute(last, 'det', down)  1.54 us
    ppermute x1, starting transfers between devices, on_device(): below = lax.ppermute(first, 'det', up)  1.43 us
    pallas_call x1, Pallas kernels, on_device(): pl.pallas_call(edges_body, in_specs=[pl.BlockSpec(memory_space=pltpu.HBM)...  1.29 us
  transfers between devices with their start and end apart: 8, of which 3 were waited for; matrix products, arithmetic and copies ran while one was open for 2% of the time, Pallas kernels for 41%

profile of v6, /device:TPU:8, one launch (start us, length us, event | category | flops | bytes accessed | tf_op | source)
XLA Modules:
  0.0 44.8 jit_solution(13419120185041863152)
XLA Ops:
  0.6 0.1 collective-permute-start.3
  0.7 1.3 %edges.1 = (f32[7,64,128]{2,1,0:T(8,128)S(1)}, f32[4,64,128]{2,1,0:T(8,128)S(1)}, f32[3,3,1,16]{3,2,1,0:T(1,128)S(1)}, f32[3,3,16,32]{3,2,1,0:T(8,128)S(1)}) custom-call(f32[64,32,128]{2,1,0:T(8,128)} %bitcast.7, f32[3,3,1,16]{3,2,1,0:T(1,128)} %e1.1, f32[3,3,16,32]{3,2,1,0:T(8,128)} %e2.1), custom_call_target="tpu_custom_call" | custom-call | tf_op jit(solution)/shard_map/edges/pallas_call | solution.py:425
  2.0 1.5 %collective-permute-start = (f32[7,64,128]{2,1,0:T(8,128)S(1)}, f32[7,64,128]{2,1,0:T(8,128)S(1)}, u32[]{:S(2)}, u32[]{:S(2)}) collective-permute-start(f32[7,64,128]{2,1,0:T(8,128)S(1)} %get-tuple-element.13), channel_id=1, source_target_pairs={{0,1},{1,2},{2,3},{3,0},{4,5},{5,6},{6,7},{7,4},{8,9},{9,10},{10,1... | collective-permute-start | bytes 688136 | tf_op jit(solution)/shard_map/ppermute | solution.py:438
  3.6 1.4 %collective-permute-start.1 = (f32[4,64,128]{2,1,0:T(8,128)S(1)}, f32[4,64,128]{2,1,0:T(8,128)S(1)}, u32[]{:S(2)}, u32[]{:S(2)}) collective-permute-start(f32[4,64,128]{2,1,0:T(8,128)S(1)} %get-tuple-element.14), channel_id=1, source_target_pairs={{1,0},{2,1},{3,2},{0,3},{5,4},{6,5},{7,6},{4,7},{9,8},{10,9},{11,1... | collective-permute-start | bytes 393224 | tf_op jit(solution)/shard_map/ppermute | solution.py:439
  5.0 0.0 copy-start
  5.0 1.2 %encoder_weights.1 = (bf16[256,1024]{1,0:T(8,128)(2,1)S(1)}, bf16[1792,256]{1,0:T(8,128)(2,1)S(1)}) custom-call(f32[3,3,1,16]{3,2,1,0:T(1,128)S(1)} %get-tuple-element.15.e1, f32[3,3,16,32]{3,2,1,0:T(8,128)S(1)} %get-tuple-element.16.e2), custom_call_target="tpu_custom_call" | custom-call | flops 2000000000 | tf_op jit(solution)/shard_map/encoder_weights/pallas_call | solution.py:449
  6.2 0.0 copy-start.1
  6.2 0.0 copy-start.2
  6.3 0.0 copy-start.3
  6.3 0.0 copy-done
  6.3 4.5 %inner_body.1.after.inner = f32[448,1024]{1,0:T(8,128)S(1)} custom-call(f32[2048,128]{1,0:T(8,128)S(1)} %bitcast.8, bf16[256,1024]{1,0:T(8,128)(2,1)S(1)} %get-tuple-element.17.w1, bf16[1792,256]{1,0:T(8,128)(2,1)S(1)} %get-tuple-element.18.w2), custom_call_target="tpu_custom_call" | custom-call | tf_op jit(solution)/shard_map/inner_body/pallas_call | solution.py:465
  10.8 0.0 copy-done.1
  10.8 0.0 copy-done.2
  10.8 0.0 copy-done.3
  10.9 2.0 %decoder_weights.1 = (bf16[512,512]{1,0:T(8,128)(2,1)S(1)}, bf16[768,256]{1,0:T(8,128)(2,1)S(1)}, bf16[4096,256]{1,0:T(8,128)(2,1)S(1)}) custom-call(f32[3,3,32,32]{3,2,1,0:T(8,128)S(1)} %copy-done.1, f32[3,3,16,32]{3,2,1,0:T(8,128)S(1)} %bitcast.11, f32[3,3,1,16]{3,2,1,0:T(1,128)S(1)} %bitcast.12, f32[448,1024]{1,0:T(8,128)S(1)} %inner_body.1.after.inner), custom_call_target="tpu_custom_call" | custom-call | tf_op jit(solution)/shard_map/decoder_weights/pallas_call | solution.py:480
  12.9 0.0 collective-permute-done
  12.9 0.8 %collective-permute-done.1 = f32[4,64,128]{2,1,0:T(8,128)S(1)} collective-permute-done((f32[4,64,128]{2,1,0:T(8,128)S(1)}, f32[4,64,128]{2,1,0:T(8,128)S(1)}, u32[]{:S(2)}, u32[]{:S(2)}) %collective-permute-start.1) | collective-permute-done | bytes 131104 | tf_op jit(solution)/shard_map/ppermute | solution.py:439
  13.7 1.0 %collective-permute-start.4 = (f32[11,64,128]{2,1,0:T(8,128)S(1)}, f32[11,64,128]{2,1,0:T(8,128)S(1)}, u32[]{:S(2)}, u32[]{:S(2)}) collective-permute-start(f32[11,64,128]{2,1,0:T(8,128)S(1)} %constant_dynamic-update-slice_fusion.halo), channel_id=1, source_target_pairs={{0,1},{1,0},{2,3},{3,2},{4,8},{5,9},{6,10},{7,11},{8,4},{9,5},{10,... | collective-permute-start | bytes 1081352 | tf_op jit(solution)/shard_map/ppermute | solution.py:444
  14.6 2.3 %own_border_body.1.own = f32[640,1024]{1,0:T(8,128)S(1)} custom-call(f32[2048,128]{1,0:T(8,128)S(1)} %bitcast.9, f32[11,64,128]{2,1,0:T(8,128)S(1)} %constant_dynamic-update-slice_fusion.halo, bf16[256,1024]{1,0:T(8,128)(2,1)S(1)} %get-tuple-element.17.w1, bf16[1792,256]{1,0:T(8,128)(2,1)S(1)} %get-tuple-element.18.w2, ...), custom_call_target="tpu_custom_call" | custom-call | tf_op jit(solution)/shard_map/own_border_body/pallas_call | solution.py:465
  16.9 0.9 %collective-permute-start.2 = (f32[640,1024]{1,0:T(8,128)S(1)}, f32[640,1024]{1,0:T(8,128)S(1)}, u32[]{:S(2)}, u32[]{:S(2)}) collective-permute-start(f32[640,1024]{1,0:T(8,128)S(1)} %own_border_body.1.own), channel_id=1, source_target_pairs={{0,4},{4,0},{8,12},{12,8},{16,20},{20,16},{24,28},{28,24},{1,5},{5... | collective-permute-start | bytes 7864328 | tf_op jit(solution)/shard_map/ppermute | solution.py:493
  17.7 0.0 collective-permute-done.3.x
  17.7 4.5 %far_inner_body.1.inner = f32[448,1024]{1,0:T(8,128)S(1)} custom-call(f32[2048,128]{1,0:T(8,128)S(1)} %collective-permute-done.3.x, bf16[256,1024]{1,0:T(8,128)(2,1)S(1)} %get-tuple-element.17.w1, bf16[1792,256]{1,0:T(8,128)(2,1)S(1)} %get-tuple-element.18.w2), custom_call_target="tpu_custom_call" | custom-call | flops 25367150592 | tf_op jit(solution)/shard_map/far_inner_body/pallas_call | solution.py:465
  22.3 0.0 collective-permute-done.4.halo
  22.3 2.4 %far_border_body.1.other = f32[640,1024]{1,0:T(8,128)S(1)} custom-call(f32[2048,128]{1,0:T(8,128)S(1)} %collective-permute-done.3.x, f32[11,64,128]{2,1,0:T(8,128)S(1)} %collective-permute-done.4.halo, bf16[256,1024]{1,0:T(8,128)(2,1)S(1)} %get-tuple-element.17.w1, bf16[1792,256]{1,0:T(8,128)(2,1)S(1)} %get-tuple-element.18.w2, ...), custom_call_target="tpu_custom_call" | custom-call | flops 10871635968 | tf_op jit(solution)/shard_map/far_border_body/pallas_call | solution.py:465
  24.7 0.0 collective-permute-done.2.sibling
  24.7 13.0 %decode.1 = (f32[2048,128]{1,0:T(8,128)S(1)}, f32[1,64]{1,0:T(1,128)S(1)}) custom-call(f32[640,1024]{1,0:T(8,128)S(1)} %own_border_body.1.own, f32[640,1024]{1,0:T(8,128)S(1)} %collective-permute-done.2.sibling, f32[640,1024]{1,0:T(8,128)S(1)} %far_border_body.1.other, f32[2048,128]{1,0:T(8,128)S(1)} %bitcast.10, ...), custom_call_target="tpu_custom_call" | custom-call | flops 7549747200 | bytes 16777216 | tf_op jit(solution)/shard_map/decode/pallas_call | solution.py:496
  37.7 1.5 %collective-permute-start.7 = (f32[1,64]{1,0:T(1,128)S(1)}, f32[1,64]{1,0:T(1,128)S(1)}, u32[]{:S(2)}, u32[]{:S(2)}) collective-permute-start(f32[1,64]{1,0:T(1,128)S(1)} %get-tuple-element.23), channel_id=1, source_target_pairs={{0,3},{1,2},{2,1},{3,0},{4,7},{5,6},{6,5},{7,4},{8,11},{9,10},{10,... | collective-permute-start | bytes 776 | tf_op jit(solution)/shard_map/ppermute | solution.py:514
  39.2 1.5 %collective-permute-start.6 = (f32[1,64]{1,0:T(1,128)S(1)}, f32[1,64]{1,0:T(1,128)S(1)}, u32[]{:S(2)}, u32[]{:S(2)}) collective-permute-start(f32[1,64]{1,0:T(1,128)S(1)} %get-tuple-element.23), channel_id=1, source_target_pairs={{0,2},{1,3},{2,0},{3,1},{4,6},{5,7},{6,4},{7,5},{8,10},{9,11},{10,... | collective-permute-start | bytes 776 | tf_op jit(solution)/shard_map/ppermute | solution.py:514
  40.8 0.5 %collective-permute-start.5 = (f32[1,64]{1,0:T(1,128)S(1)}, f32[1,64]{1,0:T(1,128)S(1)}, u32[]{:S(2)}, u32[]{:S(2)}) collective-permute-start(f32[1,64]{1,0:T(1,128)S(1)} %get-tuple-element.23), channel_id=1, source_target_pairs={{0,1},{1,0},{2,3},{3,2},{4,5},{5,4},{6,7},{7,6},{8,9},{9,8},{10,11... | collective-permute-start | bytes 776 | tf_op jit(solution)/shard_map/ppermute | solution.py:514
  41.3 1.0 %copy.9 = f32[1,64,32,128]{3,2,1,0:T(8,128)} copy(f32[1,64,32,128]{3,2,1,0:T(8,128)S(1)} %bitcast.5) | data formatting | bytes 2097152
  42.3 0.0 collective-permute-done.7
  42.3 0.5 %collective-permute-done.6 = f32[1,64]{1,0:T(1,128)S(1)} collective-permute-done((f32[1,64]{1,0:T(1,128)S(1)}, f32[1,64]{1,0:T(1,128)S(1)}, u32[]{:S(2)}, u32[]{:S(2)}) %collective-permute-start.6) | collective-permute-done | bytes 288 | tf_op jit(solution)/shard_map/ppermute | solution.py:514
  42.8 1.5 %collective-permute-done.5 = f32[1,64]{1,0:T(1,128)S(1)} collective-permute-done((f32[1,64]{1,0:T(1,128)S(1)}, f32[1,64]{1,0:T(1,128)S(1)}, u32[]{:S(2)}, u32[]{:S(2)}) %collective-permute-start.5) | collective-permute-done | bytes 288 | tf_op jit(solution)/shard_map/ppermute | solution.py:514
  44.3 0.5 %add_add_fusion = f32[1,64]{1,0:T(1,128)} fusion(f32[1,64]{1,0:T(1,128)S(1)} %collective-permute-done.7, f32[1,64]{1,0:T(1,128)S(1)} %collective-permute-done.6, f32[1,64]{1,0:T(1,128)S(1)} %get-tuple-element.23, f32[1,64]{1,0:T(1,128)S(1)} %collective-permute-done.5), kind=kLoop, calls=%fused_computation.2 | loop fusion | flops 192 | bytes 1280 | tf_op jit(solution)/shard_map/add | solution.py:514
  (2 shorter events, 0.0 us)
Async XLA Ops:
  0.6 17.1 %collective-permute-start.3 = (f32[2048,128]{1,0:T(8,128)}, f32[2048,128]{1,0:T(8,128)S(1)}, u32[]{:S(2)}, u32[]{:S(2)}) collective-permute-start(f32[2048,128]{1,0:T(8,128)} %bitcast.6), channel_id=1, source_target_pairs={{0,2},{1,3},{2,0},{3,1},{4,8},{5,9},{6,10},{7,11},{8,4},{9,5},{10,... | collective-permute-start | bytes 3145736 | tf_op jit(solution)/shard_map/ppermute | solution.py:441
  2.0 10.8 %collective-permute-start = (f32[7,64,128]{2,1,0:T(8,128)S(1)}, f32[7,64,128]{2,1,0:T(8,128)S(1)}, u32[]{:S(2)}, u32[]{:S(2)}) collective-permute-start(f32[7,64,128]{2,1,0:T(8,128)S(1)} %get-tuple-element.13), channel_id=1, source_target_pairs={{0,1},{1,2},{2,3},{3,0},{4,5},{5,6},{6,7},{7,4},{8,9},{9,10},{10,1... | collective-permute-start | bytes 688136 | tf_op jit(solution)/shard_map/ppermute | solution.py:438
  3.6 10.1 %collective-permute-start.1 = (f32[4,64,128]{2,1,0:T(8,128)S(1)}, f32[4,64,128]{2,1,0:T(8,128)S(1)}, u32[]{:S(2)}, u32[]{:S(2)}) collective-permute-start(f32[4,64,128]{2,1,0:T(8,128)S(1)} %get-tuple-element.14), channel_id=1, source_target_pairs={{1,0},{2,1},{3,2},{0,3},{5,4},{6,5},{7,6},{4,7},{9,8},{10,9},{11,1... | collective-permute-start | bytes 393224 | tf_op jit(solution)/shard_map/ppermute | solution.py:439
  5.0 1.3 %copy-start = (f32[1,64,32,128]{3,2,1,0:T(8,128)S(1)}, f32[1,64,32,128]{3,2,1,0:T(8,128)}, u32[]{:S(2)}) copy-start(f32[1,64,32,128]{3,2,1,0:T(8,128)} %param.6) | copy-start | bytes 3145732
  6.2 4.6 %copy-start.1 = (f32[3,3,32,32]{3,2,1,0:T(8,128)S(1)}, f32[3,3,32,32]{3,2,1,0:T(8,128)}, u32[]{:S(2)}) copy-start(f32[3,3,32,32]{3,2,1,0:T(8,128)} %rs.1) | copy-start | bytes 110596
  6.2 4.6 %copy-start.2 = (f32[3,3,32,16]{2,3,1,0:T(8,128)S(1)}, f32[3,3,32,16]{2,3,1,0:T(8,128)}, u32[]{:S(2)}) copy-start(f32[3,3,32,16]{2,3,1,0:T(8,128)} %param.10) | copy-start | bytes 55300
  6.3 4.6 %copy-start.3 = (f32[3,3,16,1]{2,3,1,0:T(1,128)S(1)}, f32[3,3,16,1]{2,3,1,0:T(1,128)}, u32[]{:S(2)}) copy-start(f32[3,3,16,1]{2,3,1,0:T(1,128)} %param.11) | copy-start | bytes 1732
  13.7 8.6 %collective-permute-start.4 = (f32[11,64,128]{2,1,0:T(8,128)S(1)}, f32[11,64,128]{2,1,0:T(8,128)S(1)}, u32[]{:S(2)}, u32[]{:S(2)}) collective-permute-start(f32[11,64,128]{2,1,0:T(8,128)S(1)} %constant_dynamic-update-slice_fusion.halo), channel_id=1, source_target_pairs={{0,1},{1,0},{2,3},{3,2},{4,8},{5,9},{6,10},{7,11},{8,4},{9,5},{10,... | collective-permute-start | bytes 1081352 | tf_op jit(solution)/shard_map/ppermute | solution.py:444
  16.9 7.8 %collective-permute-start.2 = (f32[640,1024]{1,0:T(8,128)S(1)}, f32[640,1024]{1,0:T(8,128)S(1)}, u32[]{:S(2)}, u32[]{:S(2)}) collective-permute-start(f32[640,1024]{1,0:T(8,128)S(1)} %own_border_body.1.own), channel_id=1, source_target_pairs={{0,4},{4,0},{8,12},{12,8},{16,20},{20,16},{24,28},{28,24},{1,5},{5... | collective-permute-start | bytes 7864328 | tf_op jit(solution)/shard_map/ppermute | solution.py:493
  37.7 4.5 %collective-permute-start.7 = (f32[1,64]{1,0:T(1,128)S(1)}, f32[1,64]{1,0:T(1,128)S(1)}, u32[]{:S(2)}, u32[]{:S(2)}) collective-permute-start(f32[1,64]{1,0:T(1,128)S(1)} %get-tuple-element.23), channel_id=1, source_target_pairs={{0,3},{1,2},{2,1},{3,0},{4,7},{5,6},{6,5},{7,4},{8,11},{9,10},{10,... | collective-permute-start | bytes 776 | tf_op jit(solution)/shard_map/ppermute | solution.py:514
  39.2 3.5 %collective-permute-start.6 = (f32[1,64]{1,0:T(1,128)S(1)}, f32[1,64]{1,0:T(1,128)S(1)}, u32[]{:S(2)}, u32[]{:S(2)}) collective-permute-start(f32[1,64]{1,0:T(1,128)S(1)} %get-tuple-element.23), channel_id=1, source_target_pairs={{0,2},{1,3},{2,0},{3,1},{4,6},{5,7},{6,4},{7,5},{8,10},{9,11},{10,... | collective-permute-start | bytes 776 | tf_op jit(solution)/shard_map/ppermute | solution.py:514
  40.8 3.5 %collective-permute-start.5 = (f32[1,64]{1,0:T(1,128)S(1)}, f32[1,64]{1,0:T(1,128)S(1)}, u32[]{:S(2)}, u32[]{:S(2)}) collective-permute-start(f32[1,64]{1,0:T(1,128)S(1)} %get-tuple-element.23), channel_id=1, source_target_pairs={{0,1},{1,0},{2,3},{3,2},{4,5},{5,4},{6,7},{7,6},{8,9},{9,8},{10,11... | collective-permute-start | bytes 776 | tf_op jit(solution)/shard_map/ppermute | solution.py:514

commit v7 on v6

--- a/solution.py
+++ b/solution.py
@@ -390,7 +390,7 @@
                 if 0 <= row < strip:
                     block = value[i * cols : (i + 1) * cols, p * LANES : (p + 1) * LANES]
                     where = pl.ds(row, cols, stride=strip)
-                    rebuilt[where, :] = block
+                    rebuilt[row * cols : (row + 1) * cols, :] = block
                     error = block - x[where, :]
                     total = total + error * error
     part[...] = jnp.sum(total.T, axis=0, keepdims=True) * (1.0 / (LANES * LANES))
@@ -514,6 +514,7 @@
             misfit = misfit + lax.ppermute(part, "det", [(i, i ^ bit) for i in range(n_det)])
     else:
         misfit = lax.psum(part, "det")
+    rebuilt = rebuilt.reshape(strip, cols, width).transpose(1, 0, 2)
     return rebuilt.reshape(patterns.shape), misfit
 
 

time: 45 us -> 44.4 us (0.987)
  Pallas kernels: 31.3 us -> 30.6 us
  local copies, waits for them, and re-layouts: 1.02 us -> 1.63 us
  waiting for transfers between devices: 2.8 us -> 2.19 us
    reshape x0 -> x1, local copies, waits for them, and re-layouts: none -> 1.58 us  [on_device(): rebuilt = rebuilt.reshape(strip, cols, width).transpose(1, 0, 2)]
    unnamed x10 -> x9, local copies, waits for them, and re-layouts: 1.01 us -> 0.04 us
    pallas_call x1, Pallas kernels: 13 us -> 12.4 us  [on_device(): pl.pallas_call(functools.partial(decode_body, strip=strip, cols=cols), ou...]
    ppermute x3, waiting for transfers between devices: 2.03 us -> 1.42 us  [on_device(): lax.ppermute(part, 'det', [(i, i ^ bit) for i in range(n_det)])]
  transfers between devices with their start and end apart: 8 -> 8, of which waited for: 3 -> 2; matrix products, arithmetic and copies ran while one was open for 2% -> 4% of each run, Pallas kernels for 41% -> 41%
where the time goes in v7:
time: 44.4 us; the launch traced here: 44.2 us
  Pallas kernels  30.6 us (69%)
  starting transfers between devices  8.43 us (19%)
  waiting for transfers between devices  2.19 us (5%)
  local copies, waits for them, and re-layouts  1.63 us (4%)
  between operations  0.79 us (2%)
  other arithmetic  0.52 us (1%)
    pallas_call x4, Pallas kernels, encode(): pl.pallas_call(functools.partial(body, runs=runs, strip=strip, cols=cols,...  13.7 us
    pallas_call x1, Pallas kernels, on_device(): pl.pallas_call(functools.partial(decode_body, strip=strip, cols=cols), ou...  12.4 us
    ppermute x3, starting transfers between devices, on_device(): lax.ppermute(part, 'det', [(i, i ^ bit) for i in range(n_det)])  3.55 us
    pallas_call x1, Pallas kernels, on_device(): pl.pallas_call(decoder_weights_body, in_specs=[pl.BlockSpec()] * 3 + [pl....  1.99 us
    reshape x1, local copies, waits for them, and re-layouts, on_device(): rebuilt = rebuilt.reshape(strip, cols, width).transpose(1, 0, 2)  1.58 us
    ppermute x1, starting transfers between devices, on_device(): above = lax.ppermute(last, 'det', down)  1.54 us
    ppermute x1, starting transfers between devices, on_device(): below = lax.ppermute(first, 'det', up)  1.43 us
    ppermute x3, waiting for transfers between devices, on_device(): lax.ppermute(part, 'det', [(i, i ^ bit) for i in range(n_det)])  1.42 us
  transfers between devices with their start and end apart: 8, of which 2 were waited for; matrix products, arithmetic and copies ran while one was open for 4% of the time, Pallas kernels for 41%

profile of v7, /device:TPU:8, one launch (start us, length us, event | category | flops | bytes accessed | tf_op | source)
XLA Modules:
  0.0 44.2 jit_solution(2700418207449702225)
XLA Ops:
  0.6 0.1 collective-permute-start.3
  0.7 1.3 %edges.1 = (f32[7,64,128]{2,1,0:T(8,128)S(1)}, f32[4,64,128]{2,1,0:T(8,128)S(1)}, f32[3,3,1,16]{3,2,1,0:T(1,128)S(1)}, f32[3,3,16,32]{3,2,1,0:T(8,128)S(1)}) custom-call(f32[64,32,128]{2,1,0:T(8,128)} %bitcast.11, f32[3,3,1,16]{3,2,1,0:T(1,128)} %e1.1, f32[3,3,16,32]{3,2,1,0:T(8,128)} %e2.1), custom_call_target="tpu_custom_call" | custom-call | tf_op jit(solution)/shard_map/edges/pallas_call | solution.py:425
  2.0 1.5 %collective-permute-start = (f32[7,64,128]{2,1,0:T(8,128)S(1)}, f32[7,64,128]{2,1,0:T(8,128)S(1)}, u32[]{:S(2)}, u32[]{:S(2)}) collective-permute-start(f32[7,64,128]{2,1,0:T(8,128)S(1)} %get-tuple-element.13), channel_id=1, source_target_pairs={{0,1},{1,2},{2,3},{3,0},{4,5},{5,6},{6,7},{7,4},{8,9},{9,10},{10,1... | collective-permute-start | bytes 688136 | tf_op jit(solution)/shard_map/ppermute | solution.py:438
  3.6 1.4 %collective-permute-start.1 = (f32[4,64,128]{2,1,0:T(8,128)S(1)}, f32[4,64,128]{2,1,0:T(8,128)S(1)}, u32[]{:S(2)}, u32[]{:S(2)}) collective-permute-start(f32[4,64,128]{2,1,0:T(8,128)S(1)} %get-tuple-element.14), channel_id=1, source_target_pairs={{1,0},{2,1},{3,2},{0,3},{5,4},{6,5},{7,6},{4,7},{9,8},{10,9},{11,1... | collective-permute-start | bytes 393224 | tf_op jit(solution)/shard_map/ppermute | solution.py:439
  5.0 0.0 copy-start
  5.0 1.2 %encoder_weights.1 = (bf16[256,1024]{1,0:T(8,128)(2,1)S(1)}, bf16[1792,256]{1,0:T(8,128)(2,1)S(1)}) custom-call(f32[3,3,1,16]{3,2,1,0:T(1,128)S(1)} %get-tuple-element.15.e1, f32[3,3,16,32]{3,2,1,0:T(8,128)S(1)} %get-tuple-element.16.e2), custom_call_target="tpu_custom_call" | custom-call | flops 2000000000 | tf_op jit(solution)/shard_map/encoder_weights/pallas_call | solution.py:449
  6.2 0.0 copy-start.1
  6.2 0.0 copy-start.2
  6.3 0.0 copy-start.3
  6.3 0.0 copy-done
  6.3 4.5 %inner_body.1.after.inner = f32[448,1024]{1,0:T(8,128)S(1)} custom-call(f32[2048,128]{1,0:T(8,128)S(1)} %bitcast.12, bf16[256,1024]{1,0:T(8,128)(2,1)S(1)} %get-tuple-element.17.w1, bf16[1792,256]{1,0:T(8,128)(2,1)S(1)} %get-tuple-element.18.w2), custom_call_target="tpu_custom_call" | custom-call | tf_op jit(solution)/shard_map/inner_body/pallas_call | solution.py:465
  10.8 0.0 copy-done.1
  10.8 0.0 copy-done.2
  10.8 0.0 copy-done.3
  10.9 2.0 %decoder_weights.1 = (bf16[512,512]{1,0:T(8,128)(2,1)S(1)}, bf16[768,256]{1,0:T(8,128)(2,1)S(1)}, bf16[4096,256]{1,0:T(8,128)(2,1)S(1)}) custom-call(f32[3,3,32,32]{3,2,1,0:T(8,128)S(1)} %copy-done.1, f32[3,3,16,32]{3,2,1,0:T(8,128)S(1)} %bitcast.16, f32[3,3,1,16]{3,2,1,0:T(1,128)S(1)} %bitcast.17, f32[448,1024]{1,0:T(8,128)S(1)} %inner_body.1.after.inner), custom_call_target="tpu_custom_call" | custom-call | tf_op jit(solution)/shard_map/decoder_weights/pallas_call | solution.py:480
  12.9 0.0 collective-permute-done
  12.9 0.8 %collective-permute-done.1 = f32[4,64,128]{2,1,0:T(8,128)S(1)} collective-permute-done((f32[4,64,128]{2,1,0:T(8,128)S(1)}, f32[4,64,128]{2,1,0:T(8,128)S(1)}, u32[]{:S(2)}, u32[]{:S(2)}) %collective-permute-start.1) | collective-permute-done | bytes 131104 | tf_op jit(solution)/shard_map/ppermute | solution.py:439
  13.7 1.0 %collective-permute-start.4 = (f32[11,64,128]{2,1,0:T(8,128)S(1)}, f32[11,64,128]{2,1,0:T(8,128)S(1)}, u32[]{:S(2)}, u32[]{:S(2)}) collective-permute-start(f32[11,64,128]{2,1,0:T(8,128)S(1)} %constant_dynamic-update-slice_fusion.halo), channel_id=1, source_target_pairs={{0,1},{1,0},{2,3},{3,2},{4,8},{5,9},{6,10},{7,11},{8,4},{9,5},{10,... | collective-permute-start | bytes 1081352 | tf_op jit(solution)/shard_map/ppermute | solution.py:444
  14.6 2.3 %own_border_body.1.own = f32[640,1024]{1,0:T(8,128)S(1)} custom-call(f32[2048,128]{1,0:T(8,128)S(1)} %bitcast.13, f32[11,64,128]{2,1,0:T(8,128)S(1)} %constant_dynamic-update-slice_fusion.halo, bf16[256,1024]{1,0:T(8,128)(2,1)S(1)} %get-tuple-element.17.w1, bf16[1792,256]{1,0:T(8,128)(2,1)S(1)} %get-tuple-element.18.w2, ...), custom_call_target="tpu_custom_call" | custom-call | tf_op jit(solution)/shard_map/own_border_body/pallas_call | solution.py:465
  16.9 0.9 %collective-permute-start.2 = (f32[640,1024]{1,0:T(8,128)S(1)}, f32[640,1024]{1,0:T(8,128)S(1)}, u32[]{:S(2)}, u32[]{:S(2)}) collective-permute-start(f32[640,1024]{1,0:T(8,128)S(1)} %own_border_body.1.own), channel_id=1, source_target_pairs={{0,4},{4,0},{8,12},{12,8},{16,20},{20,16},{24,28},{28,24},{1,5},{5... | collective-permute-start | bytes 7864328 | tf_op jit(solution)/shard_map/ppermute | solution.py:493
  17.7 0.0 collective-permute-done.3.x
  17.7 4.5 %far_inner_body.1.inner = f32[448,1024]{1,0:T(8,128)S(1)} custom-call(f32[2048,128]{1,0:T(8,128)S(1)} %collective-permute-done.3.x, bf16[256,1024]{1,0:T(8,128)(2,1)S(1)} %get-tuple-element.17.w1, bf16[1792,256]{1,0:T(8,128)(2,1)S(1)} %get-tuple-element.18.w2), custom_call_target="tpu_custom_call" | custom-call | flops 25367150592 | tf_op jit(solution)/shard_map/far_inner_body/pallas_call | solution.py:465
  22.3 0.0 collective-permute-done.4.halo
  22.3 2.4 %far_border_body.1.other = f32[640,1024]{1,0:T(8,128)S(1)} custom-call(f32[2048,128]{1,0:T(8,128)S(1)} %collective-permute-done.3.x, f32[11,64,128]{2,1,0:T(8,128)S(1)} %collective-permute-done.4.halo, bf16[256,1024]{1,0:T(8,128)(2,1)S(1)} %get-tuple-element.17.w1, bf16[1792,256]{1,0:T(8,128)(2,1)S(1)} %get-tuple-element.18.w2, ...), custom_call_target="tpu_custom_call" | custom-call | flops 10871635968 | tf_op jit(solution)/shard_map/far_border_body/pallas_call | solution.py:465
  24.7 0.0 collective-permute-done.2.sibling
  24.7 12.4 %decode.1 = (f32[2048,128]{1,0:T(8,128)S(1)}, f32[1,64]{1,0:T(1,128)S(1)}) custom-call(f32[640,1024]{1,0:T(8,128)S(1)} %own_border_body.1.own, f32[640,1024]{1,0:T(8,128)S(1)} %collective-permute-done.2.sibling, f32[640,1024]{1,0:T(8,128)S(1)} %far_border_body.1.other, f32[2048,128]{1,0:T(8,128)S(1)} %bitcast.14, ...), custom_call_target="tpu_custom_call" | custom-call | flops 7549747200 | bytes 16777216 | tf_op jit(solution)/shard_map/decode/pallas_call | solution.py:496
  37.1 1.5 %collective-permute-start.7 = (f32[1,64]{1,0:T(1,128)S(1)}, f32[1,64]{1,0:T(1,128)S(1)}, u32[]{:S(2)}, u32[]{:S(2)}) collective-permute-start(f32[1,64]{1,0:T(1,128)S(1)} %get-tuple-element.23), channel_id=1, source_target_pairs={{0,3},{1,2},{2,1},{3,0},{4,7},{5,6},{6,5},{7,4},{8,11},{9,10},{10,... | collective-permute-start | bytes 776 | tf_op jit(solution)/shard_map/ppermute | solution.py:514
  38.6 1.5 %collective-permute-start.6 = (f32[1,64]{1,0:T(1,128)S(1)}, f32[1,64]{1,0:T(1,128)S(1)}, u32[]{:S(2)}, u32[]{:S(2)}) collective-permute-start(f32[1,64]{1,0:T(1,128)S(1)} %get-tuple-element.23), channel_id=1, source_target_pairs={{0,2},{1,3},{2,0},{3,1},{4,6},{5,7},{6,4},{7,5},{8,10},{9,11},{10,... | collective-permute-start | bytes 776 | tf_op jit(solution)/shard_map/ppermute | solution.py:514
  40.1 0.5 %collective-permute-start.5 = (f32[1,64]{1,0:T(1,128)S(1)}, f32[1,64]{1,0:T(1,128)S(1)}, u32[]{:S(2)}, u32[]{:S(2)}) collective-permute-start(f32[1,64]{1,0:T(1,128)S(1)} %get-tuple-element.23), channel_id=1, source_target_pairs={{0,1},{1,0},{2,3},{3,2},{4,5},{5,4},{6,7},{7,6},{8,9},{9,8},{10,11... | collective-permute-start | bytes 776 | tf_op jit(solution)/shard_map/ppermute | solution.py:514
  40.6 1.6 %copy.10 = f32[32,64,128]{2,0,1:T(8,128)} copy(f32[32,64,128]{2,1,0:T(8,128)S(1)} %bitcast.15) | data formatting | bytes 2097152 | tf_op jit(solution)/shard_map/reshape | solution.py:517
  42.2 0.0 collective-permute-done.7
  42.2 0.0 collective-permute-done.6
  42.2 1.4 %collective-permute-done.5 = f32[1,64]{1,0:T(1,128)S(1)} collective-permute-done((f32[1,64]{1,0:T(1,128)S(1)}, f32[1,64]{1,0:T(1,128)S(1)}, u32[]{:S(2)}, u32[]{:S(2)}) %collective-permute-start.5) | collective-permute-done | bytes 288 | tf_op jit(solution)/shard_map/ppermute | solution.py:514
  43.7 0.5 %add_add_fusion = f32[1,64]{1,0:T(1,128)} fusion(f32[1,64]{1,0:T(1,128)S(1)} %collective-permute-done.7, f32[1,64]{1,0:T(1,128)S(1)} %collective-permute-done.6, f32[1,64]{1,0:T(1,128)S(1)} %get-tuple-element.23, f32[1,64]{1,0:T(1,128)S(1)} %collective-permute-done.5), kind=kLoop, calls=%fused_computation.3 | loop fusion | flops 192 | bytes 1280 | tf_op jit(solution)/shard_map/add | solution.py:514
  (2 shorter events, 0.0 us)
Async XLA Ops:
  0.6 17.1 %collective-permute-start.3 = (f32[2048,128]{1,0:T(8,128)}, f32[2048,128]{1,0:T(8,128)S(1)}, u32[]{:S(2)}, u32[]{:S(2)}) collective-permute-start(f32[2048,128]{1,0:T(8,128)} %bitcast.10), channel_id=1, source_target_pairs={{0,2},{1,3},{2,0},{3,1},{4,8},{5,9},{6,10},{7,11},{8,4},{9,5},{10,... | collective-permute-start | bytes 3145736 | tf_op jit(solution)/shard_map/ppermute | solution.py:441
  2.0 10.8 %collective-permute-start = (f32[7,64,128]{2,1,0:T(8,128)S(1)}, f32[7,64,128]{2,1,0:T(8,128)S(1)}, u32[]{:S(2)}, u32[]{:S(2)}) collective-permute-start(f32[7,64,128]{2,1,0:T(8,128)S(1)} %get-tuple-element.13), channel_id=1, source_target_pairs={{0,1},{1,2},{2,3},{3,0},{4,5},{5,6},{6,7},{7,4},{8,9},{9,10},{10,1... | collective-permute-start | bytes 688136 | tf_op jit(solution)/shard_map/ppermute | solution.py:438
  3.6 10.1 %collective-permute-start.1 = (f32[4,64,128]{2,1,0:T(8,128)S(1)}, f32[4,64,128]{2,1,0:T(8,128)S(1)}, u32[]{:S(2)}, u32[]{:S(2)}) collective-permute-start(f32[4,64,128]{2,1,0:T(8,128)S(1)} %get-tuple-element.14), channel_id=1, source_target_pairs={{1,0},{2,1},{3,2},{0,3},{5,4},{6,5},{7,6},{4,7},{9,8},{10,9},{11,1... | collective-permute-start | bytes 393224 | tf_op jit(solution)/shard_map/ppermute | solution.py:439
  5.0 1.3 %copy-start = (f32[1,64,32,128]{3,2,1,0:T(8,128)S(1)}, f32[1,64,32,128]{3,2,1,0:T(8,128)}, u32[]{:S(2)}) copy-start(f32[1,64,32,128]{3,2,1,0:T(8,128)} %param.6) | copy-start | bytes 3145732
  6.2 4.6 %copy-start.1 = (f32[3,3,32,32]{3,2,1,0:T(8,128)S(1)}, f32[3,3,32,32]{3,2,1,0:T(8,128)}, u32[]{:S(2)}) copy-start(f32[3,3,32,32]{3,2,1,0:T(8,128)} %rs.1) | copy-start | bytes 110596
  6.2 4.6 %copy-start.2 = (f32[3,3,32,16]{2,3,1,0:T(8,128)S(1)}, f32[3,3,32,16]{2,3,1,0:T(8,128)}, u32[]{:S(2)}) copy-start(f32[3,3,32,16]{2,3,1,0:T(8,128)} %param.10) | copy-start | bytes 55300
  6.3 4.6 %copy-start.3 = (f32[3,3,16,1]{2,3,1,0:T(1,128)S(1)}, f32[3,3,16,1]{2,3,1,0:T(1,128)}, u32[]{:S(2)}) copy-start(f32[3,3,16,1]{2,3,1,0:T(1,128)} %param.11) | copy-start | bytes 1732
  13.7 8.6 %collective-permute-start.4 = (f32[11,64,128]{2,1,0:T(8,128)S(1)}, f32[11,64,128]{2,1,0:T(8,128)S(1)}, u32[]{:S(2)}, u32[]{:S(2)}) collective-permute-start(f32[11,64,128]{2,1,0:T(8,128)S(1)} %constant_dynamic-update-slice_fusion.halo), channel_id=1, source_target_pairs={{0,1},{1,0},{2,3},{3,2},{4,8},{5,9},{6,10},{7,11},{8,4},{9,5},{10,... | collective-permute-start | bytes 1081352 | tf_op jit(solution)/shard_map/ppermute | solution.py:444
  16.9 7.8 %collective-permute-start.2 = (f32[640,1024]{1,0:T(8,128)S(1)}, f32[640,1024]{1,0:T(8,128)S(1)}, u32[]{:S(2)}, u32[]{:S(2)}) collective-permute-start(f32[640,1024]{1,0:T(8,128)S(1)} %own_border_body.1.own), channel_id=1, source_target_pairs={{0,4},{4,0},{8,12},{12,8},{16,20},{20,16},{24,28},{28,24},{1,5},{5... | collective-permute-start | bytes 7864328 | tf_op jit(solution)/shard_map/ppermute | solution.py:493
  37.1 5.1 %collective-permute-start.7 = (f32[1,64]{1,0:T(1,128)S(1)}, f32[1,64]{1,0:T(1,128)S(1)}, u32[]{:S(2)}, u32[]{:S(2)}) collective-permute-start(f32[1,64]{1,0:T(1,128)S(1)} %get-tuple-element.23), channel_id=1, source_target_pairs={{0,3},{1,2},{2,1},{3,0},{4,7},{5,6},{6,5},{7,4},{8,11},{9,10},{10,... | collective-permute-start | bytes 776 | tf_op jit(solution)/shard_map/ppermute | solution.py:514
  38.6 3.6 %collective-permute-start.6 = (f32[1,64]{1,0:T(1,128)S(1)}, f32[1,64]{1,0:T(1,128)S(1)}, u32[]{:S(2)}, u32[]{:S(2)}) collective-permute-start(f32[1,64]{1,0:T(1,128)S(1)} %get-tuple-element.23), channel_id=1, source_target_pairs={{0,2},{1,3},{2,0},{3,1},{4,6},{5,7},{6,4},{7,5},{8,10},{9,11},{10,... | collective-permute-start | bytes 776 | tf_op jit(solution)/shard_map/ppermute | solution.py:514
  40.1 3.5 %collective-permute-start.5 = (f32[1,64]{1,0:T(1,128)S(1)}, f32[1,64]{1,0:T(1,128)S(1)}, u32[]{:S(2)}, u32[]{:S(2)}) collective-permute-start(f32[1,64]{1,0:T(1,128)S(1)} %get-tuple-element.23), channel_id=1, source_target_pairs={{0,1},{1,0},{2,3},{3,2},{4,5},{5,4},{6,7},{7,6},{8,9},{9,8},{10,11... | collective-permute-start | bytes 776 | tf_op jit(solution)/shard_map/ppermute | solution.py:514

commit v8 on v7

--- a/solution.py
+++ b/solution.py
@@ -375,7 +375,7 @@
     lax.fori_loop(0, blocks, first, 0, unroll=True)
     total = jnp.zeros((cols, LANES), F32)
     pairs = strip // 2 + 1
-    step = 9
+    step = 12
     for begin in range(0, pairs, step):
         size = min(step, pairs - begin)
         top = slice(begin * cols, (begin + size) * cols)

time: 44.4 us -> 44.5 us (level)
  no operation moved by 1% of the time
where the time goes in v8:
time: 44.5 us; the launch traced here: 44.3 us
  Pallas kernels  30.7 us (69%)
  starting transfers between devices  8.43 us (19%)
  waiting for transfers between devices  2.16 us (5%)
  local copies, waits for them, and re-layouts  1.63 us (4%)
  between operations  0.79 us (2%)
  other arithmetic  0.52 us (1%)
    pallas_call x4, Pallas kernels, encode(): pl.pallas_call(functools.partial(body, runs=runs, strip=strip, cols=cols,...  13.7 us
    pallas_call x1, Pallas kernels, on_device(): pl.pallas_call(functools.partial(decode_body, strip=strip, cols=cols), ou...  12.5 us
    ppermute x3, starting transfers between devices, on_device(): lax.ppermute(part, 'det', [(i, i ^ bit) for i in range(n_det)])  3.55 us
    pallas_call x1, Pallas kernels, on_device(): pl.pallas_call(decoder_weights_body, in_specs=[pl.BlockSpec()] * 3 + [pl....  1.99 us
    reshape x1, local copies, waits for them, and re-layouts, on_device(): rebuilt = rebuilt.reshape(strip, cols, width).transpose(1, 0, 2)  1.58 us
    ppermute x1, starting transfers between devices, on_device(): above = lax.ppermute(last, 'det', down)  1.54 us
    ppermute x1, starting transfers between devices, on_device(): below = lax.ppermute(first, 'det', up)  1.43 us
    ppermute x3, waiting for transfers between devices, on_device(): lax.ppermute(part, 'det', [(i, i ^ bit) for i in range(n_det)])  1.39 us
  transfers between devices with their start and end apart: 8, of which 2 were waited for; matrix products, arithmetic and copies ran while one was open for 4% of the time, Pallas kernels for 41%

profile of v8, /device:TPU:8, one launch (start us, length us, event | category | flops | bytes accessed | tf_op | source)
XLA Modules:
  0.0 44.3 jit_solution(6919455385586339642)
XLA Ops:
  0.6 0.1 collective-permute-start.3
  0.7 1.3 %edges.1 = (f32[7,64,128]{2,1,0:T(8,128)S(1)}, f32[4,64,128]{2,1,0:T(8,128)S(1)}, f32[3,3,1,16]{3,2,1,0:T(1,128)S(1)}, f32[3,3,16,32]{3,2,1,0:T(8,128)S(1)}) custom-call(f32[64,32,128]{2,1,0:T(8,128)} %bitcast.11, f32[3,3,1,16]{3,2,1,0:T(1,128)} %e1.1, f32[3,3,16,32]{3,2,1,0:T(8,128)} %e2.1), custom_call_target="tpu_custom_call" | custom-call | tf_op jit(solution)/shard_map/edges/pallas_call | solution.py:425
  2.0 1.5 %collective-permute-start = (f32[7,64,128]{2,1,0:T(8,128)S(1)}, f32[7,64,128]{2,1,0:T(8,128)S(1)}, u32[]{:S(2)}, u32[]{:S(2)}) collective-permute-start(f32[7,64,128]{2,1,0:T(8,128)S(1)} %get-tuple-element.13), channel_id=1, source_target_pairs={{0,1},{1,2},{2,3},{3,0},{4,5},{5,6},{6,7},{7,4},{8,9},{9,10},{10,1... | collective-permute-start | bytes 688136 | tf_op jit(solution)/shard_map/ppermute | solution.py:438
  3.6 1.4 %collective-permute-start.1 = (f32[4,64,128]{2,1,0:T(8,128)S(1)}, f32[4,64,128]{2,1,0:T(8,128)S(1)}, u32[]{:S(2)}, u32[]{:S(2)}) collective-permute-start(f32[4,64,128]{2,1,0:T(8,128)S(1)} %get-tuple-element.14), channel_id=1, source_target_pairs={{1,0},{2,1},{3,2},{0,3},{5,4},{6,5},{7,6},{4,7},{9,8},{10,9},{11,1... | collective-permute-start | bytes 393224 | tf_op jit(solution)/shard_map/ppermute | solution.py:439
  5.0 0.0 copy-start
  5.0 1.2 %encoder_weights.1 = (bf16[256,1024]{1,0:T(8,128)(2,1)S(1)}, bf16[1792,256]{1,0:T(8,128)(2,1)S(1)}) custom-call(f32[3,3,1,16]{3,2,1,0:T(1,128)S(1)} %get-tuple-element.15.e1, f32[3,3,16,32]{3,2,1,0:T(8,128)S(1)} %get-tuple-element.16.e2), custom_call_target="tpu_custom_call" | custom-call | flops 2000000000 | tf_op jit(solution)/shard_map/encoder_weights/pallas_call | solution.py:449
  6.2 0.0 copy-start.1
  6.2 0.0 copy-start.2
  6.3 0.0 copy-start.3
  6.3 0.0 copy-done
  6.3 4.5 %inner_body.1.after.inner = f32[448,1024]{1,0:T(8,128)S(1)} custom-call(f32[2048,128]{1,0:T(8,128)S(1)} %bitcast.12, bf16[256,1024]{1,0:T(8,128)(2,1)S(1)} %get-tuple-element.17.w1, bf16[1792,256]{1,0:T(8,128)(2,1)S(1)} %get-tuple-element.18.w2), custom_call_target="tpu_custom_call" | custom-call | tf_op jit(solution)/shard_map/inner_body/pallas_call | solution.py:465
  10.8 0.0 copy-done.1
  10.8 0.0 copy-done.2
  10.8 0.0 copy-done.3
  10.9 2.0 %decoder_weights.1 = (bf16[512,512]{1,0:T(8,128)(2,1)S(1)}, bf16[768,256]{1,0:T(8,128)(2,1)S(1)}, bf16[4096,256]{1,0:T(8,128)(2,1)S(1)}) custom-call(f32[3,3,32,32]{3,2,1,0:T(8,128)S(1)} %copy-done.1, f32[3,3,16,32]{3,2,1,0:T(8,128)S(1)} %bitcast.16, f32[3,3,1,16]{3,2,1,0:T(1,128)S(1)} %bitcast.17, f32[448,1024]{1,0:T(8,128)S(1)} %inner_body.1.after.inner), custom_call_target="tpu_custom_call" | custom-call | tf_op jit(solution)/shard_map/decoder_weights/pallas_call | solution.py:480
  12.9 0.0 collective-permute-done
  12.9 0.8 %collective-permute-done.1 = f32[4,64,128]{2,1,0:T(8,128)S(1)} collective-permute-done((f32[4,64,128]{2,1,0:T(8,128)S(1)}, f32[4,64,128]{2,1,0:T(8,128)S(1)}, u32[]{:S(2)}, u32[]{:S(2)}) %collective-permute-start.1) | collective-permute-done | bytes 131104 | tf_op jit(solution)/shard_map/ppermute | solution.py:439
  13.7 1.0 %collective-permute-start.4 = (f32[11,64,128]{2,1,0:T(8,128)S(1)}, f32[11,64,128]{2,1,0:T(8,128)S(1)}, u32[]{:S(2)}, u32[]{:S(2)}) collective-permute-start(f32[11,64,128]{2,1,0:T(8,128)S(1)} %constant_dynamic-update-slice_fusion.halo), channel_id=1, source_target_pairs={{0,1},{1,0},{2,3},{3,2},{4,8},{5,9},{6,10},{7,11},{8,4},{9,5},{10,... | collective-permute-start | bytes 1081352 | tf_op jit(solution)/shard_map/ppermute | solution.py:444
  14.6 2.3 %own_border_body.1.own = f32[640,1024]{1,0:T(8,128)S(1)} custom-call(f32[2048,128]{1,0:T(8,128)S(1)} %bitcast.13, f32[11,64,128]{2,1,0:T(8,128)S(1)} %constant_dynamic-update-slice_fusion.halo, bf16[256,1024]{1,0:T(8,128)(2,1)S(1)} %get-tuple-element.17.w1, bf16[1792,256]{1,0:T(8,128)(2,1)S(1)} %get-tuple-element.18.w2, ...), custom_call_target="tpu_custom_call" | custom-call | tf_op jit(solution)/shard_map/own_border_body/pallas_call | solution.py:465
  16.9 0.9 %collective-permute-start.2 = (f32[640,1024]{1,0:T(8,128)S(1)}, f32[640,1024]{1,0:T(8,128)S(1)}, u32[]{:S(2)}, u32[]{:S(2)}) collective-permute-start(f32[640,1024]{1,0:T(8,128)S(1)} %own_border_body.1.own), channel_id=1, source_target_pairs={{0,4},{4,0},{8,12},{12,8},{16,20},{20,16},{24,28},{28,24},{1,5},{5... | collective-permute-start | bytes 7864328 | tf_op jit(solution)/shard_map/ppermute | solution.py:493
  17.7 0.0 collective-permute-done.3.x
  17.7 4.5 %far_inner_body.1.inner = f32[448,1024]{1,0:T(8,128)S(1)} custom-call(f32[2048,128]{1,0:T(8,128)S(1)} %collective-permute-done.3.x, bf16[256,1024]{1,0:T(8,128)(2,1)S(1)} %get-tuple-element.17.w1, bf16[1792,256]{1,0:T(8,128)(2,1)S(1)} %get-tuple-element.18.w2), custom_call_target="tpu_custom_call" | custom-call | flops 25367150592 | tf_op jit(solution)/shard_map/far_inner_body/pallas_call | solution.py:465
  22.3 0.0 collective-permute-done.4.halo
  22.3 2.4 %far_border_body.1.other = f32[640,1024]{1,0:T(8,128)S(1)} custom-call(f32[2048,128]{1,0:T(8,128)S(1)} %collective-permute-done.3.x, f32[11,64,128]{2,1,0:T(8,128)S(1)} %collective-permute-done.4.halo, bf16[256,1024]{1,0:T(8,128)(2,1)S(1)} %get-tuple-element.17.w1, bf16[1792,256]{1,0:T(8,128)(2,1)S(1)} %get-tuple-element.18.w2, ...), custom_call_target="tpu_custom_call" | custom-call | flops 10871635968 | tf_op jit(solution)/shard_map/far_border_body/pallas_call | solution.py:465
  24.7 0.0 collective-permute-done.2.sibling
  24.7 12.5 %decode.1 = (f32[2048,128]{1,0:T(8,128)S(1)}, f32[1,64]{1,0:T(1,128)S(1)}) custom-call(f32[640,1024]{1,0:T(8,128)S(1)} %own_border_body.1.own, f32[640,1024]{1,0:T(8,128)S(1)} %collective-permute-done.2.sibling, f32[640,1024]{1,0:T(8,128)S(1)} %far_border_body.1.other, f32[2048,128]{1,0:T(8,128)S(1)} %bitcast.14, ...), custom_call_target="tpu_custom_call" | custom-call | flops 7549747200 | bytes 16777216 | tf_op jit(solution)/shard_map/decode/pallas_call | solution.py:496
  37.2 1.5 %collective-permute-start.7 = (f32[1,64]{1,0:T(1,128)S(1)}, f32[1,64]{1,0:T(1,128)S(1)}, u32[]{:S(2)}, u32[]{:S(2)}) collective-permute-start(f32[1,64]{1,0:T(1,128)S(1)} %get-tuple-element.23), channel_id=1, source_target_pairs={{0,3},{1,2},{2,1},{3,0},{4,7},{5,6},{6,5},{7,4},{8,11},{9,10},{10,... | collective-permute-start | bytes 776 | tf_op jit(solution)/shard_map/ppermute | solution.py:514
  38.7 1.5 %collective-permute-start.6 = (f32[1,64]{1,0:T(1,128)S(1)}, f32[1,64]{1,0:T(1,128)S(1)}, u32[]{:S(2)}, u32[]{:S(2)}) collective-permute-start(f32[1,64]{1,0:T(1,128)S(1)} %get-tuple-element.23), channel_id=1, source_target_pairs={{0,2},{1,3},{2,0},{3,1},{4,6},{5,7},{6,4},{7,5},{8,10},{9,11},{10,... | collective-permute-start | bytes 776 | tf_op jit(solution)/shard_map/ppermute | solution.py:514
  40.2 0.6 %collective-permute-start.5 = (f32[1,64]{1,0:T(1,128)S(1)}, f32[1,64]{1,0:T(1,128)S(1)}, u32[]{:S(2)}, u32[]{:S(2)}) collective-permute-start(f32[1,64]{1,0:T(1,128)S(1)} %get-tuple-element.23), channel_id=1, source_target_pairs={{0,1},{1,0},{2,3},{3,2},{4,5},{5,4},{6,7},{7,6},{8,9},{9,8},{10,11... | collective-permute-start | bytes 776 | tf_op jit(solution)/shard_map/ppermute | solution.py:514
  40.8 1.6 %copy.10 = f32[32,64,128]{2,0,1:T(8,128)} copy(f32[32,64,128]{2,1,0:T(8,128)S(1)} %bitcast.15) | data formatting | bytes 2097152 | tf_op jit(solution)/shard_map/reshape | solution.py:517
  42.3 0.0 collective-permute-done.7
  42.3 0.0 collective-permute-done.6
  42.4 1.4 %collective-permute-done.5 = f32[1,64]{1,0:T(1,128)S(1)} collective-permute-done((f32[1,64]{1,0:T(1,128)S(1)}, f32[1,64]{1,0:T(1,128)S(1)}, u32[]{:S(2)}, u32[]{:S(2)}) %collective-permute-start.5) | collective-permute-done | bytes 288 | tf_op jit(solution)/shard_map/ppermute | solution.py:514
  43.7 0.5 %add_add_fusion = f32[1,64]{1,0:T(1,128)} fusion(f32[1,64]{1,0:T(1,128)S(1)} %collective-permute-done.7, f32[1,64]{1,0:T(1,128)S(1)} %collective-permute-done.6, f32[1,64]{1,0:T(1,128)S(1)} %get-tuple-element.23, f32[1,64]{1,0:T(1,128)S(1)} %collective-permute-done.5), kind=kLoop, calls=%fused_computation.3 | loop fusion | flops 192 | bytes 1280 | tf_op jit(solution)/shard_map/add | solution.py:514
  (2 shorter events, 0.0 us)
Async XLA Ops:
  0.6 17.1 %collective-permute-start.3 = (f32[2048,128]{1,0:T(8,128)}, f32[2048,128]{1,0:T(8,128)S(1)}, u32[]{:S(2)}, u32[]{:S(2)}) collective-permute-start(f32[2048,128]{1,0:T(8,128)} %bitcast.10), channel_id=1, source_target_pairs={{0,2},{1,3},{2,0},{3,1},{4,8},{5,9},{6,10},{7,11},{8,4},{9,5},{10,... | collective-permute-start | bytes 3145736 | tf_op jit(solution)/shard_map/ppermute | solution.py:441
  2.0 10.8 %collective-permute-start = (f32[7,64,128]{2,1,0:T(8,128)S(1)}, f32[7,64,128]{2,1,0:T(8,128)S(1)}, u32[]{:S(2)}, u32[]{:S(2)}) collective-permute-start(f32[7,64,128]{2,1,0:T(8,128)S(1)} %get-tuple-element.13), channel_id=1, source_target_pairs={{0,1},{1,2},{2,3},{3,0},{4,5},{5,6},{6,7},{7,4},{8,9},{9,10},{10,1... | collective-permute-start | bytes 688136 | tf_op jit(solution)/shard_map/ppermute | solution.py:438
  3.6 10.1 %collective-permute-start.1 = (f32[4,64,128]{2,1,0:T(8,128)S(1)}, f32[4,64,128]{2,1,0:T(8,128)S(1)}, u32[]{:S(2)}, u32[]{:S(2)}) collective-permute-start(f32[4,64,128]{2,1,0:T(8,128)S(1)} %get-tuple-element.14), channel_id=1, source_target_pairs={{1,0},{2,1},{3,2},{0,3},{5,4},{6,5},{7,6},{4,7},{9,8},{10,9},{11,1... | collective-permute-start | bytes 393224 | tf_op jit(solution)/shard_map/ppermute | solution.py:439
  5.0 1.3 %copy-start = (f32[1,64,32,128]{3,2,1,0:T(8,128)S(1)}, f32[1,64,32,128]{3,2,1,0:T(8,128)}, u32[]{:S(2)}) copy-start(f32[1,64,32,128]{3,2,1,0:T(8,128)} %param.6) | copy-start | bytes 3145732
  6.2 4.6 %copy-start.1 = (f32[3,3,32,32]{3,2,1,0:T(8,128)S(1)}, f32[3,3,32,32]{3,2,1,0:T(8,128)}, u32[]{:S(2)}) copy-start(f32[3,3,32,32]{3,2,1,0:T(8,128)} %rs.1) | copy-start | bytes 110596
  6.2 4.6 %copy-start.2 = (f32[3,3,32,16]{2,3,1,0:T(8,128)S(1)}, f32[3,3,32,16]{2,3,1,0:T(8,128)}, u32[]{:S(2)}) copy-start(f32[3,3,32,16]{2,3,1,0:T(8,128)} %param.10) | copy-start | bytes 55300
  6.3 4.6 %copy-start.3 = (f32[3,3,16,1]{2,3,1,0:T(1,128)S(1)}, f32[3,3,16,1]{2,3,1,0:T(1,128)}, u32[]{:S(2)}) copy-start(f32[3,3,16,1]{2,3,1,0:T(1,128)} %param.11) | copy-start | bytes 1732
  13.7 8.6 %collective-permute-start.4 = (f32[11,64,128]{2,1,0:T(8,128)S(1)}, f32[11,64,128]{2,1,0:T(8,128)S(1)}, u32[]{:S(2)}, u32[]{:S(2)}) collective-permute-start(f32[11,64,128]{2,1,0:T(8,128)S(1)} %constant_dynamic-update-slice_fusion.halo), channel_id=1, source_target_pairs={{0,1},{1,0},{2,3},{3,2},{4,8},{5,9},{6,10},{7,11},{8,4},{9,5},{10,... | collective-permute-start | bytes 1081352 | tf_op jit(solution)/shard_map/ppermute | solution.py:444
  16.9 7.8 %collective-permute-start.2 = (f32[640,1024]{1,0:T(8,128)S(1)}, f32[640,1024]{1,0:T(8,128)S(1)}, u32[]{:S(2)}, u32[]{:S(2)}) collective-permute-start(f32[640,1024]{1,0:T(8,128)S(1)} %own_border_body.1.own), channel_id=1, source_target_pairs={{0,4},{4,0},{8,12},{12,8},{16,20},{20,16},{24,28},{28,24},{1,5},{5... | collective-permute-start | bytes 7864328 | tf_op jit(solution)/shard_map/ppermute | solution.py:493
  37.2 5.1 %collective-permute-start.7 = (f32[1,64]{1,0:T(1,128)S(1)}, f32[1,64]{1,0:T(1,128)S(1)}, u32[]{:S(2)}, u32[]{:S(2)}) collective-permute-start(f32[1,64]{1,0:T(1,128)S(1)} %get-tuple-element.23), channel_id=1, source_target_pairs={{0,3},{1,2},{2,1},{3,0},{4,7},{5,6},{6,5},{7,4},{8,11},{9,10},{10,... | collective-permute-start | bytes 776 | tf_op jit(solution)/shard_map/ppermute | solution.py:514
  38.7 3.6 %collective-permute-start.6 = (f32[1,64]{1,0:T(1,128)S(1)}, f32[1,64]{1,0:T(1,128)S(1)}, u32[]{:S(2)}, u32[]{:S(2)}) collective-permute-start(f32[1,64]{1,0:T(1,128)S(1)} %get-tuple-element.23), channel_id=1, source_target_pairs={{0,2},{1,3},{2,0},{3,1},{4,6},{5,7},{6,4},{7,5},{8,10},{9,11},{10,... | collective-permute-start | bytes 776 | tf_op jit(solution)/shard_map/ppermute | solution.py:514
  40.2 3.5 %collective-permute-start.5 = (f32[1,64]{1,0:T(1,128)S(1)}, f32[1,64]{1,0:T(1,128)S(1)}, u32[]{:S(2)}, u32[]{:S(2)}) collective-permute-start(f32[1,64]{1,0:T(1,128)S(1)} %get-tuple-element.23), channel_id=1, source_target_pairs={{0,1},{1,0},{2,3},{3,2},{4,5},{5,4},{6,7},{7,6},{8,9},{9,8},{10,11... | collective-permute-start | bytes 776 | tf_op jit(solution)/shard_map/ppermute | solution.py:514
